TPU v7x, 32 devices: a whole 2x2x4 slice. The times are simulated.
32 devices in a mesh: dp: 4 (over z), ctx: 4 (over y, core), tensor: 2 (over x).
Axes of the slice: x: 2, y: 2, z: 4, core: 2. Of those that a mesh axis runs over, the one named last changes fastest.
Arguments:
- hidden_in: bfloat16 [4, 1024, 2048], P('dp', 'ctx'), may hold values from -6 to 6
- attn_norm_gain: float32 [2048], replicated, may hold values from 0.5 to 1.5
- attn_norm_bias: float32 [2048], replicated, may hold values from -2 to 2
- qkv_weight: bfloat16 [2048, 6144], P(None, 'tensor'), may hold values from -0.125 to 0.125
- qkv_bias: float32 [6144], P('tensor'), may hold values from -1.2 to 1.2
- dense_weight: bfloat16 [2048, 2048], P('tensor'), may hold values from -2 to 2
- dense_bias: float32 [2048], replicated, may hold values from -3 to 3
- mlp_norm_gain: float32 [2048], replicated, may hold values from 0.5 to 1.5
- mlp_norm_bias: float32 [2048], replicated, may hold values from -2 to 2
- up_weight: bfloat16 [2048, 8192], P(None, 'tensor'), may hold values from -0.125 to 0.125
- up_bias: float32 [8192], P('tensor'), may hold values from -3 to 3
- down_weight: bfloat16 [8192, 2048], P('tensor'), may hold values from -0.0625 to 0.0625
- down_bias: float32 [2048], replicated, may hold values from -3 to 3
- out_cotangent: bfloat16 [4, 1024, 2048], P('dp', 'ctx'), may hold values from -6 to 6
- subset_ids: int32 [4, 1024], P('dp', 'ctx'), may hold values from 0 to 21
- subset_weights: float32 [22], replicated, may hold values from 0.5 to 2
Outputs:
- layer_out: bfloat16 [4, 1024, 2048], P('dp', 'ctx')
- input_grad: bfloat16 [4, 1024, 2048], P('dp', 'ctx')
- grad_attn_norm_gain: float32 [2048], replicated
- grad_attn_norm_bias: float32 [2048], replicated
- grad_qkv_weight: float32 [2048, 6144], P(('dp', 'ctx'), 'tensor')
- grad_qkv_bias: float32 [6144], P('tensor')
- grad_dense_weight: float32 [2048, 2048], P('tensor', ('dp', 'ctx'))
- grad_dense_bias: float32 [2048], replicated
- grad_mlp_norm_gain: float32 [2048], replicated
- grad_mlp_norm_bias: float32 [2048], replicated
- grad_up_weight: float32 [2048, 8192], P(('dp', 'ctx'), 'tensor')
- grad_up_bias: float32 [8192], P('tensor')
- grad_down_weight: float32 [8192, 2048], P('tensor', ('dp', 'ctx'))
- grad_down_bias: float32 [2048], replicated
Inputs may be any that keep to these rules, and one draw needn't show every extreme that they name: `subset_ids`: the corpus subset of every token, one of 22.
All inputs are finite; a program needn't handle non-finite values.
Results may differ from a plain program's by a relative error of at most 0.012.
Values may be sent and summed in bfloat16 or wider, within the bound.
A program may use at most 256 MiB of HBM per device.

v0:
```python
import math

import jax
import jax.numpy as jnp
from jax import lax
from jax.sharding import PartitionSpec as P

HS = 256
ROT = 64


NORM_EPS = 1e-05


def rope_tables(positions, rot_dims):
    half_dims = rot_dims // 2
    freqs = 10000.0 ** (-(jnp.arange(half_dims, dtype=jnp.float32) * 2.0 / rot_dims))
    angles = positions.astype(jnp.float32)[:, None] * freqs[None, :]
    return (
        jnp.concatenate([jnp.cos(angles), jnp.cos(angles)], -1),
        jnp.concatenate([jnp.sin(angles), jnp.sin(angles)], -1),
    )


def rotate(columns, cosine_table, sine_table):
    half_dims = ROT // 2
    leading = columns[..., :ROT]
    turned = jnp.concatenate([-leading[..., half_dims:], leading[..., :half_dims]], -1)
    moved = leading * cosine_table[:, None, :] + turned * sine_table[:, None, :]
    return jnp.concatenate([moved, columns[..., ROT:]], -1)


def rotate_back(gradient, cosine_table, sine_table):
    half_dims = ROT // 2
    leading = gradient[..., :ROT]
    scaled = leading * sine_table[:, None, :]
    turned = jnp.concatenate([scaled[..., half_dims:], -scaled[..., :half_dims]], -1)
    moved = leading * cosine_table[:, None, :] + turned
    return jnp.concatenate([moved, gradient[..., ROT:]], -1)


def local(
    hidden_in,
    attn_norm_gain,
    attn_norm_bias,
    qkv_weight,
    qkv_bias,
    dense_weight,
    dense_bias,
    mlp_norm_gain,
    mlp_norm_bias,
    up_weight,
    up_bias,
    down_weight,
    down_bias,
    out_cotangent,
    subset_ids,
    subset_weights,
):
    seq_count, block_len, model_width = hidden_in.shape
    row_count = seq_count * block_len
    head_count = qkv_weight.shape[1] // (3 * HS)
    length = block_len * lax.axis_size("ctx")
    score_scale = 1.0 / math.sqrt(HS)
    inputs = hidden_in.reshape(row_count, model_width).astype(jnp.float32)
    row_mean = jnp.mean(inputs, -1, keepdims=True)
    centered = inputs - row_mean
    inv_std = lax.rsqrt(jnp.mean(centered * centered, -1, keepdims=True) + NORM_EPS)
    normed = centered * inv_std
    attn_in = (normed * attn_norm_gain + attn_norm_bias).astype(jnp.bfloat16)
    mlp_in = (normed * mlp_norm_gain + mlp_norm_bias).astype(jnp.bfloat16)
    qkv_all = jnp.dot(attn_in, qkv_weight, preferred_element_type=jnp.float32) + qkv_bias
    qkv_all = qkv_all.reshape(seq_count, block_len, head_count, 3, HS)
    positions = lax.axis_index("ctx") * block_len + jnp.arange(block_len, dtype=jnp.int32)
    cosine_table, sine_table = rope_tables(positions, ROT)
    query_rows = rotate(qkv_all[:, :, :, 0], cosine_table, sine_table).astype(jnp.bfloat16)
    key_rows = rotate(qkv_all[:, :, :, 1], cosine_table, sine_table).astype(jnp.bfloat16)
    value_rows = qkv_all[:, :, :, 2].astype(jnp.bfloat16)
    key_whole, value_whole = (
        lax.all_gather(
            key_rows.reshape(seq_count, block_len, head_count * HS), "ctx", axis=1, tiled=True
        ),
        lax.all_gather(
            value_rows.reshape(seq_count, block_len, head_count * HS), "ctx", axis=1, tiled=True
        ),
    )
    key_whole = key_whole.reshape(seq_count, length, head_count, HS)
    value_whole = value_whole.reshape(seq_count, length, head_count, HS)
    causal = jnp.arange(length, dtype=jnp.int32)[None, :] <= positions[:, None]

    def score_block():
        raw = jnp.einsum(
            "sqhd,skhd->shqk", query_rows, key_whole, preferred_element_type=jnp.float32
        )
        return jnp.where(causal, raw * score_scale, -1e30)

    scores = score_block()
    row_max = jnp.max(scores, -1, keepdims=True)
    expd = jnp.exp(scores - row_max)
    row_total = jnp.sum(expd, -1, keepdims=True)
    prob = expd / row_total
    log_total = row_max + jnp.log(row_total)
    attn_out = jnp.einsum(
        "shqk,skhd->sqhd",
        prob.astype(jnp.bfloat16),
        value_whole,
        preferred_element_type=jnp.float32,
    ).astype(jnp.bfloat16)
    attn_out = attn_out.reshape(row_count, head_count * HS)
    up_pre = jnp.dot(mlp_in, up_weight, preferred_element_type=jnp.float32) + up_bias
    activated = jax.nn.gelu(up_pre, approximate=False).astype(jnp.bfloat16)
    partial_sum = jnp.dot(attn_out, dense_weight, preferred_element_type=jnp.float32) + jnp.dot(
        activated, down_weight, preferred_element_type=jnp.float32
    )
    summed = lax.psum(partial_sum, "tensor")
    layer_out = (inputs + summed + dense_bias + down_bias).astype(jnp.bfloat16)
    layer_out = layer_out.reshape(seq_count, block_len, model_width)
    subset_count = subset_weights.shape[0]
    matches = subset_ids[..., None] == jnp.arange(subset_count, dtype=jnp.int32)
    row_weight = jnp.sum(jnp.where(matches, subset_weights, 0.0), -1).reshape(row_count, 1)
    grad_out = out_cotangent.reshape(row_count, model_width).astype(jnp.float32) * row_weight
    grad_low = grad_out.astype(jnp.bfloat16)
    grad_out_bias = jnp.sum(grad_out, 0)
    grad_down_weight = jnp.einsum(
        "rf,rd->fd", activated, grad_low, preferred_element_type=jnp.float32
    )
    grad_dense_weight = jnp.einsum(
        "rk,rd->kd", attn_out, grad_low, preferred_element_type=jnp.float32
    )
    grad_act = jnp.einsum("rd,fd->rf", grad_low, down_weight, preferred_element_type=jnp.float32)
    gelu_back = jax.vjp(lambda pre_act: jax.nn.gelu(pre_act, approximate=False), up_pre)[1]
    grad_pre = gelu_back(grad_act)[0].astype(jnp.bfloat16)
    grad_up_weight = jnp.einsum("rd,rf->df", mlp_in, grad_pre, preferred_element_type=jnp.float32)
    grad_up_bias = jnp.sum(grad_pre.astype(jnp.float32), 0)
    grad_mlp_in = jnp.einsum("rf,df->rd", grad_pre, up_weight, preferred_element_type=jnp.float32)
    grad_attn = jnp.einsum("rd,kd->rk", grad_low, dense_weight, preferred_element_type=jnp.float32)
    grad_attn = grad_attn.astype(jnp.bfloat16).reshape(seq_count, block_len, head_count, HS)
    scores = score_block()
    prob = jnp.exp(scores - log_total)
    grad_prob = jnp.einsum(
        "sqhd,skhd->shqk", grad_attn, value_whole, preferred_element_type=jnp.float32
    )
    delta = jnp.sum(grad_prob * prob, -1, keepdims=True)
    grad_scores = (prob * (grad_prob - delta)).astype(jnp.bfloat16)
    grad_query = (
        jnp.einsum("shqk,skhd->sqhd", grad_scores, key_whole, preferred_element_type=jnp.float32)
        * score_scale
    )
    grad_key_whole = (
        jnp.einsum("shqk,sqhd->skhd", grad_scores, query_rows, preferred_element_type=jnp.float32)
        * score_scale
    )
    grad_value_whole = jnp.einsum(
        "shqk,sqhd->skhd", prob.astype(jnp.bfloat16), grad_attn, preferred_element_type=jnp.float32
    )
    grad_key_rows, grad_value_rows = (
        lax.psum_scatter(
            grad_key_whole.reshape(seq_count, length, head_count * HS),
            "ctx",
            scatter_dimension=1,
            tiled=True,
        ),
        lax.psum_scatter(
            grad_value_whole.reshape(seq_count, length, head_count * HS),
            "ctx",
            scatter_dimension=1,
            tiled=True,
        ),
    )
    grad_key_rows = grad_key_rows.reshape(seq_count, block_len, head_count, HS)
    grad_value_rows = grad_value_rows.reshape(seq_count, block_len, head_count, HS)
    grad_qkv = jnp.stack(
        [
            rotate_back(grad_query, cosine_table, sine_table),
            rotate_back(grad_key_rows, cosine_table, sine_table),
            grad_value_rows,
        ],
        3,
    )
    grad_qkv = grad_qkv.reshape(row_count, head_count * 3 * HS).astype(jnp.bfloat16)
    grad_qkv_weight = jnp.einsum("rd,rc->dc", attn_in, grad_qkv, preferred_element_type=jnp.float32)
    grad_qkv_bias = jnp.sum(grad_qkv.astype(jnp.float32), 0)
    grad_attn_in = jnp.einsum("rc,dc->rd", grad_qkv, qkv_weight, preferred_element_type=jnp.float32)
    norm_parts = jnp.stack(
        [
            jnp.sum(grad_attn_in * normed, 0),
            jnp.sum(grad_attn_in, 0),
            jnp.sum(grad_mlp_in * normed, 0),
            jnp.sum(grad_mlp_in, 0),
        ]
    )
    grad_normed = grad_attn_in * attn_norm_gain + grad_mlp_in * mlp_norm_gain
    input_part = inv_std * (
        grad_normed
        - jnp.mean(grad_normed, -1, keepdims=True)
        - normed * jnp.mean(grad_normed * normed, -1, keepdims=True)
    )
    input_summed, norm_summed = lax.psum((input_part, norm_parts), "tensor")
    input_grad = (
        (grad_out + input_summed).astype(jnp.bfloat16).reshape(seq_count, block_len, model_width)
    )
    matrices = (grad_qkv_weight, grad_dense_weight, grad_up_weight, grad_down_weight)
    matrices = (
        lax.psum_scatter(matrices[0], ("dp", "ctx"), scatter_dimension=0, tiled=True),
        lax.psum_scatter(matrices[1], ("dp", "ctx"), scatter_dimension=1, tiled=True),
        lax.psum_scatter(matrices[2], ("dp", "ctx"), scatter_dimension=0, tiled=True),
        lax.psum_scatter(matrices[3], ("dp", "ctx"), scatter_dimension=1, tiled=True),
    )
    qkv_bias_sum, up_bias_sum, out_bias_sum, norm_total = lax.psum(
        (grad_qkv_bias, grad_up_bias, grad_out_bias, norm_summed), ("dp", "ctx")
    )
    return (
        layer_out,
        input_grad,
        norm_total[0],
        norm_total[1],
        matrices[0],
        qkv_bias_sum,
        matrices[1],
        out_bias_sum,
        norm_total[2],
        norm_total[3],
        matrices[2],
        up_bias_sum,
        matrices[3],
        out_bias_sum,
    )


def solution(mesh):
    return jax.shard_map(
        local,
        mesh=mesh,
        in_specs=(
            P("dp", "ctx", None),
            P(),
            P(),
            P(None, "tensor"),
            P("tensor"),
            P("tensor", None),
            P(),
            P(),
            P(),
            P(None, "tensor"),
            P("tensor"),
            P("tensor", None),
            P(),
            P("dp", "ctx", None),
            P("dp", "ctx"),
            P(),
        ),
        out_specs=(
            P("dp", "ctx", None),
            P("dp", "ctx", None),
            P(),
            P(),
            P(("dp", "ctx"), "tensor"),
            P("tensor"),
            P("tensor", ("dp", "ctx")),
            P(),
            P(),
            P(),
            P(("dp", "ctx"), "tensor"),
            P("tensor"),
            P("tensor", ("dp", "ctx")),
            P(),
        ),
        check_vma=False,
    )
```

profile of v0, /device:TPU:0, one launch (start us, length us, event | category | flops | bytes accessed | tf_op | source)
XLA Modules:
  0.0 1457.9 jit_solution(5055319917337510442)
XLA Ops:
  10.3 10.0 convolution_add_fusion.1
  42.8 3.9 convolution_convert_fusion
  47.4 19.8 %all-gather.5.cloned.1.call-done = bf16[1,1024,1024]{1,2,0:T(8,128)(2,1)} async-done(((bf16[1,256,1024]{1,2,0:T(8,128)(2,1)}), bf16[1,1024,1024]{1,2,0:T(8,128)(2,1)}) %all-gather.5.cloned.1.call-update) | async-done | bytes 2097168 | tf_op jit(solution)/shard_map/all_gather | solution.py:80
  73.0 19.2 %all-gather.3.cloned.1.call-done = bf16[1,1024,1024]{1,2,0:T(8,128)(2,1)} async-done(((bf16[1,256,1024]{1,2,0:T(8,128)(2,1)}), bf16[1,1024,1024]{1,2,0:T(8,128)(2,1)}) %all-gather.3.cloned.1.call-update) | async-done | bytes 2097168 | tf_op jit(solution)/shard_map/all_gather | solution.py:83
  92.2 4.3 multiply_reduce_fusion
  100.6 5.0 fusion.41
  107.0 20.1 %multiply_convert_fusion.1 = (bf16[256,4096]{1,0:T(8,128)(2,1)S(1)}, f32[256,4096]{1,0:T(8,128)}, f32[256,4096]{1,0:T(8,128)}) fusion(f32[4096]{0:T(1024)S(1)} %copy-done.33, bf16[2048,4096]{1,0:T(8,128)(2,1)} %param.25, bf16[1,256,2048]{2,1,0:T(8,128)(2,1)S(1)} %copy-done.3, f32[2048]{0:T(1024)S(1)} %copy-done.25, f32[2048]{0:T(1024)S(1)} %copy-done.26, ...), kind=kOutput, calls=%fused_computation.8 | convolution fusion | flops 4367319040 | bytes 28346368 | tf_op jit(solution)/shard_map/dot_general | solution.py:110
  127.1 10.3 fusion.92
  137.4 13.4 convert_reduce_fusion
  150.8 14.2 fusion.93
  178.3 14.0 reduce-scatter.9.cloned.1.call-done
  201.8 10.3 fusion.85
  214.8 9.0 psum.51
  223.9 98.8 %all-reduce.7.cloned.1.call-done = (f32[256,2048]{1,0:T(8,128)}, f32[256,2048]{1,0:T(8,128)}) async-done(((f32[256,2048]{1,0:T(8,128)}, f32[256,2048]{1,0:T(8,128)}), (f32[256,2048]{1,0:T(8,128)}, f32[256,2048]{1,0:T(8,128)})) %all-reduce.7.cloned.1.call-update) | async-done | bytes 4194320 | tf_op jit(solution)/shard_map/psum | solution.py:115
  322.7 3.5 fusion.29
  326.3 4.7 fusion.52
  331.6 11.8 fusion.48
  343.5 14.9 %fusion.82 = f32[2048,4096]{1,0:T(8,128)} fusion(bf16[256,4096]{1,0:T(8,128)(2,1)} %get-tuple-element.65, bf16[1,256,2048]{2,1,0:T(8,128)(2,1)S(1)} %copy-done.3, f32[2048]{0:T(1024)S(1)} %copy-done.25, f32[2048]{0:T(1024)S(1)} %copy-done.26, f32[256]{0:T(256)S(1)} %add_rsqrt_fusion, f32[256]{0:T(256)S(1)} %broadcast_multiply_fusion.3), kind=kOutput, calls=%fused_computation.138 | convolution fusion | flops 4298113024 | bytes 36718592 | tf_op jit(solution)/shard_map/rd,rf->df/dot_general | solution.py:133
  358.5 15.1 %fusion.75 = f32[4096,2048]{1,0:T(8,128)} fusion(bf16[256,4096]{1,0:T(8,128)(2,1)} %copy-done.13, bf16[1,256,2048]{2,1,0:T(8,128)(2,1)S(1)} %copy-done.6, f32[256]{0:T(256)S(1)} %fusion.71), kind=kOutput, calls=%fused_computation.136 | convolution fusion | flops 4296540160 | bytes 36701184 | tf_op jit(solution)/shard_map/rf,rd->fd/dot_general | solution.py:124
  376.5 37.6 %all-reduce.5.cloned.1.call-done = (f32[4,2048]{1,0:T(4,128)}, f32[3072]{0:T(1024)}, f32[2048]{0:T(1024)}, f32[4096]{0:T(1024)}) async-done(((f32[4,2048]{1,0:T(4,128)}, f32[3072]{0:T(1024)}, f32[2048]{0:T(1024)}, f32[4096]{0:T(1024)}), (f32[4,2048]{1,0:T(4,128)}, f32[3072]{0:T(1024)}, f32[2048]{0:T(1024)}, f32[4096]{0:T(1024)})) %all-reduce.5.cloned.1.call-update) | async-done | bytes 69648 | tf_op jit(solution)/shard_map/psum | solution.py:209
  415.7 108.8 %reduce-scatter.13.cloned.1.call-done = f32[1024,128]{1,0:T(8,128)} async-done(((f32[1024,2048]{1,0:T(8,128)}), f32[1024,128]{1,0:T(8,128)}) %reduce-scatter.13.cloned.1.call-update) | async-done | bytes 524304 | tf_op jit(solution)/shard_map/reduce_scatter | solution.py:205
  524.5 248.3 %reduce-scatter.11.cloned.1.call-done = f32[128,3072]{1,0:T(8,128)} async-done(((f32[2048,3072]{1,0:T(8,128)}), f32[128,3072]{1,0:T(8,128)}) %reduce-scatter.11.cloned.1.call-update) | async-done | bytes 1572880 | tf_op jit(solution)/shard_map/reduce_scatter | solution.py:204
  772.8 336.5 %reduce-scatter.15.cloned.1.call-done = f32[128,4096]{1,0:T(8,128)} async-done(((f32[2048,4096]{1,0:T(8,128)}), f32[128,4096]{1,0:T(8,128)}) %reduce-scatter.15.cloned.1.call-update) | async-done | bytes 2097168 | tf_op jit(solution)/shard_map/reduce_scatter | solution.py:206
  1109.3 336.3 %reduce-scatter.17.cloned.1.call-done = f32[4096,128]{1,0:T(8,128)} async-done(((f32[4096,2048]{1,0:T(8,128)}), f32[4096,128]{1,0:T(8,128)}) %reduce-scatter.17.cloned.1.call-update) | async-done | bytes 2097168 | tf_op jit(solution)/shard_map/reduce_scatter | solution.py:207
  (146 shorter events, 73.3 us)
Async XLA Ops:
  7.2 60.0 %all-gather.5.cloned.1.call-start = ((), (), s32[]{:S(2)}) async-start(), calls=%async_computation.7 | async-start | bytes 2621440 | tf_op jit(solution)/shard_map/all_gather | solution.py:80
  35.4 7.2 copy-start.31
  35.4 7.2 copy-start.32
  41.5 50.7 %all-gather.3.cloned.1.call-start = ((), (), s32[]{:S(2)}) async-start(), calls=%async_computation.6 | async-start | bytes 2621440 | tf_op jit(solution)/shard_map/all_gather | solution.py:83
  42.4 133.0 %reduce-scatter.7.cloned.1.call-start = ((), (), s32[]{:S(2)}) async-start(), calls=%async_computation.8 | async-start | bytes 5242880 | tf_op jit(solution)/shard_map/reduce_scatter | solution.py:157
  42.8 4.4 copy-start.4
  42.8 24.4 %copy-start.23 = (bf16[256,4,64]{2,0,1:T(8,128)(2,1)S(1)}, bf16[256,4,64]{2,0,1:T(8,128)(2,1)}, u32[]{:S(2)}) copy-start(bf16[256,4,64]{2,0,1:T(8,128)(2,1)} %get-tuple-element.47) | copy-start | bytes 393220
  46.9 45.3 %copy-start.10 = (bf16[256,1024]{0,1:T(8,128)(2,1)}, bf16[256,1024]{0,1:T(8,128)(2,1)S(1)}, u32[]{:S(2)}) copy-start(bf16[256,1024]{0,1:T(8,128)(2,1)S(1)} %copy.91) | copy-start | bytes 1572868
  47.4 25.6 %copy-start.15 = (bf16[256,4,192]{2,0,1:T(8,128)(2,1)}, bf16[256,4,192]{2,0,1:T(8,128)(2,1)S(1)}, u32[]{:S(2)}) copy-start(bf16[256,4,192]{2,0,1:T(8,128)(2,1)S(1)} %fusion.65) | copy-start | bytes 1179652
  92.2 4.3 copy-start.1
  100.5 91.8 %reduce-scatter.9.cloned.1.call-start = ((), (), s32[]{:S(2)}) async-start(), calls=%async_computation.9 | async-start | bytes 5242880 | tf_op jit(solution)/shard_map/reduce_scatter | solution.py:163
  105.6 217.1 %all-reduce.7.cloned.1.call-start = ((), (), s32[]{:S(2)}) async-start(), calls=%async_computation.15 | async-start | bytes 8388608 | tf_op jit(solution)/shard_map/psum | solution.py:115
  127.1 10.3 copy-start.13
  127.1 10.3 copy-start.5
  165.0 4.9 copy-start.2
  165.0 4.9 copy-start.22
  175.4 21.3 %copy-start.8 = (f32[1,256,4,256]{3,1,2,0:T(8,128)S(1)}, f32[1,256,4,256]{3,1,2,0:T(8,128)}, u32[]{:S(2)}) copy-start(f32[1,256,4,256]{3,1,2,0:T(8,128)} %copy-done.7) | copy-start | bytes 3145732
  201.8 10.3 copy-start.9
  212.1 110.6 %copy-start.6 = (bf16[1,256,2048]{2,1,0:T(8,128)(2,1)S(1)}, bf16[1,256,2048]{2,1,0:T(8,128)(2,1)}, u32[]{:S(2)}) copy-start(bf16[1,256,2048]{2,1,0:T(8,128)(2,1)} %param.29) | copy-start | bytes 3145732
  214.1 200.0 %all-reduce.5.cloned.1.call-start = ((), (), s32[]{:S(2)}) async-start(), calls=%async_computation.14 | async-start | bytes 139264 | tf_op jit(solution)/shard_map/psum | solution.py:209
  326.2 198.3 %reduce-scatter.13.cloned.1.call-start = ((), (), s32[]{:S(2)}) async-start(), calls=%async_computation.11 | async-start | bytes 8912896 | tf_op jit(solution)/shard_map/reduce_scatter | solution.py:205
  331.0 441.8 %reduce-scatter.11.cloned.1.call-start = ((), (), s32[]{:S(2)}) async-start(), calls=%async_computation.10 | async-start | bytes 26738688 | tf_op jit(solution)/shard_map/reduce_scatter | solution.py:204
  343.5 765.8 %reduce-scatter.15.cloned.1.call-start = ((), (), s32[]{:S(2)}) async-start(), calls=%async_computation.12 | async-start | bytes 35651584 | tf_op jit(solution)/shard_map/reduce_scatter | solution.py:206
  358.5 1087.1 %reduce-scatter.17.cloned.1.call-start = ((), (), s32[]{:S(2)}) async-start(), calls=%async_computation.13 | async-start | bytes 35651584 | tf_op jit(solution)/shard_map/reduce_scatter | solution.py:207
  (20 other events, 35.7 us)
Sparse Core Ops, SparseCore 0:
  41.6 25.5 all-gather.4
  69.3 22.8 all-gather.2
  100.7 44.4 reduce-scatter.6
  147.7 44.5 reduce-scatter.8
  214.2 108.3 all-reduce.6
  328.0 86.0 all-reduce.4
  418.8 105.6 reduce-scatter.12
  529.2 243.5 reduce-scatter.10
  777.6 331.6 reduce-scatter.14
  1114.0 331.6 reduce-scatter.16
where the time goes:
time: 1460 us
  waiting for transfers between devices  1220 us (84%)
  matrix products  150 us (10%)
  local copies, waits for them, and re-layouts  40.4 us (3%)
  other arithmetic  22.9 us (2%)
  between operations  14.8 us (1%)
    reduce_scatter x1, waiting for transfers between devices, local(): lax.psum_scatter(matrices[2], ('dp', 'ctx'), scatter_dimension=0, tiled=T...  337 us
    reduce_scatter x1, waiting for transfers between devices, local(): lax.psum_scatter(matrices[3], ('dp', 'ctx'), scatter_dimension=1, tiled=T...  336 us
    reduce_scatter x1, waiting for transfers between devices, local(): lax.psum_scatter(matrices[0], ('dp', 'ctx'), scatter_dimension=0, tiled=T...  248 us
    reduce_scatter x1, waiting for transfers between devices, local(): lax.psum_scatter(matrices[1], ('dp', 'ctx'), scatter_dimension=1, tiled=T...  109 us
    psum x1, waiting for transfers between devices, local(): summed = lax.psum(partial_sum, 'tensor')  98.8 us
    psum x1, waiting for transfers between devices, local(): lax.psum((grad_qkv_bias, grad_up_bias, grad_out_bias, norm_summed), ('dp'...  37.6 us
  transfers between devices with their start and end apart: 10, of which 9 were waited for; matrix products, arithmetic and copies ran while one was open for 9% of the time, Pallas kernels for 0%

commit v1 on v0

v1 whole, which is shorter than its diff:
```python
import math

import jax
import jax.numpy as jnp
from jax import lax
from jax.sharding import PartitionSpec as P

HS = 256
ROT = 64


NORM_EPS = 1e-05


def rope_tables(positions, rot_dims):
    half_dims = rot_dims // 2
    freqs = 10000.0 ** (-(jnp.arange(half_dims, dtype=jnp.float32) * 2.0 / rot_dims))
    angles = positions.astype(jnp.float32)[:, None] * freqs[None, :]
    return (
        jnp.concatenate([jnp.cos(angles), jnp.cos(angles)], -1),
        jnp.concatenate([jnp.sin(angles), jnp.sin(angles)], -1),
    )


def rotate(columns, cosine_table, sine_table):
    half_dims = ROT // 2
    leading = columns[..., :ROT]
    turned = jnp.concatenate([-leading[..., half_dims:], leading[..., :half_dims]], -1)
    moved = leading * cosine_table[:, None, :] + turned * sine_table[:, None, :]
    return jnp.concatenate([moved, columns[..., ROT:]], -1)


def rotate_back(gradient, cosine_table, sine_table):
    half_dims = ROT // 2
    leading = gradient[..., :ROT]
    scaled = leading * sine_table[:, None, :]
    turned = jnp.concatenate([scaled[..., half_dims:], -scaled[..., :half_dims]], -1)
    moved = leading * cosine_table[:, None, :] + turned
    return jnp.concatenate([moved, gradient[..., ROT:]], -1)


def swap(array, axis, bit):
    pairs = [(place, place ^ bit) for place in range(lax.axis_size(axis))]
    return lax.ppermute(array, axis, pairs)


def bits_down(axis):
    size = lax.axis_size(axis)
    return [1 << level for level in reversed(range(size.bit_length() - 1))]


def relative_blocks(array, axis, dim):
    place = lax.axis_index(axis)
    for bit in bits_down(axis):
        size = array.shape[dim]
        halves = array.reshape(
            array.shape[:dim] + (size // (2 * bit), 2, bit) + array.shape[dim + 1 :]
        )
        flipped = jnp.flip(halves, dim + 1)
        array = jnp.where((place & bit) != 0, flipped, halves).reshape(array.shape)
    return array


def gather_rows(rows, axis):
    for bit in bits_down(axis):
        rows = jnp.concatenate([rows, swap(rows, axis, bit)], 0)
    return rows


def exchange_rows(rows, axis):
    for bit in bits_down(axis):
        rows = jnp.concatenate([rows[:, :bit], swap(rows[:, bit:], axis, bit)], 0)
    return rows[:, 0]


def block_order(size):
    order = [0]
    bit = size // 2
    while bit:
        order = order + [entry ^ bit for entry in order]
        bit //= 2
    return order


def tensor_sum(part):
    if lax.axis_size("tensor") == 2:
        low = part.astype(jnp.bfloat16)
        return low.astype(jnp.float32) + swap(low, "tensor", 1).astype(jnp.float32)
    return lax.psum(part, "tensor")


def reduce_line(left, right, spec, dim):
    size = lax.axis_size("dp")
    width = left.shape[1] // size
    arrived = None
    bits = [1 << level for level in range(size.bit_length() - 1)]
    count = size
    total = None
    for bit in bits:
        count //= 2
        if total is None:
            send = jnp.einsum(
                spec, left[:, count * width :], right, preferred_element_type=jnp.float32
            )
            keep = jnp.einsum(
                spec, left[:, : count * width], right, preferred_element_type=jnp.float32
            )
        else:
            keep = lax.slice_in_dim(total, 0, count * width, axis=dim)
            send = lax.slice_in_dim(total, count * width, 2 * count * width, axis=dim)
        arrived = swap(send.astype(jnp.bfloat16), "dp", bit)
        total = keep + arrived.astype(jnp.float32)
    return total


def reduce_blocks(total, axis, dim, bits=None):
    size = lax.axis_size(axis)
    for bit in [1 << level for level in range(size.bit_length() - 1)]:
        half = total.shape[dim] // 2
        keep = lax.slice_in_dim(total, 0, half, axis=dim)
        send = lax.slice_in_dim(total, half, 2 * half, axis=dim)
        arrived = swap(send.astype(jnp.bfloat16), axis, bit)
        total = keep + arrived.astype(jnp.float32)
    return total


def spread_columns(rows):
    dp_size, ctx_size = lax.axis_size("dp"), lax.axis_size("ctx")
    width = rows.shape[1] // (dp_size * ctx_size)
    blocks = rows.reshape(rows.shape[0], dp_size, ctx_size, width)
    blocks = relative_blocks(relative_blocks(blocks, "dp", 1), "ctx", 2)
    blocks = jnp.stack([blocks[:, entry] for entry in block_order(dp_size)], 2)
    return blocks.reshape(rows.shape[0], ctx_size, dp_size * width)


def local(
    hidden_in,
    attn_norm_gain,
    attn_norm_bias,
    qkv_weight,
    qkv_bias,
    dense_weight,
    dense_bias,
    mlp_norm_gain,
    mlp_norm_bias,
    up_weight,
    up_bias,
    down_weight,
    down_bias,
    out_cotangent,
    subset_ids,
    subset_weights,
):
    seq_count, block_len, model_width = hidden_in.shape
    row_count = seq_count * block_len
    head_count = qkv_weight.shape[1] // (3 * HS)
    ctx_size = lax.axis_size("ctx")
    length = block_len * ctx_size
    score_scale = 1.0 / math.sqrt(HS)
    low_type = jnp.bfloat16
    hidden_rows = hidden_in.reshape(row_count, model_width)
    inputs = hidden_rows.astype(jnp.float32)
    row_mean = jnp.mean(inputs, -1, keepdims=True)
    centered = inputs - row_mean
    inv_std = lax.rsqrt(jnp.mean(centered * centered, -1, keepdims=True) + NORM_EPS)
    normed = centered * inv_std
    attn_in = (normed * attn_norm_gain + attn_norm_bias).astype(low_type)
    mlp_in = (normed * mlp_norm_gain + mlp_norm_bias).astype(low_type)

    subset_count = subset_weights.shape[0]
    matches = subset_ids[..., None] == jnp.arange(subset_count, dtype=jnp.int32)
    row_weight = jnp.sum(jnp.where(matches, subset_weights, 0.0), -1).reshape(row_count, 1)
    grad_out = out_cotangent.reshape(row_count, model_width).astype(jnp.float32) * row_weight
    grad_low = grad_out.astype(low_type)
    grad_out_bias = jnp.sum(grad_out, 0)

    low_part = exchange_rows(spread_columns(grad_low), "ctx")
    hidden_part = exchange_rows(spread_columns(hidden_rows), "ctx").astype(jnp.float32)
    stats = gather_rows(jnp.stack([row_mean[:, 0], inv_std[:, 0]])[None], "ctx")
    mean_all = stats[:, 0].reshape(ctx_size * row_count, 1)
    std_all = stats[:, 1].reshape(ctx_size * row_count, 1)
    normed_part = (hidden_part - mean_all) * std_all

    def own_columns(vector):
        return spread_columns(vector[None])[:, 0]

    mlp_part = (
        normed_part * own_columns(mlp_norm_gain) + own_columns(mlp_norm_bias)
    ).astype(low_type)
    attn_part = (
        normed_part * own_columns(attn_norm_gain) + own_columns(attn_norm_bias)
    ).astype(low_type)

    hidden_units = up_weight.shape[1]
    pieces = max(1, hidden_units // 1024)
    span = hidden_units // pieces
    down_grads, up_grads, up_bias_parts = [], [], []
    branch_part, grad_mlp_in = None, None
    for piece in range(pieces):
        cols = slice(piece * span, (piece + 1) * span)
        up_pre = (
            jnp.dot(mlp_in, up_weight[:, cols], preferred_element_type=jnp.float32) + up_bias[cols]
        )
        activated = jax.nn.gelu(up_pre, approximate=False).astype(low_type)
        activated_all = gather_rows(activated, "ctx")
        down_grads.append(reduce_line(low_part, activated_all, "rd,rf->fd", 1))
        grad_act = jnp.einsum(
            "rd,fd->rf", grad_low, down_weight[cols], preferred_element_type=jnp.float32
        )
        gelu_back = jax.vjp(lambda pre_act: jax.nn.gelu(pre_act, approximate=False), up_pre)[1]
        grad_pre = gelu_back(grad_act)[0].astype(low_type)
        grad_pre_all = gather_rows(grad_pre, "ctx")
        up_grads.append(reduce_line(mlp_part, grad_pre_all, "rd,rf->df", 0))
        up_bias_parts.append(jnp.sum(grad_pre.astype(jnp.float32), 0))
        more = jnp.dot(activated, down_weight[cols], preferred_element_type=jnp.float32)
        branch_part = more if branch_part is None else branch_part + more
        more = jnp.einsum(
            "rf,df->rd", grad_pre, up_weight[:, cols], preferred_element_type=jnp.float32
        )
        grad_mlp_in = more if grad_mlp_in is None else grad_mlp_in + more

    qkv_all = jnp.dot(attn_in, qkv_weight, preferred_element_type=jnp.float32) + qkv_bias
    qkv_all = qkv_all.reshape(seq_count, block_len, head_count, 3, HS)
    place = lax.axis_index("ctx")
    steps = jnp.arange(block_len, dtype=jnp.int32)
    positions = place * block_len + steps
    cosine_table, sine_table = rope_tables(positions, ROT)
    query_rows = rotate(qkv_all[:, :, :, 0], cosine_table, sine_table).astype(low_type)
    key_rows = rotate(qkv_all[:, :, :, 1], cosine_table, sine_table).astype(low_type)
    value_rows = qkv_all[:, :, :, 2].astype(low_type)
    pair = jnp.stack([key_rows, value_rows], 0).reshape(2 * seq_count, block_len, head_count * HS)
    whole = gather_rows(jnp.swapaxes(pair, 0, 1), "ctx")
    whole = jnp.swapaxes(whole, 0, 1).reshape(2, seq_count, length, head_count, HS)
    key_whole, value_whole = whole[0], whole[1]
    key_positions = jnp.concatenate(
        [(place ^ entry) * block_len + steps for entry in block_order(ctx_size)]
    )
    causal = key_positions[None, :] <= positions[:, None]
    raw = jnp.einsum("sqhd,skhd->shqk", query_rows, key_whole, preferred_element_type=jnp.float32)
    scores = jnp.where(causal, raw * score_scale, -1e30)
    row_max = jnp.max(scores, -1, keepdims=True)
    expd = jnp.exp(scores - row_max)
    prob = expd / jnp.sum(expd, -1, keepdims=True)
    prob_low = prob.astype(low_type)
    attn_out = jnp.einsum(
        "shqk,skhd->sqhd", prob_low, value_whole, preferred_element_type=jnp.float32
    ).astype(low_type)
    attn_out = attn_out.reshape(row_count, head_count * HS)
    attn_out_all = gather_rows(attn_out, "ctx")
    grad_dense_weight = reduce_line(low_part, attn_out_all, "rd,rf->fd", 1)
    branch_part = branch_part + jnp.dot(
        attn_out, dense_weight, preferred_element_type=jnp.float32
    )
    layer_out = (inputs + tensor_sum(branch_part) + dense_bias + down_bias).astype(low_type)
    layer_out = layer_out.reshape(seq_count, block_len, model_width)

    grad_attn = jnp.einsum("rd,kd->rk", grad_low, dense_weight, preferred_element_type=jnp.float32)
    grad_attn = grad_attn.astype(low_type).reshape(seq_count, block_len, head_count, HS)
    grad_prob = jnp.einsum(
        "sqhd,skhd->shqk", grad_attn, value_whole, preferred_element_type=jnp.float32
    )
    delta = jnp.sum(grad_prob * prob, -1, keepdims=True)
    grad_scores = (prob * (grad_prob - delta)).astype(low_type)
    grad_query = (
        jnp.einsum("shqk,skhd->sqhd", grad_scores, key_whole, preferred_element_type=jnp.float32)
        * score_scale
    )
    grad_key_whole = (
        jnp.einsum("shqk,sqhd->kshd", grad_scores, query_rows, preferred_element_type=jnp.float32)
        * score_scale
    )
    grad_value_whole = jnp.einsum(
        "shqk,sqhd->kshd", prob_low, grad_attn, preferred_element_type=jnp.float32
    )
    grad_pair = jnp.concatenate(
        [
            grad_key_whole.reshape(length, seq_count * head_count * HS),
            grad_value_whole.reshape(length, seq_count * head_count * HS),
        ],
        1,
    )
    grad_pair = reduce_blocks(grad_pair, "ctx", 0)
    grad_pair = grad_pair.reshape(block_len, 2, seq_count, head_count, HS)
    grad_key_rows = jnp.swapaxes(grad_pair[:, 0], 0, 1)
    grad_value_rows = jnp.swapaxes(grad_pair[:, 1], 0, 1)
    grad_qkv = jnp.stack(
        [
            rotate_back(grad_query, cosine_table, sine_table),
            rotate_back(grad_key_rows, cosine_table, sine_table),
            grad_value_rows,
        ],
        3,
    )
    grad_qkv = grad_qkv.reshape(row_count, head_count * 3 * HS).astype(low_type)
    qkv_grads = []
    for head in range(head_count):
        piece = grad_qkv[:, head * 3 * HS : (head + 1) * 3 * HS]
        qkv_grads.append(reduce_line(attn_part, gather_rows(piece, "ctx"), "rd,rc->dc", 0))
    grad_qkv_bias = jnp.sum(grad_qkv.astype(jnp.float32), 0)
    grad_attn_in = jnp.einsum("rc,dc->rd", grad_qkv, qkv_weight, preferred_element_type=jnp.float32)
    norm_parts = jnp.stack(
        [
            jnp.sum(grad_attn_in * normed, 0),
            jnp.sum(grad_attn_in, 0),
            jnp.sum(grad_mlp_in * normed, 0),
            jnp.sum(grad_mlp_in, 0),
        ]
    )
    grad_normed = grad_attn_in * attn_norm_gain + grad_mlp_in * mlp_norm_gain
    input_part = inv_std * (
        grad_normed
        - jnp.mean(grad_normed, -1, keepdims=True)
        - normed * jnp.mean(grad_normed * normed, -1, keepdims=True)
    )
    input_grad = (
        (grad_out + tensor_sum(input_part))
        .astype(low_type)
        .reshape(seq_count, block_len, model_width)
    )
    norm_total = lax.psum(norm_parts, ("dp", "ctx", "tensor"))
    qkv_bias_sum, up_bias_sum, out_bias_sum = lax.psum(
        (grad_qkv_bias, jnp.concatenate(up_bias_parts), grad_out_bias), ("dp", "ctx")
    )
    return (
        layer_out,
        input_grad,
        norm_total[0],
        norm_total[1],
        jnp.concatenate(qkv_grads, 1),
        qkv_bias_sum,
        grad_dense_weight,
        out_bias_sum,
        norm_total[2],
        norm_total[3],
        jnp.concatenate(up_grads, 1),
        up_bias_sum,
        jnp.concatenate(down_grads, 0),
        out_bias_sum,
    )


def solution(mesh):
    return jax.shard_map(
        local,
        mesh=mesh,
        in_specs=(
            P("dp", "ctx", None),
            P(),
            P(),
            P(None, "tensor"),
            P("tensor"),
            P("tensor", None),
            P(),
            P(),
            P(),
            P(None, "tensor"),
            P("tensor"),
            P("tensor", None),
            P(),
            P("dp", "ctx", None),
            P("dp", "ctx"),
            P(),
        ),
        out_specs=(
            P("dp", "ctx", None),
            P("dp", "ctx", None),
            P(),
            P(),
            P(("dp", "ctx"), "tensor"),
            P("tensor"),
            P("tensor", ("dp", "ctx")),
            P(),
            P(),
            P(),
            P(("dp", "ctx"), "tensor"),
            P("tensor"),
            P("tensor", ("dp", "ctx")),
            P(),
        ),
        check_vma=False,
    )
```

time: 1460 us -> 702 us (0.48)
  waiting for transfers between devices: 1220 us -> 248 us
  blocking collectives: 9.04 us -> 121 us
  other arithmetic: 22.9 us -> 74.1 us
  starting transfers between devices: 0.88 us -> 51.7 us
    reduce_scatter x6 -> x0, waiting for transfers between devices: 1040 us -> none  [the longest x1 337 us: local(): lax.psum_scatter(matrices[2], ('dp', 'ctx'), scatter_dimension=0, tiled=T...]
    ppermute x0 -> x64, waiting for transfers between devices: none -> 248 us  [swap(): return lax.ppermute(array, axis, pairs)]
    psum x2 -> x0, waiting for transfers between devices: 136 us -> none  [the longest x1 98.8 us: local(): summed = lax.psum(partial_sum, 'tensor')]
    psum x1 -> x2, blocking collectives: 9.04 us -> 121 us  [the longest x1 61.6 us: local(): lax.psum((grad_qkv_bias, jnp.concatenate(up_bias_parts), grad_out_bias),...]
    ppermute x0 -> x64, starting transfers between devices: none -> 51.7 us  [swap(): return lax.ppermute(array, axis, pairs)]
    all_gather x2 -> x0, waiting for transfers between devices: 38.9 us -> none  [the longest x1 19.8 us: local(): lax.all_gather(key_rows.reshape(seq_count, block_len, head_count * HS), '...]
    concatenate x0 -> x25, other arithmetic: none -> 29 us  [the longest x16 24.4 us: gather_rows(): rows = jnp.concatenate([rows, swap(rows, axis, bit)], 0)]
    dot_general x12 -> x46, matrix products: 116 us -> 119 us  [the longest x13 24 us: reduce_line(): jnp.einsum(spec, left[:, count * width:], right, preferred_element_type=j...]
  transfers between devices with their start and end apart: 10 -> 64, of which waited for: 9 -> 27; matrix products, arithmetic and copies ran while one was open for 9% -> 36% of each run, Pallas kernels for 0% -> 0%
where the time goes in v1:
time: 702 us; the launch traced here: 692 us
  waiting for transfers between devices  248 us (35%)
  matrix products  147 us (21%)
  blocking collectives  121 us (17%)
  other arithmetic  74.1 us (11%)
  starting transfers between devices  51.7 us (7%)
  local copies, waits for them, and re-layouts  46.3 us (7%)
    ppermute x64, waiting for transfers between devices, swap(): return lax.ppermute(array, axis, pairs)  248 us
    psum x1, blocking collectives, local(): lax.psum((grad_qkv_bias, jnp.concatenate(up_bias_parts), grad_out_bias),...  61.6 us
    psum x1, blocking collectives, local(): norm_total = lax.psum(norm_parts, ('dp', 'ctx', 'tensor'))  59.7 us
    ppermute x64, starting transfers between devices, swap(): return lax.ppermute(array, axis, pairs)  51.7 us
    concatenate x16, other arithmetic, gather_rows(): rows = jnp.concatenate([rows, swap(rows, axis, bit)], 0)  24.4 us
    dot_general x13, matrix products, reduce_line(): jnp.einsum(spec, left[:, count * width:], right, preferred_element_type=j...  24 us
    dot_general x13, matrix products, reduce_line(): jnp.einsum(spec, left[:, :count * width], right, preferred_element_type=j...  23.1 us
    dot_general x4, matrix products, local(): jnp.einsum('rd,fd->rf', grad_low, down_weight[cols], preferred_element_ty...  21.9 us
  transfers between devices with their start and end apart: 64, of which 27 were waited for; matrix products, arithmetic and copies ran while one was open for 36% of the time, Pallas kernels for 0%

profile of v1, /device:TPU:0, one launch (start us, length us, event | category | flops | bytes accessed | tf_op | source)
XLA Modules:
  0.0 691.7 jit_solution(6590537447660785061)
XLA Ops:
  4.1 6.9 multiply_convert_fusion.5
  34.3 9.9 %convolution_add_fusion = f32[256,3072]{1,0:T(8,128)} fusion(bf16[2048,3072]{1,0:T(8,128)(2,1)} %param.19, f32[3072]{0:T(1024)S(1)} %copy-done.93, bf16[1,256,2048]{2,1,0:T(8,128)(2,1)S(1)} %copy-done, f32[2048]{0:T(1024)S(1)} %copy-done.67, f32[2048]{0:T(1024)S(1)} %copy-done.70, f32[256]{0:T(256)S(1)} %add_rsqrt_fusion, f32[256]{0:T(256)S(1)} %broadcast_multiply_fusion.2), kind=kOutput, calls=%fused_computation.12 | convolution fusion | flops 3225157632 | bytes 16807936 | tf_op jit(solution)/shard_map/dot_general | solution.py:222
  85.4 7.3 %convert_reduce_fusion.5 = (f32[1024]{0:T(1024)}, bf16[256,1024]{1,0:T(8,128)(2,1)}) fusion(f32[256,1024]{1,0:T(8,128)S(1)} %copy-done.94, bf16[4096,2048]{1,0:T(8,128)(2,1)} %param.27, bf16[1,256,2048]{2,1,0:T(8,128)(2,1)S(1)} %copy-done.3, f32[256]{0:T(256)S(1)} %fusion.188), kind=kOutput, calls=%fused_computation.202 | convolution fusion | flops 1094712320 | bytes 6820864 | tf_op jit(solution)/shard_map/rd,fd->rf/dot_general | solution.py:207
  158.5 20.1 %collective-permute-done.6 = bf16[256,2,512]{0,2,1:T(8,128)(2,1)S(1)} collective-permute-done((bf16[256,2,512]{0,2,1:T(8,128)(2,1)S(1)}, bf16[256,2,512]{0,2,1:T(8,128)(2,1)S(1)}, u32[]{:S(2)}, u32[]{:S(2)}) %collective-permute-start.6) | collective-permute-done | bytes 524320 | tf_op jit(solution)/shard_map/ppermute | solution.py:44
  178.7 11.0 %collective-permute-done.28 = bf16[256,2,512]{0,2,1:T(8,128)(2,1)S(1)} collective-permute-done((bf16[256,2,512]{0,2,1:T(8,128)(2,1)S(1)}, bf16[256,2,512]{0,2,1:T(8,128)(2,1)S(1)}, u32[]{:S(2)}, u32[]{:S(2)}) %collective-permute-start.28) | collective-permute-done | bytes 524320 | tf_op jit(solution)/shard_map/ppermute | solution.py:44
  191.4 9.6 %collective-permute-done.40 = bf16[256,1024]{1,0:T(8,128)(2,1)S(1)} collective-permute-done((bf16[256,1024]{1,0:T(8,128)(2,1)}, bf16[256,1024]{1,0:T(8,128)(2,1)S(1)}, u32[]{:S(2)}, u32[]{:S(2)}) %collective-permute-start.40) | collective-permute-done | bytes 524320 | tf_op jit(solution)/shard_map/ppermute | solution.py:44
  203.3 31.0 %collective-permute-done.44 = bf16[256,1024]{1,0:T(8,128)(2,1)S(1)} collective-permute-done((bf16[256,1024]{1,0:T(8,128)(2,1)S(1)}, bf16[256,1024]{1,0:T(8,128)(2,1)S(1)}, u32[]{:S(2)}, u32[]{:S(2)}) %collective-permute-start.44) | collective-permute-done | bytes 524320 | tf_op jit(solution)/shard_map/ppermute | solution.py:44
  270.6 7.4 %collective-permute-done.54 = bf16[1024,256]{1,0:T(8,128)(2,1)S(1)} collective-permute-done((bf16[1024,256]{1,0:T(8,128)(2,1)S(1)}, bf16[1024,256]{1,0:T(8,128)(2,1)S(1)}, u32[]{:S(2)}, u32[]{:S(2)}) %collective-permute-start.54) | collective-permute-done | bytes 524320 | tf_op jit(solution)/shard_map/ppermute | solution.py:44
  281.8 7.4 %collective-permute-done.58 = bf16[1024,256]{1,0:T(8,128)(2,1)S(1)} collective-permute-done((bf16[1024,256]{1,0:T(8,128)(2,1)S(1)}, bf16[1024,256]{1,0:T(8,128)(2,1)S(1)}, u32[]{:S(2)}, u32[]{:S(2)}) %collective-permute-start.58) | collective-permute-done | bytes 524320 | tf_op jit(solution)/shard_map/ppermute | solution.py:44
  293.2 7.3 %collective-permute-done.62 = bf16[1024,256]{1,0:T(8,128)(2,1)S(1)} collective-permute-done((bf16[1024,256]{1,0:T(8,128)(2,1)S(1)}, bf16[1024,256]{1,0:T(8,128)(2,1)S(1)}, u32[]{:S(2)}, u32[]{:S(2)}) %collective-permute-start.62) | collective-permute-done | bytes 524320 | tf_op jit(solution)/shard_map/ppermute | solution.py:44
  304.0 7.7 %collective-permute-done.34 = bf16[256,1024]{1,0:T(8,128)(2,1)S(1)} collective-permute-done((bf16[256,1024]{1,0:T(8,128)(2,1)S(1)}, bf16[256,1024]{1,0:T(8,128)(2,1)S(1)}, u32[]{:S(2)}, u32[]{:S(2)}) %collective-permute-start.34) | collective-permute-done | bytes 524320 | tf_op jit(solution)/shard_map/ppermute | solution.py:44
  316.3 12.3 %collective-permute-done.38 = bf16[256,1024]{1,0:T(8,128)(2,1)S(1)} collective-permute-done((bf16[256,1024]{1,0:T(8,128)(2,1)S(1)}, bf16[256,1024]{1,0:T(8,128)(2,1)S(1)}, u32[]{:S(2)}, u32[]{:S(2)}) %collective-permute-start.38) | collective-permute-done | bytes 524320 | tf_op jit(solution)/shard_map/ppermute | solution.py:44
  332.3 13.1 %collective-permute-done.42 = bf16[256,1024]{1,0:T(8,128)(2,1)S(1)} collective-permute-done((bf16[256,1024]{1,0:T(8,128)(2,1)S(1)}, bf16[256,1024]{1,0:T(8,128)(2,1)S(1)}, u32[]{:S(2)}, u32[]{:S(2)}) %collective-permute-start.42) | collective-permute-done | bytes 524320 | tf_op jit(solution)/shard_map/ppermute | solution.py:44
  348.9 7.1 %collective-permute-done.46 = bf16[256,1024]{1,0:T(8,128)(2,1)S(1)} collective-permute-done((bf16[256,1024]{1,0:T(8,128)(2,1)S(1)}, bf16[256,1024]{1,0:T(8,128)(2,1)S(1)}, u32[]{:S(2)}, u32[]{:S(2)}) %collective-permute-start.46) | collective-permute-done | bytes 524320 | tf_op jit(solution)/shard_map/ppermute | solution.py:44
  364.0 21.9 %collective-permute-done.59 = bf16[1024,128]{1,0:T(8,128)(2,1)S(1)} collective-permute-done((bf16[1024,128]{1,0:T(8,128)(2,1)S(1)}, bf16[1024,128]{1,0:T(8,128)(2,1)S(1)}, u32[]{:S(2)}, u32[]{:S(2)}) %collective-permute-start.59) | collective-permute-done | bytes 262176 | tf_op jit(solution)/shard_map/ppermute | solution.py:44
  386.0 11.2 %collective-permute-done.63 = bf16[1024,128]{1,0:T(8,128)(2,1)S(1)} collective-permute-done((bf16[1024,128]{1,0:T(8,128)(2,1)S(1)}, bf16[1024,128]{1,0:T(8,128)(2,1)S(1)}, u32[]{:S(2)}, u32[]{:S(2)}) %collective-permute-start.63) | collective-permute-done | bytes 262176 | tf_op jit(solution)/shard_map/ppermute | solution.py:44
  397.2 11.2 %collective-permute-done.35 = bf16[128,1024]{1,0:T(8,128)(2,1)S(1)} collective-permute-done((bf16[128,1024]{1,0:T(8,128)(2,1)S(1)}, bf16[128,1024]{1,0:T(8,128)(2,1)S(1)}, u32[]{:S(2)}, u32[]{:S(2)}) %collective-permute-start.35) | collective-permute-done | bytes 262176 | tf_op jit(solution)/shard_map/ppermute | solution.py:44
  420.8 8.5 %collective-permute-done.26 = bf16[256,1024]{0,1:T(8,128)(2,1)S(1)} collective-permute-done((bf16[256,1024]{0,1:T(8,128)(2,1)S(1)}, bf16[256,1024]{0,1:T(8,128)(2,1)S(1)}, u32[]{:S(2)}, u32[]{:S(2)}) %collective-permute-start.26) | collective-permute-done | bytes 524320 | tf_op jit(solution)/shard_map/ppermute | solution.py:44
  451.6 12.3 %collective-permute-done.31 = bf16[1024,128]{1,0:T(8,128)(2,1)S(1)} collective-permute-done((bf16[1024,128]{1,0:T(8,128)(2,1)S(1)}, bf16[1024,128]{1,0:T(8,128)(2,1)S(1)}, u32[]{:S(2)}, u32[]{:S(2)}) %collective-permute-start.31) | collective-permute-done | bytes 262176 | tf_op jit(solution)/shard_map/ppermute | solution.py:44
  478.2 9.7 %fusion.236 = (f32[256]{0:T(256)S(1)}, f32[256]{0:T(256)S(1)}, f32[2048]{0:T(1024)S(1)}, f32[2048]{0:T(1024)S(1)}, f32[2048]{0:T(1024)S(1)}, /*index=5*/f32[2048]{0:T(1024)S(1)}, f32[256,2048]{1,0:T(8,128)S(1)}) fusion(f32[256]{0:T(256)S(1)} %copy-done.62, f32[256]{0:T(256)S(1)} %copy-done.54, bf16[1,256,2048]{2,1,0:T(8,128)(2,1)S(1)} %copy-done.1, ...), kind=kOutput, calls=%fused_computation.457 | convolution fusion | flops 3229081088 | bytes 19451904 | tf_op jit(solution)/shard_map/rc,dc->rd/dot_general | solution.py:300
  498.3 59.7 %psum.28 = f32[4,2048]{1,0:T(4,128)S(1)} all-reduce(f32[4,2048]{1,0:T(4,128)S(1)} %pad_maximum_fusion.68), channel_id=1, replica_groups=mesh['dp'=4,'ctx'=4,'tensor'=2] {'dp','ctx','tensor'}, use_global_device_ids=true, to_apply=%region_12.13 | all-reduce | flops 8192 | bytes 65536 | tf_op jit(solution)/shard_map/psum | solution.py:320
  568.9 61.6 %all-reduce = (f32[3072]{0:T(1024)}, f32[2048]{0:T(1024)S(1)}, f32[4096]{0:T(1024)}) all-reduce(f32[3072]{0:T(1024)S(1)} %reduce_sum.167, f32[2048]{0:T(1024)S(1)} %get-tuple-element.40, f32[4096]{0:T(1024)S(1)} %pad_maximum_fusion.69), channel_id=1, replica_groups=mesh['dp'=4,'ctx'=4,'tensor'=2] {'dp','ctx'}, use_global_device_ids=true, to_apply=%region_14.15 | all-reduce | flops 9216 | bytes 73728 | tf_op jit(solution)/shard_map/psum | solution.py:321
  648.9 10.6 %collective-permute-done.16 = bf16[256,768]{1,0:T(8,128)(2,1)S(1)} collective-permute-done((bf16[256,768]{1,0:T(8,128)(2,1)S(1)}, bf16[256,768]{1,0:T(8,128)(2,1)S(1)}, u32[]{:S(2)}, u32[]{:S(2)}) %collective-permute-start.16) | collective-permute-done | bytes 393248 | tf_op jit(solution)/shard_map/ppermute | solution.py:44
  673.4 9.9 %collective-permute-done.17 = bf16[128,768]{1,0:T(8,128)(2,1)S(1)} collective-permute-done((bf16[128,768]{1,0:T(8,128)(2,1)S(1)}, bf16[128,768]{1,0:T(8,128)(2,1)S(1)}, u32[]{:S(2)}, u32[]{:S(2)}) %collective-permute-start.17) | collective-permute-done | bytes 196640 | tf_op jit(solution)/shard_map/ppermute | solution.py:44
  (545 shorter events, 314.0 us)
Async XLA Ops:
  11.1 131.1 %collective-permute-start.48 = (bf16[256,1024]{1,0:T(8,128)(2,1)}, bf16[256,1024]{1,0:T(8,128)(2,1)}, u32[]{:S(2)}, u32[]{:S(2)}) collective-permute-start(bf16[256,1024]{1,0:T(8,128)(2,1)} %get-tuple-element.108), channel_id=1, source_target_pairs={{0,4},{2,6},{4,0},{6,2},{1,5},{3,7},{5,1},{7,3},{8,12},{10,14},{12... | collective-permute-start | bytes 1572872 | tf_op jit(solution)/shard_map/ppermute | solution.py:44
  18.7 127.8 %collective-permute-start.52 = (bf16[256,1024]{1,0:T(8,128)(2,1)}, bf16[256,1024]{1,0:T(8,128)(2,1)}, u32[]{:S(2)}, u32[]{:S(2)}) collective-permute-start(bf16[256,1024]{1,0:T(8,128)(2,1)} %get-tuple-element.106), channel_id=1, source_target_pairs={{0,4},{2,6},{4,0},{6,2},{1,5},{3,7},{5,1},{7,3},{8,12},{10,14},{12... | collective-permute-start | bytes 1572872 | tf_op jit(solution)/shard_map/ppermute | solution.py:44
  23.3 125.5 %collective-permute-start.56 = (bf16[256,1024]{1,0:T(8,128)(2,1)}, bf16[256,1024]{1,0:T(8,128)(2,1)}, u32[]{:S(2)}, u32[]{:S(2)}) collective-permute-start(bf16[256,1024]{1,0:T(8,128)(2,1)} %get-tuple-element.110), channel_id=1, source_target_pairs={{0,4},{2,6},{4,0},{6,2},{1,5},{3,7},{5,1},{7,3},{8,12},{10,14},{12... | collective-permute-start | bytes 1572872 | tf_op jit(solution)/shard_map/ppermute | solution.py:44
  30.1 123.0 %collective-permute-start.60 = (bf16[256,1024]{1,0:T(8,128)(2,1)}, bf16[256,1024]{1,0:T(8,128)(2,1)}, u32[]{:S(2)}, u32[]{:S(2)}) collective-permute-start(bf16[256,1024]{1,0:T(8,128)(2,1)} %get-tuple-element.112), channel_id=1, source_target_pairs={{0,4},{2,6},{4,0},{6,2},{1,5},{3,7},{5,1},{7,3},{8,12},{10,14},{12... | collective-permute-start | bytes 1572872 | tf_op jit(solution)/shard_map/ppermute | solution.py:44
  30.7 107.6 %collective-permute-start.8 = (f32[1,2,256]{2,1,0:T(2,128)}, f32[1,2,256]{2,1,0:T(2,128)}, u32[]{:S(2)}, u32[]{:S(2)}) collective-permute-start(f32[1,2,256]{2,1,0:T(2,128)} %maximum_bitcast_fusion.9), channel_id=1, source_target_pairs={{0,4},{2,6},{4,0},{6,2},{1,5},{3,7},{5,1},{7,3},{8,12},{10,14},{12... | collective-permute-start | bytes 6152 | tf_op jit(solution)/shard_map/ppermute | solution.py:44
  156.0 81.7 %collective-permute-start = (bf16[256,2,1024]{0,2,1:T(8,128)(2,1)S(1)}, bf16[256,2,1024]{0,2,1:T(8,128)(2,1)S(1)}, u32[]{:S(2)}, u32[]{:S(2)}) collective-permute-start(bf16[256,2,1024]{0,2,1:T(8,128)(2,1)S(1)} %maximum_bitcast_fusion.1), channel_id=1, source_target_pairs={{0,4},{2,6},{4,0},{6,2},{1,5},{3,7},{5,1},{7,3},{8,12},{10,14},{12... | collective-permute-start | bytes 3145736 | tf_op jit(solution)/shard_map/ppermute | solution.py:44
  178.5 55.8 %collective-permute-start.44 = (bf16[256,1024]{1,0:T(8,128)(2,1)S(1)}, bf16[256,1024]{1,0:T(8,128)(2,1)S(1)}, u32[]{:S(2)}, u32[]{:S(2)}) collective-permute-start(bf16[256,1024]{1,0:T(8,128)(2,1)S(1)} %get-tuple-element.115), channel_id=1, source_target_pairs={{0,4},{2,6},{4,0},{6,2},{1,5},{3,7},{5,1},{7,3},{8,12},{10,14},{12... | collective-permute-start | bytes 1572872 | tf_op jit(solution)/shard_map/ppermute | solution.py:44
  189.7 51.6 %collective-permute-start.49 = (bf16[512,1024]{1,0:T(8,128)(2,1)}, bf16[512,1024]{1,0:T(8,128)(2,1)}, u32[]{:S(2)}, u32[]{:S(2)}) collective-permute-start(bf16[512,1024]{1,0:T(8,128)(2,1)} %pad_maximum_fusion.26), channel_id=1, source_target_pairs={{0,2},{2,0},{4,6},{6,4},{1,3},{3,1},{5,7},{7,5},{8,10},{10,8},{12,... | collective-permute-start | bytes 3145736 | tf_op jit(solution)/shard_map/ppermute | solution.py:44
  249.4 159.1 %collective-permute-start.1 = (bf16[512,2,1024]{0,2,1:T(8,128)(2,1)S(1)}, bf16[512,2,1024]{0,2,1:T(8,128)(2,1)S(1)}, u32[]{:S(2)}, u32[]{:S(2)}) collective-permute-start(bf16[512,2,1024]{0,2,1:T(8,128)(2,1)S(1)} %copy-done.12), channel_id=1, source_target_pairs={{0,2},{2,0},{4,6},{6,4},{1,3},{3,1},{5,7},{7,5},{8,10},{10,8},{12,... | collective-permute-start | bytes 6291464 | tf_op jit(solution)/shard_map/ppermute | solution.py:44
  278.0 50.6 %collective-permute-start.38 = (bf16[256,1024]{1,0:T(8,128)(2,1)S(1)}, bf16[256,1024]{1,0:T(8,128)(2,1)S(1)}, u32[]{:S(2)}, u32[]{:S(2)}) collective-permute-start(bf16[256,1024]{1,0:T(8,128)(2,1)S(1)} %convolution_convert_fusion.6), channel_id=1, source_target_pairs={{0,8},{8,0},{16,24},{24,16},{1,9},{9,1},{17,25},{25,17},{2,10},{10... | collective-permute-start | bytes 1572872 | tf_op jit(solution)/shard_map/ppermute | solution.py:44
  289.2 56.2 %collective-permute-start.42 = (bf16[256,1024]{1,0:T(8,128)(2,1)S(1)}, bf16[256,1024]{1,0:T(8,128)(2,1)S(1)}, u32[]{:S(2)}, u32[]{:S(2)}) collective-permute-start(bf16[256,1024]{1,0:T(8,128)(2,1)S(1)} %convolution_convert_fusion.5), channel_id=1, source_target_pairs={{0,8},{8,0},{16,24},{24,16},{1,9},{9,1},{17,25},{25,17},{2,10},{10... | collective-permute-start | bytes 1572872 | tf_op jit(solution)/shard_map/ppermute | solution.py:44
  300.5 55.5 %collective-permute-start.46 = (bf16[256,1024]{1,0:T(8,128)(2,1)S(1)}, bf16[256,1024]{1,0:T(8,128)(2,1)S(1)}, u32[]{:S(2)}, u32[]{:S(2)}) collective-permute-start(bf16[256,1024]{1,0:T(8,128)(2,1)S(1)} %convolution_convert_fusion.4), channel_id=1, source_target_pairs={{0,8},{8,0},{16,24},{24,16},{1,9},{9,1},{17,25},{25,17},{2,10},{10... | collective-permute-start | bytes 1572872 | tf_op jit(solution)/shard_map/ppermute | solution.py:44
  311.7 48.8 %collective-permute-start.51 = (bf16[1024,128]{1,0:T(8,128)(2,1)S(1)}, bf16[1024,128]{1,0:T(8,128)(2,1)S(1)}, u32[]{:S(2)}, u32[]{:S(2)}) collective-permute-start(bf16[1024,128]{1,0:T(8,128)(2,1)S(1)} %slice.843), channel_id=1, source_target_pairs={{0,16},{8,24},{16,0},{24,8},{1,17},{9,25},{17,1},{25,9},{2,18},{10... | collective-permute-start | bytes 786440 | tf_op jit(solution)/shard_map/ppermute | solution.py:44
  362.3 56.0 %collective-permute-start.39 = (bf16[128,1024]{1,0:T(8,128)(2,1)}, bf16[128,1024]{1,0:T(8,128)(2,1)}, u32[]{:S(2)}, u32[]{:S(2)}) collective-permute-start(bf16[128,1024]{1,0:T(8,128)(2,1)} %slice.846), channel_id=1, source_target_pairs={{0,16},{8,24},{16,0},{24,8},{1,17},{9,25},{17,1},{25,9},{2,18},{10... | collective-permute-start | bytes 786440 | tf_op jit(solution)/shard_map/ppermute | solution.py:44
  441.1 48.3 %collective-permute-start.2 = (bf16[256,2048]{1,0:T(8,128)(2,1)}, bf16[256,2048]{1,0:T(8,128)(2,1)}, u32[]{:S(2)}, u32[]{:S(2)}) collective-permute-start(bf16[256,2048]{1,0:T(8,128)(2,1)} %fusion.57), channel_id=1, source_target_pairs={{0,1},{1,0},{2,3},{3,2},{4,5},{5,4},{6,7},{7,6},{8,9},{9,8},{10,11... | collective-permute-start | bytes 3145736 | tf_op jit(solution)/shard_map/ppermute | solution.py:44
  489.0 69.0 %collective-permute-start.10 = (bf16[256,768]{0,1:T(8,128)(2,1)}, bf16[256,768]{0,1:T(8,128)(2,1)}, u32[]{:S(2)}, u32[]{:S(2)}) collective-permute-start(bf16[256,768]{0,1:T(8,128)(2,1)} %get-tuple-element.34), channel_id=1, source_target_pairs={{0,4},{2,6},{4,0},{6,2},{1,5},{3,7},{5,1},{7,3},{8,12},{10,14},{12... | collective-permute-start | bytes 1179656 | tf_op jit(solution)/shard_map/ppermute | solution.py:44
  493.1 72.9 %collective-permute-start.5 = (bf16[256,2048]{1,0:T(8,128)(2,1)S(1)}, bf16[256,2048]{1,0:T(8,128)(2,1)}, u32[]{:S(2)}, u32[]{:S(2)}) collective-permute-start(bf16[256,2048]{1,0:T(8,128)(2,1)S(1)} %get-tuple-element.58), channel_id=1, source_target_pairs={{0,1},{1,0},{2,3},{3,2},{4,5},{5,4},{6,7},{7,6},{8,9},{9,8},{10,11... | collective-permute-start | bytes 3145736 | tf_op jit(solution)/shard_map/ppermute | solution.py:44
  494.7 66.1 %collective-permute-start.14 = (bf16[256,768]{0,1:T(8,128)(2,1)}, bf16[256,768]{0,1:T(8,128)(2,1)S(1)}, u32[]{:S(2)}, u32[]{:S(2)}) collective-permute-start(bf16[256,768]{0,1:T(8,128)(2,1)} %get-tuple-element.37), channel_id=1, source_target_pairs={{0,4},{2,6},{4,0},{6,2},{1,5},{3,7},{5,1},{7,3},{8,12},{10,14},{12... | collective-permute-start | bytes 1179656 | tf_op jit(solution)/shard_map/ppermute | solution.py:44
  496.2 67.3 %collective-permute-start.18 = (bf16[256,768]{0,1:T(8,128)(2,1)S(1)}, bf16[256,768]{0,1:T(8,128)(2,1)S(1)}, u32[]{:S(2)}, u32[]{:S(2)}) collective-permute-start(bf16[256,768]{0,1:T(8,128)(2,1)S(1)} %get-tuple-element.36), channel_id=1, source_target_pairs={{0,4},{2,6},{4,0},{6,2},{1,5},{3,7},{5,1},{7,3},{8,12},{10,14},{12... | collective-permute-start | bytes 1179656 | tf_op jit(solution)/shard_map/ppermute | solution.py:44
  496.7 67.8 %collective-permute-start.22 = (bf16[256,768]{0,1:T(8,128)(2,1)S(1)}, bf16[256,768]{0,1:T(8,128)(2,1)S(1)}, u32[]{:S(2)}, u32[]{:S(2)}) collective-permute-start(bf16[256,768]{0,1:T(8,128)(2,1)S(1)} %get-tuple-element.35), channel_id=1, source_target_pairs={{0,4},{2,6},{4,0},{6,2},{1,5},{3,7},{5,1},{7,3},{8,12},{10,14},{12... | collective-permute-start | bytes 1179656 | tf_op jit(solution)/shard_map/ppermute | solution.py:44
  560.1 70.4 %collective-permute-start.11 = (bf16[512,768]{0,1:T(8,128)(2,1)}, bf16[512,768]{0,1:T(8,128)(2,1)}, u32[]{:S(2)}, u32[]{:S(2)}) collective-permute-start(bf16[512,768]{0,1:T(8,128)(2,1)} %pad_maximum_fusion.48), channel_id=1, source_target_pairs={{0,2},{2,0},{4,6},{6,4},{1,3},{3,1},{5,7},{7,5},{8,10},{10,8},{12,... | collective-permute-start | bytes 2359304 | tf_op jit(solution)/shard_map/ppermute | solution.py:44
  562.9 69.7 %collective-permute-start.15 = (bf16[512,768]{0,1:T(8,128)(2,1)}, bf16[512,768]{0,1:T(8,128)(2,1)}, u32[]{:S(2)}, u32[]{:S(2)}) collective-permute-start(bf16[512,768]{0,1:T(8,128)(2,1)} %pad_maximum_fusion.49), channel_id=1, source_target_pairs={{0,2},{2,0},{4,6},{6,4},{1,3},{3,1},{5,7},{7,5},{8,10},{10,8},{12,... | collective-permute-start | bytes 2359304 | tf_op jit(solution)/shard_map/ppermute | solution.py:44
  564.5 72.1 %collective-permute-start.19 = (bf16[512,768]{0,1:T(8,128)(2,1)}, bf16[512,768]{0,1:T(8,128)(2,1)}, u32[]{:S(2)}, u32[]{:S(2)}) collective-permute-start(bf16[512,768]{0,1:T(8,128)(2,1)} %pad_maximum_fusion.50), channel_id=1, source_target_pairs={{0,2},{2,0},{4,6},{6,4},{1,3},{3,1},{5,7},{7,5},{8,10},{10,8},{12,... | collective-permute-start | bytes 2359304 | tf_op jit(solution)/shard_map/ppermute | solution.py:44
  565.5 73.0 %collective-permute-start.23 = (bf16[512,768]{0,1:T(8,128)(2,1)}, bf16[512,768]{0,1:T(8,128)(2,1)}, u32[]{:S(2)}, u32[]{:S(2)}) collective-permute-start(bf16[512,768]{0,1:T(8,128)(2,1)} %pad_maximum_fusion.51), channel_id=1, source_target_pairs={{0,2},{2,0},{4,6},{6,4},{1,3},{3,1},{5,7},{7,5},{8,10},{10,8},{12,... | collective-permute-start | bytes 2359304 | tf_op jit(solution)/shard_map/ppermute | solution.py:44
  (154 other events, 2057.0 us)

commit v2 on v1

--- a/solution.py
+++ b/solution.py
@@ -1,12 +1,16 @@
+import functools
 import math
 
 import jax
 import jax.numpy as jnp
 from jax import lax
+from jax.experimental import pallas as pl
+from jax.experimental.pallas import tpu as pltpu
 from jax.sharding import PartitionSpec as P
 
 HS = 256
 ROT = 64
+LANES = 128
 
 
 NORM_EPS = 1e-05
@@ -87,30 +91,6 @@
         low = part.astype(jnp.bfloat16)
         return low.astype(jnp.float32) + swap(low, "tensor", 1).astype(jnp.float32)
     return lax.psum(part, "tensor")
-
-
-def reduce_line(left, right, spec, dim):
-    size = lax.axis_size("dp")
-    width = left.shape[1] // size
-    arrived = None
-    bits = [1 << level for level in range(size.bit_length() - 1)]
-    count = size
-    total = None
-    for bit in bits:
-        count //= 2
-        if total is None:
-            send = jnp.einsum(
-                spec, left[:, count * width :], right, preferred_element_type=jnp.float32
-            )
-            keep = jnp.einsum(
-                spec, left[:, : count * width], right, preferred_element_type=jnp.float32
-            )
-        else:
-            keep = lax.slice_in_dim(total, 0, count * width, axis=dim)
-            send = lax.slice_in_dim(total, count * width, 2 * count * width, axis=dim)
-        arrived = swap(send.astype(jnp.bfloat16), "dp", bit)
-        total = keep + arrived.astype(jnp.float32)
-    return total
 
 
 def reduce_blocks(total, axis, dim, bits=None):
@@ -131,6 +111,288 @@
     blocks = relative_blocks(relative_blocks(blocks, "dp", 1), "ctx", 2)
     blocks = jnp.stack([blocks[:, entry] for entry in block_order(dp_size)], 2)
     return blocks.reshape(rows.shape[0], ctx_size, dp_size * width)
+
+
+MESH = pl.DeviceIdType.MESH
+
+
+def flip(place, bit):
+    return place + bit - 2 * bit * ((place // bit) % 2)
+
+
+def device_of(axis, bit):
+    return {axis: flip(lax.axis_index(axis), bit)}
+
+
+def send_to(source, target, send_sem, recv_sem, axis, bit):
+    return pltpu.make_async_remote_copy(
+        src_ref=source,
+        dst_ref=target,
+        send_sem=send_sem,
+        recv_sem=recv_sem,
+        device_id=device_of(axis, bit),
+        device_id_type=MESH,
+    )
+
+
+def weight_kernel(
+    plan,
+    left_ref,
+    right_ref,
+    small_ref,
+    out_ref,
+    small_out,
+    rows_all,
+    first_send,
+    first_recv,
+    second_send,
+    second_recv,
+    held,
+    small_held,
+    small_recv,
+    local_sem,
+    out_sem,
+    ctx_send,
+    ctx_recv,
+    dp_send,
+    dp_recv,
+    small_sems,
+):
+    groups, count, span, rows, shared = plan
+    width = held.shape[1] // 2
+    steps = (("ctx", 1), ("ctx", 2), ("dp", 1), ("dp", 2))
+    tensor_bits = [1 << level for level in range(lax.axis_size("tensor").bit_length() - 1)]
+    small_steps = steps + tuple(("tensor", bit) for bit in tensor_bits)
+
+    barrier = pltpu.get_barrier_semaphore()
+    for axis, bit in small_steps:
+        pl.semaphore_signal(barrier, 1, device_id=device_of(axis, bit), device_id_type=MESH)
+    pl.semaphore_wait(barrier, len(small_steps))
+
+    def columns(piece):
+        return pl.ds(pl.multiple_of(piece * span, span), span)
+
+    def own(piece):
+        return pltpu.make_async_copy(
+            right_ref.at[:, columns(piece)], rows_all.at[piece, pl.ds(0, rows)], local_sem.at[piece]
+        )
+
+    def across(piece):
+        return send_to(
+            right_ref.at[:, columns(piece)],
+            rows_all.at[piece, pl.ds(rows, rows)],
+            ctx_send.at[piece, 0],
+            ctx_recv.at[piece, 0],
+            "ctx",
+            2,
+        )
+
+    def beside(piece, part):
+        source = (
+            right_ref.at[:, columns(piece)] if part == 0 else rows_all.at[piece, pl.ds(rows, rows)]
+        )
+        return send_to(
+            source,
+            rows_all.at[piece, pl.ds((2 + part) * rows, rows)],
+            ctx_send.at[piece, 1 + part],
+            ctx_recv.at[piece, 1 + part],
+            "ctx",
+            1,
+        )
+
+    def first(piece):
+        return send_to(
+            first_send.at[piece],
+            first_recv.at[piece],
+            dp_send.at[piece, 0],
+            dp_recv.at[piece, 0],
+            "dp",
+            1,
+        )
+
+    def second(piece):
+        return send_to(
+            second_send.at[piece],
+            second_recv.at[piece],
+            dp_send.at[piece, 1],
+            dp_recv.at[piece, 1],
+            "dp",
+            2,
+        )
+
+    def result(piece):
+        return pltpu.make_async_copy(
+            held.at[piece % 4, pl.ds(0, width)], out_ref.at[:, columns(piece)], out_sem.at[piece]
+        )
+
+    def small(step):
+        axis, bit = small_steps[step]
+        return send_to(
+            small_held.at[step],
+            small_recv.at[step],
+            small_sems.at[0, step],
+            small_sems.at[1, step],
+            axis,
+            bit,
+        )
+
+    def start(piece):
+        across(piece).start()
+        own(piece).start()
+        beside(piece, 0).start()
+
+    small_held[0] = small_ref[...]
+    small(0).start()
+    start(0)
+    start(1)
+
+    def step(now, carry):
+        @pl.when(now + 2 < count)
+        def _():
+            start(now + 2)
+
+        @pl.when(now < count)
+        def _():
+            across(now).wait_recv()
+            beside(now, 1).start()
+
+        for entry in range(len(small_steps)):
+
+            @pl.when(now == entry + 1)
+            def _():
+                small(entry).wait_recv()
+                if small_steps[entry][0] == "tensor":
+                    some = pl.ds(0, shared)
+                    rest = pl.ds(shared, small_ref.shape[0] - shared)
+                    small_held[entry + 1, some] = small_held[entry, some] + small_recv[entry, some]
+                    small_held[entry + 1, rest] = small_held[entry, rest]
+                else:
+                    small_held[entry + 1] = small_held[entry] + small_recv[entry]
+                if entry + 1 < len(small_steps):
+                    small(entry + 1).start()
+
+        multiply = now - 1
+
+        @pl.when((multiply >= 0) & (multiply < count))
+        def _():
+            own(multiply).wait()
+            beside(multiply, 0).wait_recv()
+            beside(multiply, 1).wait_recv()
+
+            @pl.when(multiply >= 4)
+            def _():
+                result(multiply - 4).wait()
+
+            for group, low, high in groups:
+
+                @pl.when((multiply >= low) & (multiply < high))
+                def _():
+                    first_send[multiply] = jnp.dot(
+                        left_ref[group, pl.ds(2 * width, 2 * width)],
+                        rows_all[multiply],
+                        preferred_element_type=jnp.float32,
+                    ).astype(jnp.bfloat16)
+                    first(multiply).start()
+                    held[multiply % 4] = jnp.dot(
+                        left_ref[group, pl.ds(0, 2 * width)],
+                        rows_all[multiply],
+                        preferred_element_type=jnp.float32,
+                    )
+
+        add = now - 2
+
+        @pl.when((add >= 0) & (add < count))
+        def _():
+            first(add).wait_recv()
+            second_send[add] = (
+                held[add % 4, pl.ds(width, width)]
+                + first_recv[add, pl.ds(width, width)].astype(jnp.float32)
+            ).astype(jnp.bfloat16)
+            second(add).start()
+
+        last = now - 3
+
+        @pl.when((last >= 0) & (last < count))
+        def _():
+            second(last).wait_recv()
+            held[last % 4, pl.ds(0, width)] = (
+                held[last % 4, pl.ds(0, width)]
+                + first_recv[last, pl.ds(0, width)].astype(jnp.float32)
+                + second_recv[last].astype(jnp.float32)
+            )
+            result(last).start()
+
+        return carry
+
+    lax.fori_loop(0, max(count + 3, len(small_steps) + 1), step, 0)
+    small_out[...] = small_held[len(small_steps)]
+    for entry in range(len(small_steps)):
+        small(entry).wait_send()
+
+    def finish(piece, carry):
+        across(piece).wait_send()
+        beside(piece, 0).wait_send()
+        beside(piece, 1).wait_send()
+        first(piece).wait_send()
+        second(piece).wait_send()
+
+        @pl.when(piece >= max(count - 4, 0))
+        def _():
+            result(piece).wait()
+
+        return carry
+
+    lax.fori_loop(0, count, finish, 0)
+
+
+def weight_gradients(lefts, rights, small, shared):
+    width = lefts[0].shape[0] // lax.axis_size("dp")
+    span = min(512, math.gcd(*[right.shape[1] for _, right in rights]))
+    groups, at = [], 0
+    for number, right in rights:
+        groups.append((number, at, at + right.shape[1] // span))
+        at += right.shape[1] // span
+    count = at
+    rows = rights[0][1].shape[0]
+    tokens = rows * lax.axis_size("ctx")
+    left = jnp.stack(lefts)
+    right = jnp.concatenate([right for _, right in rights], 1)
+    steps = sum(lax.axis_size(axis).bit_length() - 1 for axis in ("dp", "ctx", "tensor"))
+    low = jnp.bfloat16
+    vmem = pl.BlockSpec(memory_space=pltpu.VMEM)
+    hbm = pl.BlockSpec(memory_space=pl.ANY)
+    dma = pltpu.SemaphoreType.DMA
+    out, small_out = pl.pallas_call(
+        functools.partial(weight_kernel, (groups, count, span, rows, shared)),
+        out_shape=(
+            jax.ShapeDtypeStruct((width, right.shape[1]), jnp.float32),
+            jax.ShapeDtypeStruct(small.shape, jnp.float32),
+        ),
+        in_specs=[vmem, hbm, vmem],
+        out_specs=(hbm, vmem),
+        scratch_shapes=[
+            pltpu.VMEM((count, tokens, span), low),
+            pltpu.VMEM((count, 2 * width, span), low),
+            pltpu.VMEM((count, 2 * width, span), low),
+            pltpu.VMEM((count, width, span), low),
+            pltpu.VMEM((count, width, span), low),
+            pltpu.VMEM((4, 2 * width, span), jnp.float32),
+            pltpu.VMEM((steps + 1, *small.shape), jnp.float32),
+            pltpu.VMEM((steps, *small.shape), jnp.float32),
+            dma((count,)),
+            dma((count,)),
+            dma((count, 3)),
+            dma((count, 3)),
+            dma((count, 2)),
+            dma((count, 2)),
+            dma((2, steps)),
+        ],
+        compiler_params=pltpu.CompilerParams(
+            collective_id=0, has_side_effects=True, vmem_limit_bytes=60 << 20
+        ),
+    )(left, right, small)
+    outs = [out[:, low_at * span : high_at * span] for _, low_at, high_at in groups]
+    return outs, small_out
 
 
 def local(
@@ -191,33 +453,14 @@
         normed_part * own_columns(attn_norm_gain) + own_columns(attn_norm_bias)
     ).astype(low_type)
 
-    hidden_units = up_weight.shape[1]
-    pieces = max(1, hidden_units // 1024)
-    span = hidden_units // pieces
-    down_grads, up_grads, up_bias_parts = [], [], []
-    branch_part, grad_mlp_in = None, None
-    for piece in range(pieces):
-        cols = slice(piece * span, (piece + 1) * span)
-        up_pre = (
-            jnp.dot(mlp_in, up_weight[:, cols], preferred_element_type=jnp.float32) + up_bias[cols]
-        )
-        activated = jax.nn.gelu(up_pre, approximate=False).astype(low_type)
-        activated_all = gather_rows(activated, "ctx")
-        down_grads.append(reduce_line(low_part, activated_all, "rd,rf->fd", 1))
-        grad_act = jnp.einsum(
-            "rd,fd->rf", grad_low, down_weight[cols], preferred_element_type=jnp.float32
-        )
-        gelu_back = jax.vjp(lambda pre_act: jax.nn.gelu(pre_act, approximate=False), up_pre)[1]
-        grad_pre = gelu_back(grad_act)[0].astype(low_type)
-        grad_pre_all = gather_rows(grad_pre, "ctx")
-        up_grads.append(reduce_line(mlp_part, grad_pre_all, "rd,rf->df", 0))
-        up_bias_parts.append(jnp.sum(grad_pre.astype(jnp.float32), 0))
-        more = jnp.dot(activated, down_weight[cols], preferred_element_type=jnp.float32)
-        branch_part = more if branch_part is None else branch_part + more
-        more = jnp.einsum(
-            "rf,df->rd", grad_pre, up_weight[:, cols], preferred_element_type=jnp.float32
-        )
-        grad_mlp_in = more if grad_mlp_in is None else grad_mlp_in + more
+    up_pre = jnp.dot(mlp_in, up_weight, preferred_element_type=jnp.float32) + up_bias
+    activated = jax.nn.gelu(up_pre, approximate=False).astype(low_type)
+    grad_act = jnp.einsum("rd,fd->rf", grad_low, down_weight, preferred_element_type=jnp.float32)
+    gelu_back = jax.vjp(lambda pre_act: jax.nn.gelu(pre_act, approximate=False), up_pre)[1]
+    grad_pre = gelu_back(grad_act)[0].astype(low_type)
+    grad_up_bias = jnp.sum(grad_pre.astype(jnp.float32), 0)
+    branch_part = jnp.dot(activated, down_weight, preferred_element_type=jnp.float32)
+    grad_mlp_in = jnp.einsum("rf,df->rd", grad_pre, up_weight, preferred_element_type=jnp.float32)
 
     qkv_all = jnp.dot(attn_in, qkv_weight, preferred_element_type=jnp.float32) + qkv_bias
     qkv_all = qkv_all.reshape(seq_count, block_len, head_count, 3, HS)
@@ -246,8 +489,6 @@
         "shqk,skhd->sqhd", prob_low, value_whole, preferred_element_type=jnp.float32
     ).astype(low_type)
     attn_out = attn_out.reshape(row_count, head_count * HS)
-    attn_out_all = gather_rows(attn_out, "ctx")
-    grad_dense_weight = reduce_line(low_part, attn_out_all, "rd,rf->fd", 1)
     branch_part = branch_part + jnp.dot(
         attn_out, dense_weight, preferred_element_type=jnp.float32
     )
@@ -292,10 +533,6 @@
         3,
     )
     grad_qkv = grad_qkv.reshape(row_count, head_count * 3 * HS).astype(low_type)
-    qkv_grads = []
-    for head in range(head_count):
-        piece = grad_qkv[:, head * 3 * HS : (head + 1) * 3 * HS]
-        qkv_grads.append(reduce_line(attn_part, gather_rows(piece, "ctx"), "rd,rc->dc", 0))
     grad_qkv_bias = jnp.sum(grad_qkv.astype(jnp.float32), 0)
     grad_attn_in = jnp.einsum("rc,dc->rd", grad_qkv, qkv_weight, preferred_element_type=jnp.float32)
     norm_parts = jnp.stack(
@@ -317,24 +554,37 @@
         .astype(low_type)
         .reshape(seq_count, block_len, model_width)
     )
-    norm_total = lax.psum(norm_parts, ("dp", "ctx", "tensor"))
-    qkv_bias_sum, up_bias_sum, out_bias_sum = lax.psum(
-        (grad_qkv_bias, jnp.concatenate(up_bias_parts), grad_out_bias), ("dp", "ctx")
-    )
+    small = jnp.concatenate(
+        [norm_parts.reshape(-1), grad_out_bias, grad_qkv_bias, grad_up_bias]
+    ).reshape(-1, LANES)
+    shared = norm_parts.size // LANES
+    (down_grad, up_grad, dense_grad, qkv_grad), small = weight_gradients(
+        [low_part.T, mlp_part.T, attn_part.T],
+        [(0, activated), (1, grad_pre), (0, attn_out), (2, grad_qkv)],
+        small,
+        shared,
+    )
+    small = small.reshape(-1)
+    norm_total = small[: norm_parts.size].reshape(norm_parts.shape)
+    cuts = [norm_parts.size, grad_out_bias.size, grad_qkv_bias.size, grad_up_bias.size]
+    cuts = [sum(cuts[: place + 1]) for place in range(4)]
+    out_bias_sum, qkv_bias_sum, up_bias_sum = [
+        small[cuts[place] : cuts[place + 1]] for place in range(3)
+    ]
     return (
         layer_out,
         input_grad,
         norm_total[0],
         norm_total[1],
-        jnp.concatenate(qkv_grads, 1),
+        qkv_grad,
         qkv_bias_sum,
-        grad_dense_weight,
+        dense_grad.T,
         out_bias_sum,
         norm_total[2],
         norm_total[3],
-        jnp.concatenate(up_grads, 1),
+        up_grad,
         up_bias_sum,
-        jnp.concatenate(down_grads, 0),
+        down_grad.T,
         out_bias_sum,
     )
 

time: 702 us -> 505 us (0.72)
  Pallas kernels: 0 us -> 238 us
  waiting for transfers between devices: 248 us -> 27.1 us
  blocking collectives: 121 us -> 0 us
  matrix products: 147 us -> 99.1 us
  starting transfers between devices: 51.7 us -> 11.7 us
  other arithmetic: 74.1 us -> 58.9 us
  local copies, waits for them, and re-layouts: 46.3 us -> 59.8 us
    pallas_call x0 -> x1, Pallas kernels: none -> 238 us  [weight_gradients(): pl.pallas_call(functools.partial(weight_kernel, (groups, count, span, row...]
    ppermute x64 -> x12, waiting for transfers between devices: 248 us -> 27.1 us  [swap(): return lax.ppermute(array, axis, pairs)]
    psum x2 -> x0, blocking collectives: 121 us -> none  [the longest x1 61.6 us: local(): lax.psum((grad_qkv_bias, jnp.concatenate(up_bias_parts), grad_out_bias),...]
    dot_general x42 -> x4, matrix products: 115 us -> 62.2 us  [the longest x1 19.5 us: local(): jnp.einsum('rd,fd->rf', grad_low, down_weight, preferred_element_type=jnp...]
    ppermute x64 -> x12, starting transfers between devices: 51.7 us -> 11.7 us  [swap(): return lax.ppermute(array, axis, pairs)]
    concatenate x16 -> x3, other arithmetic: 24.4 us -> 4.13 us  [gather_rows(): rows = jnp.concatenate([rows, swap(rows, axis, bit)], 0)]
  transfers between devices with their start and end apart: 64 -> 12, of which waited for: 27 -> 3; matrix products, arithmetic and copies ran while one was open for 36% -> 38% of each run, Pallas kernels for 0% -> 0%
where the time goes in v2:
time: 505 us; the launch traced here: 497 us
  Pallas kernels  238 us (47%)
  matrix products  99.1 us (20%)
  local copies, waits for them, and re-layouts  59.8 us (12%)
  other arithmetic  58.9 us (12%)
  waiting for transfers between devices  27.1 us (5%)
  starting transfers between devices  11.7 us (2%)
    pallas_call x1, Pallas kernels, weight_gradients(): pl.pallas_call(functools.partial(weight_kernel, (groups, count, span, row...  238 us
    ppermute x12, waiting for transfers between devices, swap(): return lax.ppermute(array, axis, pairs)  27.1 us
    dot_general x1, matrix products, local(): jnp.einsum('rd,fd->rf', grad_low, down_weight, preferred_element_type=jnp...  19.5 us
    dot_general x1, matrix products, local(): jnp.dot(mlp_in, up_weight, preferred_element_type=jnp.float32) + up_bias  18.1 us
    dot_general x1, matrix products, local(): jnp.einsum('rf,df->rd', grad_pre, up_weight, preferred_element_type=jnp.f...  12.3 us
    dot_general x1, matrix products, local(): jnp.dot(activated, down_weight, preferred_element_type=jnp.float32)  12.3 us
    ppermute x12, starting transfers between devices, swap(): return lax.ppermute(array, axis, pairs)  11.7 us
    unnamed x124, local copies, waits for them, and re-layouts  11.3 us
  transfers between devices with their start and end apart: 12, of which 3 were waited for; matrix products, arithmetic and copies ran while one was open for 38% of the time, Pallas kernels for 0%

profile of v2, /device:TPU:0, one launch (start us, length us, event | category | flops | bytes accessed | tf_op | source)
XLA Modules:
  0.0 496.7 jit_solution(16234359851907574434)
XLA Ops:
  4.4 3.0 collective-permute-start.10
  7.4 2.6 reshape_reshape_reshape.3
  11.8 2.1 fusion.51
  17.0 2.4 copy.131
  26.0 9.8 %convolution_add_fusion.1 = f32[256,3072]{1,0:T(8,128)} fusion(bf16[2048,3072]{1,0:T(8,128)(2,1)} %param.19, f32[3072]{0:T(1024)S(1)} %copy-done.57, bf16[1,256,2048]{2,1,0:T(8,128)(2,1)S(1)} %copy-done.1, f32[2048]{0:T(1024)S(1)} %copy-done.36, f32[2048]{0:T(1024)S(1)} %copy-done.42, f32[256]{0:T(256)S(1)} %add_rsqrt_fusion, ...), kind=kOutput, calls=%fused_computation.32 | convolution fusion | flops 3225157632 | bytes 16807936 | tf_op jit(solution)/shard_map/dot_general | solution.py:465
  35.8 3.8 copy.117
  41.7 2.6 fusion.101
  60.7 4.6 convolution_convert_fusion
  65.4 18.1 %multiply_convert_fusion.1 = (bf16[256,4096]{1,0:T(8,128)(2,1)}, f32[256,4096]{1,0:T(8,128)S(1)}) fusion(f32[4096]{0:T(1024)S(1)} %copy-done.56, bf16[2048,4096]{1,0:T(8,128)(2,1)} %param.25, bf16[1,256,2048]{2,1,0:T(8,128)(2,1)S(1)} %copy-done.1, f32[2048]{0:T(1024)S(1)} %copy-done.38, f32[2048]{0:T(1024)S(1)} %copy-done.40, f32[256]{0:T(256)S(1)} %copy-done.31, ...), kind=kOutput, calls=%fused_computation.18 | convolution fusion | flops 4367319040 | bytes 24152064 | tf_op jit(solution)/shard_map/dot_general | solution.py:456
  83.4 19.5 %convert_reduce_fusion = (f32[4096]{0:T(1024)}, bf16[256,4096]{1,0:T(8,128)(2,1)}) fusion(f32[256,4096]{1,0:T(8,128)S(1)} %get-tuple-element.159, bf16[4096,2048]{1,0:T(8,128)(2,1)} %param.27, bf16[1,256,2048]{2,1,0:T(8,128)(2,1)S(1)} %copy-done.8, f32[256]{0:T(256)S(1)} %copy-done.28), kind=kOutput, calls=%fused_computation.12 | convolution fusion | flops 4374130688 | bytes 24134656 | tf_op jit(solution)/shard_map/rd,fd->rf/dot_general | solution.py:458
  103.0 12.3 %fusion.109 = f32[256,2048]{1,0:T(8,128)} fusion(bf16[256,4096]{1,0:T(8,128)(2,1)} %get-tuple-element.161, bf16[2048,4096]{1,0:T(8,128)(2,1)} %param.25), kind=kOutput, calls=%fused_computation.257 | convolution fusion | flops 4294967296 | bytes 20971520 | tf_op jit(solution)/shard_map/rf,df->rd/dot_general | solution.py:463
  115.3 2.8 pad_maximum_fusion.3
  122.6 12.3 %fusion.108 = f32[256,2048]{1,0:T(8,128)} fusion(bf16[256,4096]{1,0:T(8,128)(2,1)} %get-tuple-element.158, bf16[4096,2048]{1,0:T(8,128)(2,1)} %param.27), kind=kOutput, calls=%fused_computation.256 | convolution fusion | flops 4294967296 | bytes 20971520 | tf_op jit(solution)/shard_map/dot_general | solution.py:462
  134.9 2.3 maximum_bitcast_fusion
  161.2 2.5 fusion.48
  165.8 4.0 fusion.13
  171.3 10.0 %collective-permute-done.4 = bf16[256,2048]{0,1:T(8,128)(2,1)} collective-permute-done((bf16[256,2048]{0,1:T(8,128)(2,1)}, bf16[256,2048]{0,1:T(8,128)(2,1)}, u32[]{:S(2)}, u32[]{:S(2)}) %collective-permute-start.4) | collective-permute-done | bytes 1048608 | tf_op jit(solution)/shard_map/ppermute | solution.py:48
  199.2 10.6 %fusion.99 = (f32[256]{0:T(256)S(1)}, f32[256]{0:T(256)S(1)}, f32[2048]{0:T(1024)S(1)}, f32[2048]{0:T(1024)S(1)}, f32[2048]{0:T(1024)S(1)}, /*index=5*/f32[2048]{0:T(1024)S(1)}, f32[256,2048]{1,0:T(8,128)}) fusion(f32[256]{0:T(256)S(1)} %copy-done.32, f32[256]{0:T(256)S(1)} %copy-done.26, bf16[1,256,2048]{2,1,0:T(8,128)(2,1)S(1)} %copy-done.1, ...), kind=kOutput, calls=%fused_computation.247 | convolution fusion | flops 3229081088 | bytes 19451904 | tf_op jit(solution)/shard_map/rc,dc->rd/dot_general | solution.py:537
  211.7 4.4 fusion.29
  217.8 6.7 %pad_maximum_fusion.right_ref = bf16[256,12288]{1,0:T(8,128)(2,1)} fusion(bf16[256,3072]{1,0:T(8,128)(2,1)S(1)} %copy.144, bf16[256,1024]{1,0:T(8,128)(2,1)S(1)} %copy-done.10, bf16[256,4096]{1,0:T(8,128)(2,1)S(1)} %copy-done.15, bf16[256,4096]{1,0:T(8,128)(2,1)S(1)} %copy-done.14), kind=kLoop, calls=%fused_computation.3 | loop fusion | flops 25165824 | bytes 12582912 | tf_op jit(solution)/shard_map/concatenate | solution.py:359
  224.6 16.2 %collective-permute-done.5 = bf16[256,2048]{1,0:T(8,128)(2,1)S(1)} collective-permute-done((bf16[256,2048]{1,0:T(8,128)(2,1)S(1)}, bf16[256,2048]{1,0:T(8,128)(2,1)S(1)}, u32[]{:S(2)}, u32[]{:S(2)}) %collective-permute-start.5) | collective-permute-done | bytes 1048608 | tf_op jit(solution)/shard_map/ppermute | solution.py:48
  243.1 238.0 %shard_map.266 = (f32[128,12288]{1,0:T(8,128)}, f32[136,128]{1,0:T(8,128)}) custom-call(bf16[3,512,1024]{2,1,0:T(8,128)(2,1)} %pad_maximum_fusion.2.left_ref, bf16[256,12288]{1,0:T(8,128)(2,1)} %pad_maximum_fusion.right_ref, f32[136,128]{1,0:T(8,128)} %maximum_bitcast_fusion.6.small_ref), custom_call_target="tpu_custom_call" | custom-call | tf_op jit(solution)/shard_map/pallas_call | solution.py:365
  486.2 2.7 slice.325
  488.9 4.0 slice_bitcast_fusion
  (258 shorter events, 97.3 us)
Async XLA Ops:
  0.7 11.0 %copy-start.54 = (f32[22]{0:T(128)S(1)}, f32[22]{0:T(128)}, u32[]{:S(2)}) copy-start(f32[22]{0:T(128)} %param.31) | copy-start | bytes 268
  0.7 11.0 %copy-start.52 = (s32[1,256]{1,0:T(1,128)S(1)}, s32[1,256]{1,0:T(1,128)}, u32[]{:S(2)}) copy-start(s32[1,256]{1,0:T(1,128)} %param.30) | copy-start | bytes 3076
  2.2 23.8 %copy-start.24 = (f32[256]{0:T(256)}, f32[256]{0:T(256)S(1)}, u32[]{:S(2)}) copy-start(f32[256]{0:T(256)S(1)} %broadcast_multiply_fusion.2) | copy-start | bytes 3076
  3.9 22.1 %copy-start.30 = (f32[256]{0:T(256)}, f32[256]{0:T(256)S(1)}, u32[]{:S(2)}) copy-start(f32[256]{0:T(256)S(1)} %add_rsqrt_fusion) | copy-start | bytes 3076
  4.4 140.9 %collective-permute-start.10 = (f32[1,2,256]{2,1,0:T(2,128)}, f32[1,2,256]{2,1,0:T(2,128)}, u32[]{:S(2)}, u32[]{:S(2)}) collective-permute-start(f32[1,2,256]{2,1,0:T(2,128)} %maximum_bitcast_fusion.12), channel_id=1, source_target_pairs={{0,4},{2,6},{4,0},{6,2},{1,5},{3,7},{5,1},{7,3},{8,12},{10,14},{12... | collective-permute-start | bytes 6152 | tf_op jit(solution)/shard_map/ppermute | solution.py:48
  21.2 125.0 %collective-permute-start.6 = (bf16[256,2,512]{0,2,1:T(8,128)(2,1)}, bf16[256,2,512]{0,2,1:T(8,128)(2,1)}, u32[]{:S(2)}, u32[]{:S(2)}) collective-permute-start(bf16[256,2,512]{0,2,1:T(8,128)(2,1)} %get-tuple-element.100), channel_id=1, source_target_pairs={{0,4},{2,6},{4,0},{6,2},{1,5},{3,7},{5,1},{7,3},{8,12},{10,14},{12... | collective-permute-start | bytes 1572872 | tf_op jit(solution)/shard_map/ppermute | solution.py:48
  24.0 123.7 %collective-permute-start.8 = (bf16[256,2,512]{0,2,1:T(8,128)(2,1)}, bf16[256,2,512]{0,2,1:T(8,128)(2,1)}, u32[]{:S(2)}, u32[]{:S(2)}) collective-permute-start(bf16[256,2,512]{0,2,1:T(8,128)(2,1)} %get-tuple-element.108), channel_id=1, source_target_pairs={{0,4},{2,6},{4,0},{6,2},{1,5},{3,7},{5,1},{7,3},{8,12},{10,14},{12... | collective-permute-start | bytes 1572872 | tf_op jit(solution)/shard_map/ppermute | solution.py:48
  52.7 62.6 %collective-permute-start = (bf16[256,2,1024]{0,2,1:T(8,128)(2,1)S(1)}, bf16[256,2,1024]{0,2,1:T(8,128)(2,1)}, u32[]{:S(2)}, u32[]{:S(2)}) collective-permute-start(bf16[256,2,1024]{0,2,1:T(8,128)(2,1)S(1)} %maximum_bitcast_fusion.1), channel_id=1, source_target_pairs={{0,4},{2,6},{4,0},{6,2},{1,5},{3,7},{5,1},{7,3},{8,12},{10,14},{12... | collective-permute-start | bytes 3145736 | tf_op jit(solution)/shard_map/ppermute | solution.py:48
  65.3 18.1 %copy-start.8 = (bf16[1,256,2048]{2,1,0:T(8,128)(2,1)S(1)}, bf16[1,256,2048]{2,1,0:T(8,128)(2,1)}, u32[]{:S(2)}) copy-start(bf16[1,256,2048]{2,1,0:T(8,128)(2,1)} %param.29) | copy-start | bytes 3145732
  65.4 18.1 %copy-start.28 = (f32[256]{0:T(256)S(1)}, f32[256]{0:T(256)}, u32[]{:S(2)}) copy-start(f32[256]{0:T(256)} %copy-done.27) | copy-start | bytes 3076
  118.0 16.8 %collective-permute-start.1 = (bf16[512,2,1024]{0,2,1:T(8,128)(2,1)}, bf16[512,2,1024]{0,2,1:T(8,128)(2,1)}, u32[]{:S(2)}, u32[]{:S(2)}) collective-permute-start(bf16[512,2,1024]{0,2,1:T(8,128)(2,1)} %pad_maximum_fusion.3), channel_id=1, source_target_pairs={{0,2},{2,0},{4,6},{6,4},{1,3},{3,1},{5,7},{7,5},{8,10},{10,8},{12,... | collective-permute-start | bytes 6291464 | tf_op jit(solution)/shard_map/ppermute | solution.py:48
  144.6 8.8 %collective-permute-start.3 = (bf16[512,2048]{0,1:T(8,128)(2,1)S(1)}, bf16[512,2048]{0,1:T(8,128)(2,1)S(1)}, u32[]{:S(2)}, u32[]{:S(2)}) collective-permute-start(bf16[512,2048]{0,1:T(8,128)(2,1)S(1)} %fusion.4), channel_id=1, source_target_pairs={{0,2},{2,0},{4,6},{6,4},{1,3},{3,1},{5,7},{7,5},{8,10},{10,8},{12,... | collective-permute-start | bytes 6291464 | tf_op jit(solution)/shard_map/ppermute | solution.py:48
  146.0 3.1 collective-permute-start.11
  147.3 2.5 collective-permute-start.7
  148.8 2.0 collective-permute-start.9
  155.5 25.8 %collective-permute-start.4 = (bf16[256,2048]{0,1:T(8,128)(2,1)}, bf16[256,2048]{0,1:T(8,128)(2,1)}, u32[]{:S(2)}, u32[]{:S(2)}) collective-permute-start(bf16[256,2048]{0,1:T(8,128)(2,1)} %slice.486), channel_id=1, source_target_pairs={{0,4},{2,6},{4,0},{6,2},{1,5},{3,7},{5,1},{7,3},{8,12},{10,14},{12... | collective-permute-start | bytes 3145736 | tf_op jit(solution)/shard_map/ppermute | solution.py:48
  165.8 15.5 %copy-start.3 = (f32[512,2048]{0,1:T(8,128)S(1)}, f32[512,2048]{0,1:T(8,128)}, u32[]{:S(2)}) copy-start(f32[512,2048]{0,1:T(8,128)} %copy-done.2) | copy-start | bytes 12582916
  169.8 41.9 %collective-permute-start.2 = (bf16[256,2048]{1,0:T(8,128)(2,1)}, bf16[256,2048]{1,0:T(8,128)(2,1)}, u32[]{:S(2)}, u32[]{:S(2)}) collective-permute-start(bf16[256,2048]{1,0:T(8,128)(2,1)} %fusion.13), channel_id=1, source_target_pairs={{0,1},{1,0},{2,3},{3,2},{4,5},{5,4},{6,7},{7,6},{8,9},{9,8},{10,11... | collective-permute-start | bytes 3145736 | tf_op jit(solution)/shard_map/ppermute | solution.py:48
  199.2 12.5 %copy-start.34 = (f32[2048]{0:T(1024)S(1)}, f32[2048]{0:T(1024)}, u32[]{:S(2)}) copy-start(f32[2048]{0:T(1024)} %param.28) | copy-start | bytes 24580
  199.2 12.5 %copy-start.35 = (f32[2048]{0:T(1024)S(1)}, f32[2048]{0:T(1024)}, u32[]{:S(2)}) copy-start(f32[2048]{0:T(1024)} %param.22) | copy-start | bytes 24580
  216.1 24.7 %copy-start.9 = (bf16[1,256,2048]{2,1,0:T(8,128)(2,1)S(1)}, bf16[1,256,2048]{2,1,0:T(8,128)(2,1)}, u32[]{:S(2)}) copy-start(bf16[1,256,2048]{2,1,0:T(8,128)(2,1)} %param.29) | copy-start | bytes 3145732
  216.1 24.7 %copy-start.29 = (f32[256]{0:T(256)S(1)}, f32[256]{0:T(256)}, u32[]{:S(2)}) copy-start(f32[256]{0:T(256)} %copy-done.27) | copy-start | bytes 3076
  216.1 24.7 %collective-permute-start.5 = (bf16[256,2048]{1,0:T(8,128)(2,1)S(1)}, bf16[256,2048]{1,0:T(8,128)(2,1)S(1)}, u32[]{:S(2)}, u32[]{:S(2)}) collective-permute-start(bf16[256,2048]{1,0:T(8,128)(2,1)S(1)} %get-tuple-element.113), channel_id=1, source_target_pairs={{0,1},{1,0},{2,3},{3,2},{4,5},{5,4},{6,7},{7,6},{8,9},{9,8},{10,11... | collective-permute-start | bytes 3145736 | tf_op jit(solution)/shard_map/ppermute | solution.py:48
  224.6 17.9 %copy-start.23 = (f32[4096]{0:T(1024)S(1)}, f32[4096]{0:T(1024)}, u32[]{:S(2)}) copy-start(f32[4096]{0:T(1024)} %get-tuple-element.160) | copy-start | bytes 49156
  (46 other events, 186.0 us)

commit v3 on v0

v3 whole, which is shorter than its diff:
```python
import functools
import math
import types

import jax
import jax.numpy as jnp
from jax import lax
from jax.experimental import pallas as pl
from jax.experimental.pallas import tpu as pltpu
from jax.sharding import PartitionSpec as P

HS = 256
ROT = 64
LANES = 128
RING = 8
NORM_EPS = 1e-05
MESH = pl.DeviceIdType.MESH
ORDER = (0, 2, 1, 3)
LOW = jnp.bfloat16
F32 = jnp.float32


def flip(place, bits):
    bit = 1
    while bit <= bits:
        if bits & bit:
            place = place + bit - 2 * bit * ((place // bit) % 2)
        bit *= 2
    return place


def send_to(source, target, send_sem, recv_sem, axis, bits):
    return pltpu.make_async_remote_copy(
        src_ref=source,
        dst_ref=target,
        send_sem=send_sem,
        recv_sem=recv_sem,
        device_id={axis: flip(lax.axis_index(axis), bits)},
        device_id_type=MESH,
    )


def dot(left, right):
    return jnp.dot(left, right, preferred_element_type=F32)


def dot_rows(left, right):
    return lax.dot_general(left, right, (((1,), (1,)), ((), ())), preferred_element_type=F32)


def axis_bits(axis):
    return [1 << level for level in range(lax.axis_size(axis).bit_length() - 1)]


def blocks_of(total, size):
    return pl.ds(pl.multiple_of(total * size, size), size)


def layer_kernel(plan, names, *refs):
    at = types.SimpleNamespace(**dict(zip(names, refs)))
    rows, span, count, width = plan.rows, plan.span, plan.count, plan.width
    pairs, heads, late = plan.pairs, plan.heads, 2 * plan.pairs
    attn_pieces = heads * HS // span
    per_piece = span // HS
    model = at.hidden.shape[1]
    ctx, dp = lax.axis_index("ctx"), lax.axis_index("dp")
    own_rows = pl.ds(0, rows)
    tensor_bits = axis_bits("tensor")
    halving = (("ctx", 1), ("ctx", 2), ("dp", 1), ("dp", 2))
    small_steps = halving + tuple(("tensor", bit) for bit in tensor_bits)
    scale = 1.0 / math.sqrt(HS)

    def up_load(piece):
        return pltpu.make_async_copy(
            at.up_weight.at[:, blocks_of(piece, span)], at.up_held, at.load_sem.at[0]
        )

    def down_load(piece):
        return pltpu.make_async_copy(
            at.down_weight.at[blocks_of(piece, span)], at.down_held, at.load_sem.at[1]
        )

    def qkv_load(head):
        return pltpu.make_async_copy(
            at.qkv_weight.at[:, blocks_of(head, 3 * HS)], at.qkv_held, at.load_sem.at[2]
        )

    def gate_load(head):
        return pltpu.make_async_copy(
            at.dense_weight.at[blocks_of(head, HS)], at.gate_held, at.load_sem.at[3]
        )

    def dense_load(head):
        return pltpu.make_async_copy(
            at.dense_weight.at[blocks_of(head, HS)], at.dense_held, at.load_sem.at[4]
        )

    def part_copy(kind, place, block):
        source = (at.low, at.hidden)[kind]
        target = (at.low_part, at.hidden_part)[kind]
        column = block * 4 + flip(ctx, place)
        return send_to(
            source.at[:, blocks_of(column, width)],
            target.at[pl.ds(ORDER.index(place) * rows, rows), pl.ds(block * width, width)],
            at.part_send.at[kind, place - 1, block],
            at.part_recv.at[kind, place - 1, block],
            "ctx",
            place,
        )

    def stats_copy(place):
        return send_to(
            at.stats.at[own_rows],
            at.stats.at[pl.ds(ORDER.index(place) * rows, rows)],
            at.stats_send.at[place - 1],
            at.stats_recv.at[place - 1],
            "ctx",
            place,
        )

    def across(piece):
        slot = piece % RING
        return send_to(
            at.rows_all.at[slot, own_rows],
            at.rows_all.at[slot, pl.ds(rows, rows)],
            at.ctx_send.at[slot, 0],
            at.ctx_recv.at[slot, 0],
            "ctx",
            2,
        )

    def beside(piece, part):
        slot = piece % RING
        return send_to(
            at.rows_all.at[slot, pl.ds(part * rows, rows)],
            at.rows_all.at[slot, pl.ds((2 + part) * rows, rows)],
            at.ctx_send.at[slot, 1 + part],
            at.ctx_recv.at[slot, 1 + part],
            "ctx",
            1,
        )

    def first(piece):
        return send_to(
            at.first_send.at[piece % 2],
            at.first_recv.at[piece % RING],
            at.dp_send.at[piece % RING, 0],
            at.dp_recv.at[piece % RING, 0],
            "dp",
            1,
        )

    def second(piece):
        return send_to(
            at.second_send.at[piece % 2],
            at.second_recv.at[piece % RING],
            at.dp_send.at[piece % RING, 1],
            at.dp_recv.at[piece % RING, 1],
            "dp",
            2,
        )

    def results(piece):
        slot = piece % 2
        turned, plain = at.turned.at[slot], at.plain.at[slot]
        feed = piece < late
        dense = (piece >= late) & (piece < late + attn_pieces)
        return (
            (feed & (piece % 2 == 0), turned, at.down_out.at[blocks_of(piece // 2, span)]),
            (feed & (piece % 2 == 1), plain, at.up_out.at[:, blocks_of(piece // 2, span)]),
            (dense, turned, at.dense_out.at[blocks_of(piece - late, span)]),
            (
                piece >= late + attn_pieces,
                plain,
                at.qkv_out.at[:, blocks_of(piece - late - attn_pieces, span)],
            ),
        )

    def for_result(piece, act):
        for holds, source, target in results(piece):

            @pl.when(holds)
            def _():
                act(pltpu.make_async_copy(source, target, at.out_sem.at[piece % 2]))

    def kv_across(head):
        return send_to(
            at.kv.at[head, own_rows],
            at.kv.at[head, pl.ds(rows, rows)],
            at.kv_send.at[head, 0],
            at.kv_recv.at[head, 0],
            "ctx",
            2,
        )

    def kv_beside(head, part):
        return send_to(
            at.kv.at[head, pl.ds(part * rows, rows)],
            at.kv.at[head, pl.ds((2 + part) * rows, rows)],
            at.kv_send.at[head, 1 + part],
            at.kv_recv.at[head, 1 + part],
            "ctx",
            1,
        )

    def pair_beside(head):
        return send_to(
            at.pair_send,
            at.pair_recv.at[head],
            at.kv_send.at[head, 3],
            at.kv_recv.at[head, 3],
            "ctx",
            1,
        )

    def pair_across(head):
        return send_to(
            at.pair_send_low.at[head % 2],
            at.pair_recv_low.at[head],
            at.kv_send.at[head, 4],
            at.kv_recv.at[head, 4],
            "ctx",
            2,
        )

    def tensor_copy(which, level):
        return send_to(
            at.sum_send.at[level],
            at.sum_recv.at[which, level],
            at.sum_sems.at[0, which, level],
            at.sum_sems.at[1, which, level],
            "tensor",
            tensor_bits[level],
        )

    def small_copy(entry):
        axis, bit = small_steps[entry]
        return send_to(
            at.small.at[entry],
            at.small_recv.at[entry],
            at.small_sems.at[0, entry],
            at.small_sems.at[1, entry],
            axis,
            bit,
        )

    def vector(number):
        return at.vectors[pl.ds(number, 1)]

    def turn(heads_rows, back):
        start_part = heads_rows[:, :LANES]
        ahead = pltpu.roll(start_part, LANES - ROT // 2, 1) * at.angles[1]
        behind = pltpu.roll(start_part, ROT // 2, 1) * at.angles[2]
        straight = start_part * at.angles[0]
        moved = straight - ahead - behind if back else straight + ahead + behind
        return jnp.concatenate([moved, heads_rows[:, LANES:]], 1)

    def late_block(block):
        piece = attn_pieces + block // per_piece
        return at.late.at[piece, :, blocks_of(block % per_piece, HS)]

    up_load(0).start()
    down_load(0).start()
    qkv_load(0).start()
    gate_load(0).start()
    dense_load(0).start()
    barrier = pltpu.get_barrier_semaphore()
    partners = small_steps + (("ctx", 3),)
    for axis, bits in partners:
        pl.semaphore_signal(
            barrier,
            1,
            device_id={axis: flip(lax.axis_index(axis), bits)},
            device_id_type=MESH,
        )
    pl.semaphore_wait(barrier, len(partners))
    for place in (2, 3, 1):
        for block in range(4):
            part_copy(1, place, block).start()
    at.small[0] = jnp.zeros_like(at.small[0])
    step_rows = 32

    @pl.loop(0, rows // step_rows)
    def _(block):
        some = blocks_of(block, step_rows)
        inputs = at.hidden[some].astype(F32)
        mean = jnp.mean(inputs, -1, keepdims=True)
        centered = inputs - mean
        inv_std = lax.rsqrt(jnp.mean(centered * centered, -1, keepdims=True) + NORM_EPS)
        normed = centered * inv_std
        at.attn_in[some] = (normed * vector(0) + vector(1)).astype(LOW)
        at.mlp_in[some] = (normed * vector(2) + vector(3)).astype(LOW)
        lane = lax.broadcasted_iota(jnp.int32, (step_rows, LANES), 1)
        at.stats[some] = jnp.where(lane < LANES // 2, mean, inv_std)
        grad_out = at.cotangent[some].astype(F32) * at.row_weight[some]
        at.low[some] = grad_out.astype(LOW)
        at.small[0, pl.ds(2, 1), pl.ds(0, model)] += jnp.sum(grad_out, 0, keepdims=True)
        zeros = jnp.zeros((step_rows, model), F32)
        at.branch[some] = zeros
        at.grad_mlp[some] = zeros
        at.grad_attn[some] = zeros

    for place in (2, 3, 1):
        stats_copy(place).start()
        for block in range(4):
            part_copy(0, place, block).start()
    for block in range(4):
        column = blocks_of(block * 4 + ctx, width)
        at.low_part[own_rows, pl.ds(block * width, width)] = at.low[:, column]
        at.hidden_part[own_rows, pl.ds(block * width, width)] = at.hidden[:, column]

    def low_left():
        for place in (1, 2, 3):
            for block in range(4):
                part_copy(0, place, block).wait_recv()
        for entry, bits in enumerate(ORDER):
            block = at.low_part[:, blocks_of(flip(dp, bits), width)]
            at.left[0, pl.ds(entry * width, width)] = block.T

    def hidden_left():
        for place in (1, 2, 3):
            stats_copy(place).wait_recv()
            for block in range(4):
                part_copy(1, place, block).wait_recv()
        for entry, bits in enumerate(ORDER):
            place = flip(dp, bits)
            block = at.hidden_part[:, blocks_of(place, width)].astype(F32)
            normed = (block - at.stats[:, :1]) * at.stats[:, LANES // 2 : LANES // 2 + 1]
            column = blocks_of(place * 4 + ctx, width)
            to = pl.ds(entry * width, width)
            for number in range(2):
                gain = at.vectors[pl.ds(2 - 2 * number, 1), column]
                bias = at.vectors[pl.ds(3 - 2 * number, 1), column]
                at.left[1 + number, to] = (normed * gain + bias).astype(LOW).T

    def start_piece(piece):
        @pl.when(piece >= RING)
        def _():
            pl.semaphore_wait(at.free.at[0], 1)
            pl.semaphore_wait(at.free.at[1], 1)

        @pl.when(piece >= late)
        def _():
            at.rows_all[piece % RING, own_rows] = at.late[piece - late]

        across(piece).start()
        beside(piece, 0).start()

    def feed_forward(pair):
        up_load(pair).wait()
        down_load(pair).wait()
        pre = dot(at.mlp_in[...], at.up_held[...]) + at.up_bias[:, blocks_of(pair, span)]
        cumulative = 0.5 * (1.0 + lax.erf(pre * math.sqrt(0.5)))
        at.rows_all[(2 * pair) % RING, own_rows] = (pre * cumulative).astype(LOW)
        start_piece(2 * pair)
        grad_act = dot_rows(at.low[...], at.down_held[...])
        density = jnp.exp(-0.5 * pre * pre) * (1.0 / math.sqrt(2.0 * math.pi))
        grad_pre = (grad_act * (cumulative + pre * density)).astype(LOW)
        at.rows_all[(2 * pair + 1) % RING, own_rows] = grad_pre
        at.small[0, pl.ds(4, 1), blocks_of(pair, span)] = jnp.sum(
            grad_pre.astype(F32), 0, keepdims=True
        )
        start_piece(2 * pair + 1)
        at.branch[...] += dot(at.rows_all[(2 * pair) % RING, own_rows], at.down_held[...])
        at.grad_mlp[...] += dot_rows(
            at.rows_all[(2 * pair + 1) % RING, own_rows], at.up_held[...]
        )

        @pl.when(pair + 1 < pairs)
        def _():
            up_load(pair + 1).start()
            down_load(pair + 1).start()

    def project(head):
        qkv_load(head).wait()
        out = dot(at.attn_in[...], at.qkv_held[...]) + at.qkv_bias[:, blocks_of(head, 3 * HS)]
        at.kv[head, own_rows, pl.ds(0, HS)] = turn(out[:, HS : 2 * HS], False).astype(LOW)
        at.kv[head, own_rows, pl.ds(HS, HS)] = out[:, 2 * HS :].astype(LOW)
        kv_across(head).start()
        kv_beside(head, 0).start()
        at.query[head] = turn(out[:, :HS], False).astype(LOW)
        gate_load(head).wait()
        at.gate[head] = dot_rows(at.low[...], at.gate_held[...]).astype(LOW)
        qkv_load((head + 1) % heads).start()

        @pl.when(head + 1 < heads)
        def _():
            gate_load(head + 1).start()

    def kv_forward(head):
        kv_across(head).wait_recv()
        kv_beside(head, 1).start()

    def attend(head):
        kv_beside(head, 0).wait_recv()
        kv_beside(head, 1).wait_recv()
        query, gate = at.query[head], at.gate[head]
        keys, values = at.kv[head, :, :HS], at.kv[head, :, HS:]
        shape = (rows, 4 * rows)
        key_place = lax.broadcasted_iota(jnp.int32, shape, 1)
        shift = jnp.full(shape, flip(ctx, ORDER[3]) * rows - 3 * rows, jnp.int32)
        for entry in (2, 1, 0):
            here = flip(ctx, ORDER[entry]) * rows - entry * rows
            shift = jnp.where(key_place < (entry + 1) * rows, here, shift)
        query_place = lax.broadcasted_iota(jnp.int32, shape, 0) + ctx * rows
        scores = jnp.where(
            key_place + shift <= query_place, dot_rows(query, keys) * scale, -1e30
        )
        expd = jnp.exp(scores - jnp.max(scores, -1, keepdims=True))
        prob = expd * (1.0 / jnp.sum(expd, -1, keepdims=True))
        prob_low = prob.astype(LOW)
        attended = dot(prob_low, values).astype(LOW)
        at.late[head // per_piece, :, blocks_of(head % per_piece, HS)] = attended
        grad_prob = dot_rows(gate, values)
        delta = jnp.sum(grad_prob * prob, -1, keepdims=True)
        grad_scores = (prob * (grad_prob - delta)).astype(LOW)
        grad_key = dot(grad_scores.T, query) * scale
        grad_value = dot(prob_low.T, gate)
        at.pair_send[:, pl.ds(0, HS)] = grad_key[2 * rows :].astype(LOW)
        at.pair_send[:, pl.ds(HS, HS)] = grad_value[2 * rows :].astype(LOW)
        pair_beside(head).start()
        at.pair[head % 2, :, pl.ds(0, HS)] = grad_key[: 2 * rows]
        at.pair[head % 2, :, pl.ds(HS, HS)] = grad_value[: 2 * rows]
        late_block(3 * head)[...] = turn(dot(grad_scores, keys) * scale, True).astype(LOW)
        dense_load(head).wait()
        at.branch[...] += dot(attended, at.dense_held[...])

        @pl.when(head + 1 < heads)
        def _():
            dense_load(head + 1).start()

    def pair_halve(head):
        pair_beside(head).wait()
        at.pair[head % 2] += at.pair_recv[head].astype(F32)
        at.pair_send_low[head % 2] = at.pair[head % 2, pl.ds(rows, rows)].astype(LOW)
        pair_across(head).start()

    def pair_finish(head):
        pair_across(head).wait()
        total = at.pair[head % 2, own_rows] + at.pair_recv_low[head].astype(F32)
        late_block(3 * head + 1)[...] = turn(total[:, :HS], True).astype(LOW)
        late_block(3 * head + 2)[...] = total[:, HS:].astype(LOW)
        for number in range(3):
            at.small[0, pl.ds(3, 1), blocks_of(3 * head + number, HS)] = jnp.sum(
                late_block(3 * head + number)[...].astype(F32), 0, keepdims=True
            )

    def project_back(head):
        qkv_load(head).wait()
        at.grad_attn[...] += (
            dot_rows(late_block(3 * head)[...], at.qkv_held[:, :HS])
            + dot_rows(late_block(3 * head + 1)[...], at.qkv_held[:, HS : 2 * HS])
            + dot_rows(late_block(3 * head + 2)[...], at.qkv_held[:, 2 * HS :])
        )

        @pl.when(head + 1 < heads)
        def _():
            qkv_load(head + 1).start()

    def branch_send():
        at.sum_send[0] = at.branch[...].astype(LOW)
        tensor_copy(0, 0).start()

    def tensor_step(which, level):
        tensor_copy(which, level).wait()
        if level + 1 < len(tensor_bits):
            at.sum_send[level + 1] = (
                at.sum_send[level].astype(F32) + at.sum_recv[which, level].astype(F32)
            ).astype(LOW)
            tensor_copy(which, level + 1).start()
            return

        @pl.loop(0, rows // step_rows)
        def _(block):
            some = blocks_of(block, step_rows)
            total = at.sum_send[level, some].astype(F32) + at.sum_recv[which, level, some].astype(
                F32
            )
            if which == 0:
                total = at.hidden[some].astype(F32) + total + vector(4) + vector(5)
                at.layer_out[some] = total.astype(LOW)
            else:
                grad_out = at.cotangent[some].astype(F32) * at.row_weight[some]
                at.input_grad[some] = (grad_out + total).astype(LOW)

    def norm_back():
        @pl.loop(0, rows // step_rows)
        def _(block):
            some = blocks_of(block, step_rows)
            stats = at.stats[some]
            inv_std = stats[:, LANES // 2 : LANES // 2 + 1]
            normed = (at.hidden[some].astype(F32) - stats[:, :1]) * inv_std
            grad_attn, grad_mlp = at.grad_attn[some], at.grad_mlp[some]
            for row, grad in enumerate((grad_attn, grad_mlp)):
                at.small[0, pl.ds(row, 1), pl.ds(0, model)] += jnp.sum(
                    grad * normed, 0, keepdims=True
                )
                at.small[0, pl.ds(row, 1), pl.ds(model, model)] += jnp.sum(grad, 0, keepdims=True)
            grad = grad_attn * vector(0) + grad_mlp * vector(2)
            part = inv_std * (
                grad
                - jnp.mean(grad, -1, keepdims=True)
                - normed * jnp.mean(grad * normed, -1, keepdims=True)
            )
            at.sum_send[0, some] = part.astype(LOW)

        tensor_copy(1, 0).start()
        small_copy(0).start()

    def small_step(entry):
        small_copy(entry).wait()
        if small_steps[entry][0] == "tensor":
            both, rest = pl.ds(0, 2), pl.ds(2, at.small.shape[1] - 2)
            at.small[entry + 1, both] = at.small[entry, both] + at.small_recv[entry, both]
            at.small[entry + 1, rest] = at.small[entry, rest]
        else:
            at.small[entry + 1] = at.small[entry] + at.small_recv[entry]
        if entry + 1 < len(small_steps):
            small_copy(entry + 1).start()
        else:
            at.small_out[...] = at.small[entry + 1]

    attend_at = 5
    last_attend = attend_at + 2 * (heads - 1)
    last_feed = 2 * (pairs - 1) - 2
    branch_at = max(last_attend, last_feed) + 1
    back_at = last_attend + 5
    assert branch_at + 3 * len(tensor_bits) <= back_at or heads == 1
    back_at = max(back_at, branch_at + 3 * len(tensor_bits) + 1)
    total_steps = max(
        count + 3, back_at + 1 + len(small_steps), back_at + 3 * len(tensor_bits) + 1
    )

    def step(turn_number, carry):
        now = turn_number - 2

        def job(start, stride, times, act):
            index = now - start

            @pl.when((index >= 0) & (index < stride * times) & (index % stride == 0))
            def _():
                act(index // stride)

        @pl.when((now >= 0) & (now < count))
        def _():
            across(now).wait_recv()
            beside(now, 1).start()

        multiply = now - 1

        @pl.when((multiply >= 0) & (multiply < count))
        def _():
            beside(multiply, 0).wait_recv()
            beside(multiply, 1).wait_recv()

            @pl.when(multiply >= RING)
            def _():
                pl.semaphore_wait(at.free.at[2], 1)

            @pl.when(multiply >= 2)
            def _():
                first(multiply - 2).wait_send()

            feed = multiply < late
            group = jnp.where(
                feed, multiply % 2, jnp.where(multiply < late + attn_pieces, 0, 2)
            )
            at.first_send[multiply % 2] = dot(
                at.left[group, pl.ds(2 * width, 2 * width)], at.rows_all[multiply % RING]
            ).astype(LOW)
            first(multiply).start()
            at.held[multiply % 3] = dot(
                at.left[group, pl.ds(0, 2 * width)], at.rows_all[multiply % RING]
            )

        add = now - 2

        @pl.when((add >= 0) & (add < count))
        def _():
            first(add).wait_recv()

            @pl.when(add >= RING)
            def _():
                pl.semaphore_wait(at.free.at[3], 1)

            @pl.when(add >= 2)
            def _():
                second(add - 2).wait_send()

            lower = pl.ds(width, width)
            at.second_send[add % 2] = (
                at.held[add % 3, lower] + at.first_recv[add % RING, lower].astype(F32)
            ).astype(LOW)
            second(add).start()
            across(add).wait_send()
            beside(add, 0).wait_send()
            beside(add, 1).wait_send()

            @pl.when(add < count - RING)
            def _():
                for number, bit in ((0, 2), (1, 1)):
                    pl.semaphore_signal(
                        at.free.at[number],
                        1,
                        device_id={"ctx": flip(ctx, bit)},
                        device_id_type=MESH,
                    )

        last = now - 3

        @pl.when((last >= 0) & (last < count))
        def _():
            second(last).wait_recv()

            @pl.when(last >= 2)
            def _():
                for_result(last - 2, lambda copy: copy.wait())

            upper = pl.ds(0, width)
            total = (
                at.held[last % 3, upper]
                + at.first_recv[last % RING, upper].astype(F32)
                + at.second_recv[last % RING].astype(F32)
            )
            flat = ((last < late) & (last % 2 == 1)) | (last >= late + attn_pieces)

            @pl.when(flat)
            def _():
                at.plain[last % 2] = total

            @pl.when(jnp.logical_not(flat))
            def _():
                at.turned[last % 2] = total.T

            for_result(last, lambda copy: copy.start())

            @pl.when(last < count - RING)
            def _():
                for number, bit in ((2, 1), (3, 2)):
                    pl.semaphore_signal(
                        at.free.at[number],
                        1,
                        device_id={"dp": flip(dp, bit)},
                        device_id_type=MESH,
                    )

        job(0, 1, 1, lambda _: low_left())
        job(1, 1, 1, lambda _: hidden_left())
        job(-2, 2, pairs, feed_forward)
        job(-1, 2, heads, project)
        job(1, 2, heads, kv_forward)
        job(attend_at + 3, 2, heads, pair_finish)
        job(attend_at + 1, 2, heads, pair_halve)
        job(attend_at, 2, heads, attend)
        job(attend_at + 4, 2, heads, project_back)
        job(branch_at, 1, 1, lambda _: branch_send())
        for level in range(len(tensor_bits)):
            job(branch_at + 3 * (level + 1), 1, 1, lambda _: tensor_step(0, level))
        job(back_at, 1, 1, lambda _: norm_back())
        for level in range(len(tensor_bits)):
            job(back_at + 3 * (level + 1), 1, 1, lambda _: tensor_step(1, level))
        for entry in range(len(small_steps)):
            job(back_at + 1 + entry, 1, 1, lambda _: small_step(entry))

        @pl.when((now + 2 >= late) & (now + 2 < count))
        def _():
            start_piece(now + 2)

        return carry

    lax.fori_loop(0, total_steps + 2, step, 0)

    for place in (1, 2, 3):
        stats_copy(place).wait_send()
        for kind in range(2):
            for block in range(4):
                part_copy(kind, place, block).wait_send()

    @pl.loop(0, heads)
    def _(head):
        kv_across(head).wait_send()
        kv_beside(head, 0).wait_send()
        kv_beside(head, 1).wait_send()

    @pl.loop(count - 2, count)
    def _(piece):
        first(piece).wait_send()
        second(piece).wait_send()
        for_result(piece, lambda copy: copy.wait())


def local(
    hidden_in,
    attn_norm_gain,
    attn_norm_bias,
    qkv_weight,
    qkv_bias,
    dense_weight,
    dense_bias,
    mlp_norm_gain,
    mlp_norm_bias,
    up_weight,
    up_bias,
    down_weight,
    down_bias,
    out_cotangent,
    subset_ids,
    subset_weights,
):
    seq_count, rows, model = hidden_in.shape
    heads = qkv_weight.shape[1] // (3 * HS)
    units = up_weight.shape[1]
    width = model // (lax.axis_size("dp") * lax.axis_size("ctx"))
    span = min(512, math.gcd(units, heads * HS, heads * 3 * HS))
    pairs = units // span
    late_count = heads * 4 * HS // span
    plan = types.SimpleNamespace(
        rows=rows, span=span, width=width, pairs=pairs, heads=heads, count=2 * pairs + late_count
    )
    tokens = rows * lax.axis_size("ctx")

    subset_count = subset_weights.shape[0]
    matches = subset_ids[..., None] == jnp.arange(subset_count, dtype=jnp.int32)
    row_weight = jnp.sum(jnp.where(matches, subset_weights, 0.0), -1).reshape(rows, 1)
    positions = lax.axis_index("ctx") * rows + jnp.arange(rows, dtype=jnp.int32)
    half = ROT // 2
    freqs = 10000.0 ** (-(jnp.arange(half, dtype=F32) * 2.0 / ROT))
    table = positions.astype(F32)[:, None] * freqs[None, :]
    cosine, sine = jnp.cos(table), jnp.sin(table)
    none, rest = jnp.zeros_like(sine), jnp.zeros((rows, LANES - ROT), F32)
    angles = jnp.stack(
        [
            jnp.concatenate([cosine, cosine, rest + 1.0], 1),
            jnp.concatenate([-sine, none, rest], 1),
            jnp.concatenate([none, sine, rest], 1),
        ]
    )
    vectors = jnp.stack(
        [attn_norm_gain, attn_norm_bias, mlp_norm_gain, mlp_norm_bias, dense_bias, down_bias]
    )

    bits = lax.axis_size("tensor").bit_length() - 1
    steps = 4 + bits
    small_width = max(2 * model, units, heads * 3 * HS)
    dma = pltpu.SemaphoreType.DMA
    vmem = pl.BlockSpec(memory_space=pltpu.VMEM)
    hbm = pl.BlockSpec(memory_space=pl.ANY)
    inputs = {
        "hidden": (hidden_in.reshape(rows, model), vmem),
        "cotangent": (out_cotangent.reshape(rows, model), vmem),
        "row_weight": (row_weight, vmem),
        "angles": (angles, vmem),
        "vectors": (vectors, vmem),
        "qkv_bias": (qkv_bias[None], vmem),
        "up_bias": (up_bias[None], vmem),
        "qkv_weight": (qkv_weight, hbm),
        "dense_weight": (dense_weight, hbm),
        "up_weight": (up_weight, hbm),
        "down_weight": (down_weight, hbm),
    }
    outputs = {
        "layer_out": ((rows, model), LOW, vmem),
        "input_grad": ((rows, model), LOW, vmem),
        "small_out": ((8, small_width), F32, vmem),
        "down_out": ((units, width), F32, hbm),
        "up_out": ((width, units), F32, hbm),
        "dense_out": ((heads * HS, width), F32, hbm),
        "qkv_out": ((width, heads * 3 * HS), F32, hbm),
    }
    scratch = {
        "rows_all": pltpu.VMEM((RING, tokens, span), LOW),
        "first_send": pltpu.VMEM((2, 2 * width, span), LOW),
        "first_recv": pltpu.VMEM((RING, 2 * width, span), LOW),
        "second_send": pltpu.VMEM((2, width, span), LOW),
        "second_recv": pltpu.VMEM((RING, width, span), LOW),
        "held": pltpu.VMEM((3, 2 * width, span), F32),
        "plain": pltpu.VMEM((2, width, span), F32),
        "turned": pltpu.VMEM((2, span, width), F32),
        "left": pltpu.VMEM((3, 4 * width, tokens), LOW),
        "low_part": pltpu.VMEM((tokens, 4 * width), LOW),
        "hidden_part": pltpu.VMEM((tokens, 4 * width), LOW),
        "stats": pltpu.VMEM((tokens, LANES), F32),
        "attn_in": pltpu.VMEM((rows, model), LOW),
        "mlp_in": pltpu.VMEM((rows, model), LOW),
        "low": pltpu.VMEM((rows, model), LOW),
        "up_held": pltpu.VMEM((model, span), LOW),
        "down_held": pltpu.VMEM((span, model), LOW),
        "qkv_held": pltpu.VMEM((model, 3 * HS), LOW),
        "gate_held": pltpu.VMEM((HS, model), LOW),
        "dense_held": pltpu.VMEM((HS, model), LOW),
        "query": pltpu.VMEM((heads, rows, HS), LOW),
        "gate": pltpu.VMEM((heads, rows, HS), LOW),
        "kv": pltpu.VMEM((heads, tokens, 2 * HS), LOW),
        "pair": pltpu.VMEM((2, 2 * rows, 2 * HS), F32),
        "pair_send": pltpu.VMEM((2 * rows, 2 * HS), LOW),
        "pair_recv": pltpu.VMEM((heads, 2 * rows, 2 * HS), LOW),
        "pair_send_low": pltpu.VMEM((2, rows, 2 * HS), LOW),
        "pair_recv_low": pltpu.VMEM((heads, rows, 2 * HS), LOW),
        "late": pltpu.VMEM((late_count, rows, span), LOW),
        "branch": pltpu.VMEM((rows, model), F32),
        "grad_mlp": pltpu.VMEM((rows, model), F32),
        "grad_attn": pltpu.VMEM((rows, model), F32),
        "sum_send": pltpu.VMEM((bits, rows, model), LOW),
        "sum_recv": pltpu.VMEM((2, bits, rows, model), LOW),
        "small": pltpu.VMEM((steps + 1, 8, small_width), F32),
        "small_recv": pltpu.VMEM((steps, 8, small_width), F32),
        "load_sem": dma((5,)),
        "part_send": dma((2, 3, 4)),
        "part_recv": dma((2, 3, 4)),
        "stats_send": dma((3,)),
        "stats_recv": dma((3,)),
        "ctx_send": dma((RING, 3)),
        "ctx_recv": dma((RING, 3)),
        "dp_send": dma((RING, 2)),
        "dp_recv": dma((RING, 2)),
        "out_sem": dma((2,)),
        "kv_send": dma((heads, 5)),
        "kv_recv": dma((heads, 5)),
        "sum_sems": dma((2, 2, bits)),
        "small_sems": dma((2, steps)),
        "free": pltpu.SemaphoreType.REGULAR((4,)),
    }
    names = [*inputs, *outputs, *scratch]
    results = pl.pallas_call(
        functools.partial(layer_kernel, plan, names),
        out_shape=[jax.ShapeDtypeStruct(shape, kind) for shape, kind, _ in outputs.values()],
        in_specs=[spec for _, spec in inputs.values()],
        out_specs=[spec for _, _, spec in outputs.values()],
        scratch_shapes=list(scratch.values()),
        compiler_params=pltpu.CompilerParams(
            collective_id=0, has_side_effects=True, vmem_limit_bytes=63 << 20
        ),
        name="layer",
    )(*[array for array, _ in inputs.values()])
    layer_out, input_grad, small, down_grad, up_grad, dense_grad, qkv_grad = results
    shape = (seq_count, rows, model)
    out_bias_sum = small[2, :model]
    return (
        layer_out.reshape(shape),
        input_grad.reshape(shape),
        small[0, :model],
        small[0, model : 2 * model],
        qkv_grad,
        small[3, : heads * 3 * HS],
        dense_grad,
        out_bias_sum,
        small[1, :model],
        small[1, model : 2 * model],
        up_grad,
        small[4, :units],
        down_grad,
        out_bias_sum,
    )


def solution(mesh):
    return jax.shard_map(
        local,
        mesh=mesh,
        in_specs=(
            P("dp", "ctx", None),
            P(),
            P(),
            P(None, "tensor"),
            P("tensor"),
            P("tensor", None),
            P(),
            P(),
            P(),
            P(None, "tensor"),
            P("tensor"),
            P("tensor", None),
            P(),
            P("dp", "ctx", None),
            P("dp", "ctx"),
            P(),
        ),
        out_specs=(
            P("dp", "ctx", None),
            P("dp", "ctx", None),
            P(),
            P(),
            P(("dp", "ctx"), "tensor"),
            P("tensor"),
            P("tensor", ("dp", "ctx")),
            P(),
            P(),
            P(),
            P(("dp", "ctx"), "tensor"),
            P("tensor"),
            P("tensor", ("dp", "ctx")),
            P(),
        ),
        check_vma=False,
    )
```

time: 1460 us -> 293 us (0.20)
  waiting for transfers between devices: 1220 us -> 0 us
  Pallas kernels: 0 us -> 271 us
  matrix products: 150 us -> 0 us
  local copies, waits for them, and re-layouts: 40.4 us -> 17.2 us
  other arithmetic: 22.9 us -> 2.3 us
    reduce_scatter x6 -> x0, waiting for transfers between devices: 1040 us -> none  [the longest x1 337 us: local(): lax.psum_scatter(matrices[2], ('dp', 'ctx'), scatter_dimension=0, tiled=T...]
    pallas_call x0 -> x1, Pallas kernels: none -> 271 us  [local(): pl.pallas_call(functools.partial(layer_kernel, plan, names), out_shape=[j...]
    dot_general x18 -> x0, matrix products: 150 us -> none  [the longest x1 20.1 us: local(): jnp.dot(mlp_in, up_weight, preferred_element_type=jnp.float32) + up_bias]
    psum x2 -> x0, waiting for transfers between devices: 136 us -> none  [the longest x1 98.8 us: local(): summed = lax.psum(partial_sum, 'tensor')]
    all_gather x2 -> x0, waiting for transfers between devices: 38.9 us -> none  [the longest x1 19.8 us: local(): lax.all_gather(key_rows.reshape(seq_count, block_len, head_count * HS), '...]
  transfers between devices with their start and end apart: 10 -> 0, of which waited for: 9 -> 0; matrix products, arithmetic and copies ran while one was open for 9% -> 0% of each run, Pallas kernels for 0% -> 0%
where the time goes in v3:
time: 293 us; the launch traced here: 292 us
  Pallas kernels  271 us (92%)
  local copies, waits for them, and re-layouts  17.2 us (6%)
    pallas_call x1, Pallas kernels, local(): pl.pallas_call(functools.partial(layer_kernel, plan, names), out_shape=[j...  271 us
    unnamed x19, local copies, waits for them, and re-layouts  10 us

profile of v3, /device:TPU:0, one launch (start us, length us, event | category | flops | bytes accessed | tf_op | source)
XLA Modules:
  0.0 291.5 jit_solution(6118502112159035288)
XLA Ops:
  0.7 0.1 pad.8.clone
  0.7 0.1 pad.11.clone
  0.8 0.8 fusion.1
  1.6 1.5 stack.43.refs_4_
  3.1 0.8 copy.31.refs_2_
  3.9 0.5 multiply_cosine_fusion
  4.5 0.2 maximum_bitcast_fusion.1
  4.7 0.8 pad_maximum_fusion.refs_3_
  5.4 271.3 %layer.1 = (bf16[256,2048]{1,0:T(8,128)(2,1)}, bf16[256,2048]{1,0:T(8,128)(2,1)}, f32[8,4096]{1,0:T(8,128)}, f32[4096,128]{1,0:T(8,128)}, f32[128,4096]{1,0:T(8,...) custom-call(bf16[256,2048]{1,0:T(8,128)(2,1)} %bitcast.27, bf16[256,2048]{1,0:T(8,128)(2,1)} %bitcast.28, ...), custom_call_target="tpu_custom_call" | custom-call | tf_op jit(solution)/shard_map/layer/pallas_call | solution.py:824
  276.8 0.0 copy-start.3
  276.8 1.6 slice.23
  278.4 1.5 slice.27
  279.9 1.6 fusion.2
  281.5 0.6 copy.39
  282.1 2.4 copy.40
  284.6 1.0 copy.41
  285.5 0.0 copy-done.2
  285.5 1.1 copy.42
  286.7 0.2 copy-done.4
  286.9 0.8 copy.43
  287.7 0.2 copy-done.1
  287.9 1.3 copy.44
  289.2 1.0 copy-done
  290.2 1.3 copy.45
  (12 shorter events, 0.0 us)
Async XLA Ops:
  276.8 7.8 %copy-start.3 = (bf16[256,2048]{1,0:T(8,128)(2,1)S(1)}, bf16[256,2048]{1,0:T(8,128)(2,1)}, u32[]{:S(2)}) copy-start(bf16[256,2048]{1,0:T(8,128)(2,1)} %get-tuple-element.22) | copy-start | bytes 3145732
  281.5 4.0 %copy-start.5 = (f32[1,2048]{1,0:T(1,128)}, f32[1,2048]{1,0:T(1,128)S(1)}, u32[]{:S(2)}) copy-start(f32[1,2048]{1,0:T(1,128)S(1)} %get-tuple-element.32) | copy-start | bytes 24580
  282.1 3.4 %copy-start.2 = (f32[128,3072]{1,0:T(8,128)S(1)}, f32[128,3072]{1,0:T(8,128)}, u32[]{:S(2)}) copy-start(f32[128,3072]{1,0:T(8,128)} %get-tuple-element.85) | copy-start | bytes 4718596
  285.5 1.4 copy-start.4
  285.5 2.3 copy-start.1
  287.9 2.3 copy-start

commit v4 on v3

--- a/solution.py
+++ b/solution.py
@@ -110,8 +110,8 @@
 
     def stats_copy(place):
         return send_to(
-            at.stats.at[own_rows],
-            at.stats.at[pl.ds(ORDER.index(place) * rows, rows)],
+            at.stats_line.at[0],
+            at.stats_line.at[ORDER.index(place)],
             at.stats_send.at[place - 1],
             at.stats_recv.at[place - 1],
             "ctx",
@@ -142,7 +142,7 @@
 
     def first(piece):
         return send_to(
-            at.first_send.at[piece % 2],
+            at.first_send.at[piece % 3],
             at.first_recv.at[piece % RING],
             at.dp_send.at[piece % RING, 0],
             at.dp_recv.at[piece % RING, 0],
@@ -152,7 +152,7 @@
 
     def second(piece):
         return send_to(
-            at.second_send.at[piece % 2],
+            at.second_send.at[piece % 3],
             at.second_recv.at[piece % RING],
             at.dp_send.at[piece % RING, 1],
             at.dp_recv.at[piece % RING, 1],
@@ -160,14 +160,19 @@
             2,
         )
 
+    def is_given(piece):
+        return (piece < 4) | ((piece >= 8) & (piece % 4 < 2))
+
     def results(piece):
         slot = piece % 2
         turned, plain = at.turned.at[slot], at.plain.at[slot]
         feed = piece < late
+        pair = jnp.where(piece < 8, piece % 4, piece // 4 * 2 + piece % 2)
+        gives = is_given(piece)
         dense = (piece >= late) & (piece < late + attn_pieces)
         return (
-            (feed & (piece % 2 == 0), turned, at.down_out.at[blocks_of(piece // 2, span)]),
-            (feed & (piece % 2 == 1), plain, at.up_out.at[:, blocks_of(piece // 2, span)]),
+            (feed & gives, turned, at.down_out.at[blocks_of(pair, span)]),
+            (feed & jnp.logical_not(gives), plain, at.up_out.at[:, blocks_of(pair, span)]),
             (dense, turned, at.dense_out.at[blocks_of(piece - late, span)]),
             (
                 piece >= late + attn_pieces,
@@ -215,7 +220,7 @@
 
     def pair_across(head):
         return send_to(
-            at.pair_send_low.at[head % 2],
+            at.pair_send_low,
             at.pair_recv_low.at[head],
             at.kv_send.at[head, 4],
             at.kv_recv.at[head, 4],
@@ -244,14 +249,11 @@
             bit,
         )
 
-    def vector(number):
-        return at.vectors[pl.ds(number, 1)]
-
     def turn(heads_rows, back):
         start_part = heads_rows[:, :LANES]
-        ahead = pltpu.roll(start_part, LANES - ROT // 2, 1) * at.angles[1]
-        behind = pltpu.roll(start_part, ROT // 2, 1) * at.angles[2]
-        straight = start_part * at.angles[0]
+        ahead = pltpu.roll(start_part, LANES - ROT // 2, 1) * at.sine_ahead[...]
+        behind = pltpu.roll(start_part, ROT // 2, 1) * at.sine_behind[...]
+        straight = start_part * at.cosine[...]
         moved = straight - ahead - behind if back else straight + ahead + behind
         return jnp.concatenate([moved, heads_rows[:, LANES:]], 1)
 
@@ -274,11 +276,25 @@
             device_id_type=MESH,
         )
     pl.semaphore_wait(barrier, len(partners))
+    step_rows = 32
+    at.small[0] = jnp.zeros_like(at.small[0])
+    ids = at.subset_ids[...]
+    weight_line = jnp.zeros(ids.shape, F32)
+    for number in range(at.subset_weights.shape[0]):
+        weight_line = jnp.where(ids == number, at.subset_weights[number], weight_line)
+    at.row_weight[...] = jnp.broadcast_to(weight_line, (LANES, rows)).T
+
+    def grad_of(some):
+        return at.cotangent[some].astype(F32) * at.row_weight[some, pl.ds(0, 1)]
+
+    @pl.loop(0, rows // step_rows)
+    def _(block):
+        some = blocks_of(block, step_rows)
+        at.low[some] = grad_of(some).astype(LOW)
+
     for place in (2, 3, 1):
         for block in range(4):
-            part_copy(1, place, block).start()
-    at.small[0] = jnp.zeros_like(at.small[0])
-    step_rows = 32
+            part_copy(0, place, block).start()
 
     @pl.loop(0, rows // step_rows)
     def _(block):
@@ -288,28 +304,27 @@
         centered = inputs - mean
         inv_std = lax.rsqrt(jnp.mean(centered * centered, -1, keepdims=True) + NORM_EPS)
         normed = centered * inv_std
-        at.attn_in[some] = (normed * vector(0) + vector(1)).astype(LOW)
-        at.mlp_in[some] = (normed * vector(2) + vector(3)).astype(LOW)
+        at.attn_in[some] = (normed * at.attn_gain[...] + at.attn_bias[...]).astype(LOW)
+        at.mlp_in[some] = (normed * at.mlp_gain[...] + at.mlp_bias[...]).astype(LOW)
         lane = lax.broadcasted_iota(jnp.int32, (step_rows, LANES), 1)
         at.stats[some] = jnp.where(lane < LANES // 2, mean, inv_std)
-        grad_out = at.cotangent[some].astype(F32) * at.row_weight[some]
-        at.low[some] = grad_out.astype(LOW)
-        at.small[0, pl.ds(2, 1), pl.ds(0, model)] += jnp.sum(grad_out, 0, keepdims=True)
-        zeros = jnp.zeros((step_rows, model), F32)
-        at.branch[some] = zeros
-        at.grad_mlp[some] = zeros
-        at.grad_attn[some] = zeros
-
-    for place in (2, 3, 1):
-        stats_copy(place).start()
+
+    def send_hidden():
+        line = at.stats[own_rows].T
+        at.stats_line[0, pl.ds(0, 8)] = line[:8]
+        at.stats_line[0, pl.ds(8, 8)] = line[LANES // 2 : LANES // 2 + 8]
+        for place in (2, 3, 1):
+            stats_copy(place).start()
+            for block in range(4):
+                part_copy(1, place, block).start()
         for block in range(4):
-            part_copy(0, place, block).start()
-    for block in range(4):
-        column = blocks_of(block * 4 + ctx, width)
-        at.low_part[own_rows, pl.ds(block * width, width)] = at.low[:, column]
-        at.hidden_part[own_rows, pl.ds(block * width, width)] = at.hidden[:, column]
+            column = blocks_of(block * 4 + ctx, width)
+            at.hidden_part[own_rows, pl.ds(block * width, width)] = at.hidden[:, column]
 
     def low_left():
+        for block in range(4):
+            column = blocks_of(block * 4 + ctx, width)
+            at.low_part[own_rows, pl.ds(block * width, width)] = at.low[:, column]
         for place in (1, 2, 3):
             for block in range(4):
                 part_copy(0, place, block).wait_recv()
@@ -322,16 +337,19 @@
             stats_copy(place).wait_recv()
             for block in range(4):
                 part_copy(1, place, block).wait_recv()
+        for slot in range(1, 4):
+            half = lax.broadcasted_iota(jnp.int32, (LANES, rows), 0) < LANES // 2
+            line = jnp.where(half, at.stats_line[slot, :1], at.stats_line[slot, 8:9])
+            at.stats[pl.ds(slot * rows, rows)] = line.T
         for entry, bits in enumerate(ORDER):
             place = flip(dp, bits)
             block = at.hidden_part[:, blocks_of(place, width)].astype(F32)
             normed = (block - at.stats[:, :1]) * at.stats[:, LANES // 2 : LANES // 2 + 1]
             column = blocks_of(place * 4 + ctx, width)
             to = pl.ds(entry * width, width)
-            for number in range(2):
-                gain = at.vectors[pl.ds(2 - 2 * number, 1), column]
-                bias = at.vectors[pl.ds(3 - 2 * number, 1), column]
-                at.left[1 + number, to] = (normed * gain + bias).astype(LOW).T
+            sides = ((at.mlp_gain, at.mlp_bias), (at.attn_gain, at.attn_bias))
+            for number, (gain, bias) in enumerate(sides):
+                at.left[1 + number, to] = (normed * gain[:, column] + bias[:, column]).astype(LOW).T
 
     def start_piece(piece):
         @pl.when(piece >= RING)
@@ -351,20 +369,28 @@
         down_load(pair).wait()
         pre = dot(at.mlp_in[...], at.up_held[...]) + at.up_bias[:, blocks_of(pair, span)]
         cumulative = 0.5 * (1.0 + lax.erf(pre * math.sqrt(0.5)))
-        at.rows_all[(2 * pair) % RING, own_rows] = (pre * cumulative).astype(LOW)
-        start_piece(2 * pair)
+        feed_piece = jnp.where(pair < 4, pair, pair // 2 * 4 + pair % 2)
+        grad_piece = feed_piece + jnp.where(pair < 4, 4, 2)
+        at.rows_all[feed_piece % RING, own_rows] = (pre * cumulative).astype(LOW)
+        start_piece(feed_piece)
         grad_act = dot_rows(at.low[...], at.down_held[...])
         density = jnp.exp(-0.5 * pre * pre) * (1.0 / math.sqrt(2.0 * math.pi))
         grad_pre = (grad_act * (cumulative + pre * density)).astype(LOW)
-        at.rows_all[(2 * pair + 1) % RING, own_rows] = grad_pre
+        at.rows_all[grad_piece % RING, own_rows] = grad_pre
         at.small[0, pl.ds(4, 1), blocks_of(pair, span)] = jnp.sum(
             grad_pre.astype(F32), 0, keepdims=True
         )
-        start_piece(2 * pair + 1)
-        at.branch[...] += dot(at.rows_all[(2 * pair) % RING, own_rows], at.down_held[...])
-        at.grad_mlp[...] += dot_rows(
-            at.rows_all[(2 * pair + 1) % RING, own_rows], at.up_held[...]
-        )
+        @pl.when(pair == 3)
+        def _():
+            send_hidden()
+
+        @pl.when(pair == 0)
+        def _():
+            for held in (at.branch, at.grad_mlp, at.grad_attn):
+                held[...] = jnp.zeros_like(held)
+
+        at.branch[...] += dot(at.rows_all[feed_piece % RING, own_rows], at.down_held[...])
+        at.grad_mlp[...] += dot_rows(at.rows_all[grad_piece % RING, own_rows], at.up_held[...])
 
         @pl.when(pair + 1 < pairs)
         def _():
@@ -376,7 +402,11 @@
         out = dot(at.attn_in[...], at.qkv_held[...]) + at.qkv_bias[:, blocks_of(head, 3 * HS)]
         at.kv[head, own_rows, pl.ds(0, HS)] = turn(out[:, HS : 2 * HS], False).astype(LOW)
         at.kv[head, own_rows, pl.ds(HS, HS)] = out[:, 2 * HS :].astype(LOW)
-        kv_across(head).start()
+
+        @pl.when(ctx < 2)
+        def _():
+            kv_across(head).start()
+
         kv_beside(head, 0).start()
         at.query[head] = turn(out[:, :HS], False).astype(LOW)
         gate_load(head).wait()
@@ -388,12 +418,23 @@
             gate_load(head + 1).start()
 
     def kv_forward(head):
-        kv_across(head).wait_recv()
-        kv_beside(head, 1).start()
+        @pl.when(ctx >= 2)
+        def _():
+            kv_across(head).wait_recv()
+            kv_beside(head, 1).start()
+
+        @pl.when(ctx < 2)
+        def _():
+            for slot in (1, 3):
+                at.kv[head, pl.ds(slot * rows, rows)] = jnp.zeros((rows, 2 * HS), LOW)
 
     def attend(head):
         kv_beside(head, 0).wait_recv()
-        kv_beside(head, 1).wait_recv()
+
+        @pl.when(ctx >= 2)
+        def _():
+            kv_beside(head, 1).wait_recv()
+
         query, gate = at.query[head], at.gate[head]
         keys, values = at.kv[head, :, :HS], at.kv[head, :, HS:]
         shape = (rows, 4 * rows)
@@ -419,8 +460,8 @@
         at.pair_send[:, pl.ds(0, HS)] = grad_key[2 * rows :].astype(LOW)
         at.pair_send[:, pl.ds(HS, HS)] = grad_value[2 * rows :].astype(LOW)
         pair_beside(head).start()
-        at.pair[head % 2, :, pl.ds(0, HS)] = grad_key[: 2 * rows]
-        at.pair[head % 2, :, pl.ds(HS, HS)] = grad_value[: 2 * rows]
+        at.pair[:, pl.ds(0, HS)] = grad_key[: 2 * rows]
+        at.pair[:, pl.ds(HS, HS)] = grad_value[: 2 * rows]
         late_block(3 * head)[...] = turn(dot(grad_scores, keys) * scale, True).astype(LOW)
         dense_load(head).wait()
         at.branch[...] += dot(attended, at.dense_held[...])
@@ -431,13 +472,28 @@
 
     def pair_halve(head):
         pair_beside(head).wait()
-        at.pair[head % 2] += at.pair_recv[head].astype(F32)
-        at.pair_send_low[head % 2] = at.pair[head % 2, pl.ds(rows, rows)].astype(LOW)
-        pair_across(head).start()
+
+        @pl.when(ctx >= 2)
+        def _():
+            other = pl.ds(rows, rows)
+            at.pair_send_low[...] = (
+                at.pair[other] + at.pair_recv[head, other].astype(F32)
+            ).astype(LOW)
+            pair_across(head).start()
+
+        at.pair_own[...] = at.pair[own_rows] + at.pair_recv[head, own_rows].astype(F32)
 
     def pair_finish(head):
-        pair_across(head).wait()
-        total = at.pair[head % 2, own_rows] + at.pair_recv_low[head].astype(F32)
+        @pl.when(ctx < 2)
+        def _():
+            pair_across(head).wait_recv()
+            at.pair_own[...] += at.pair_recv_low[head].astype(F32)
+
+        @pl.when(ctx >= 2)
+        def _():
+            pair_across(head).wait_send()
+
+        total = at.pair_own[...]
         late_block(3 * head + 1)[...] = turn(total[:, :HS], True).astype(LOW)
         late_block(3 * head + 2)[...] = total[:, HS:].astype(LOW)
         for number in range(3):
@@ -477,11 +533,19 @@
                 F32
             )
             if which == 0:
-                total = at.hidden[some].astype(F32) + total + vector(4) + vector(5)
-                at.layer_out[some] = total.astype(LOW)
+                total = (
+                    at.hidden[some].astype(F32) + total + at.dense_bias[...] + at.down_bias[...]
+                )
+                at.mlp_in[some] = total.astype(LOW)
             else:
-                grad_out = at.cotangent[some].astype(F32) * at.row_weight[some]
-                at.input_grad[some] = (grad_out + total).astype(LOW)
+                at.attn_in[some] = (grad_of(some) + total).astype(LOW)
+
+        row_result(which).start()
+
+    def row_result(which):
+        source = (at.mlp_in, at.attn_in)[which]
+        target = (at.layer_out, at.input_grad)[which]
+        return pltpu.make_async_copy(source, target, at.row_sem.at[which])
 
     def norm_back():
         @pl.loop(0, rows // step_rows)
@@ -491,12 +555,13 @@
             inv_std = stats[:, LANES // 2 : LANES // 2 + 1]
             normed = (at.hidden[some].astype(F32) - stats[:, :1]) * inv_std
             grad_attn, grad_mlp = at.grad_attn[some], at.grad_mlp[some]
+            at.small[0, pl.ds(2, 1), pl.ds(0, model)] += jnp.sum(grad_of(some), 0, keepdims=True)
             for row, grad in enumerate((grad_attn, grad_mlp)):
                 at.small[0, pl.ds(row, 1), pl.ds(0, model)] += jnp.sum(
                     grad * normed, 0, keepdims=True
                 )
                 at.small[0, pl.ds(row, 1), pl.ds(model, model)] += jnp.sum(grad, 0, keepdims=True)
-            grad = grad_attn * vector(0) + grad_mlp * vector(2)
+            grad = grad_attn * at.attn_gain[...] + grad_mlp * at.mlp_gain[...]
             part = inv_std * (
                 grad
                 - jnp.mean(grad, -1, keepdims=True)
@@ -520,15 +585,30 @@
         else:
             at.small_out[...] = at.small[entry + 1]
 
-    attend_at = 5
-    last_attend = attend_at + 2 * (heads - 1)
-    last_feed = 2 * (pairs - 1) - 2
-    branch_at = max(last_attend, last_feed) + 1
-    back_at = last_attend + 5
-    assert branch_at + 3 * len(tensor_bits) <= back_at or heads == 1
-    back_at = max(back_at, branch_at + 3 * len(tensor_bits) + 1)
+    lead, grad_lead = 3, 4
+    assert pairs % 2 == 0 and pairs >= 4
+
+    def places(*lags):
+        return [
+            [2 + 2 * head + sum(lags[:stage]) for stage in range(5)] for head in range(heads)
+        ]
+
+    def in_time(jobs):
+        for piece in range(attn_pieces):
+            if jobs[(piece + 1) * per_piece - 1][2] > late + piece - lead:
+                return False
+        for block in range(3 * heads):
+            if jobs[block // 3][4] > late + attn_pieces + block // per_piece - lead:
+                return False
+        return True
+
+    jobs = next(pace for pace in (places(4, 2, 2, 2), places(1, 1, 1, 1)) if in_time(pace))
+    project_at, forward_at, attend_at, halve_at, finish_at = jobs[0]
+    feed_end = max(2 * (pairs - 1) - 5, 1)
+    branch_at = max(attend_at + 2 * (heads - 1), feed_end) + 1
+    back_at = max(finish_at + 2 * (heads - 1) + 2, branch_at + 3 * len(tensor_bits) + 1)
     total_steps = max(
-        count + 3, back_at + 1 + len(small_steps), back_at + 3 * len(tensor_bits) + 1
+        count + 5, back_at + 1 + len(small_steps), back_at + 3 * len(tensor_bits) + 1
     )
 
     def step(turn_number, carry):
@@ -541,11 +621,6 @@
             def _():
                 act(index // stride)
 
-        @pl.when((now >= 0) & (now < count))
-        def _():
-            across(now).wait_recv()
-            beside(now, 1).start()
-
         multiply = now - 1
 
         @pl.when((multiply >= 0) & (multiply < count))
@@ -557,23 +632,25 @@
             def _():
                 pl.semaphore_wait(at.free.at[2], 1)
 
-            @pl.when(multiply >= 2)
+            @pl.when(multiply >= 3)
             def _():
-                first(multiply - 2).wait_send()
+                first(multiply - 3).wait_send()
 
             feed = multiply < late
             group = jnp.where(
-                feed, multiply % 2, jnp.where(multiply < late + attn_pieces, 0, 2)
+                feed,
+                jnp.where(is_given(multiply), 0, 1),
+                jnp.where(multiply < late + attn_pieces, 0, 2),
             )
-            at.first_send[multiply % 2] = dot(
+            at.first_send[multiply % 3] = dot(
                 at.left[group, pl.ds(2 * width, 2 * width)], at.rows_all[multiply % RING]
             ).astype(LOW)
             first(multiply).start()
-            at.held[multiply % 3] = dot(
+            at.held[multiply % 5] = dot(
                 at.left[group, pl.ds(0, 2 * width)], at.rows_all[multiply % RING]
             )
 
-        add = now - 2
+        add = now - 3
 
         @pl.when((add >= 0) & (add < count))
         def _():
@@ -583,30 +660,17 @@
             def _():
                 pl.semaphore_wait(at.free.at[3], 1)
 
-            @pl.when(add >= 2)
+            @pl.when(add >= 3)
             def _():
-                second(add - 2).wait_send()
+                second(add - 3).wait_send()
 
             lower = pl.ds(width, width)
-            at.second_send[add % 2] = (
-                at.held[add % 3, lower] + at.first_recv[add % RING, lower].astype(F32)
+            at.second_send[add % 3] = (
+                at.held[add % 5, lower] + at.first_recv[add % RING, lower].astype(F32)
             ).astype(LOW)
             second(add).start()
-            across(add).wait_send()
-            beside(add, 0).wait_send()
-            beside(add, 1).wait_send()
-
-            @pl.when(add < count - RING)
-            def _():
-                for number, bit in ((0, 2), (1, 1)):
-                    pl.semaphore_signal(
-                        at.free.at[number],
-                        1,
-                        device_id={"ctx": flip(ctx, bit)},
-                        device_id_type=MESH,
-                    )
-
-        last = now - 3
+
+        last = now - 5
 
         @pl.when((last >= 0) & (last < count))
         def _():
@@ -618,11 +682,11 @@
 
             upper = pl.ds(0, width)
             total = (
-                at.held[last % 3, upper]
+                at.held[last % 5, upper]
                 + at.first_recv[last % RING, upper].astype(F32)
                 + at.second_recv[last % RING].astype(F32)
             )
-            flat = ((last < late) & (last % 2 == 1)) | (last >= late + attn_pieces)
+            flat = ((last < late) & jnp.logical_not(is_given(last))) | (last >= late + attn_pieces)
 
             @pl.when(flat)
             def _():
@@ -644,15 +708,53 @@
                         device_id_type=MESH,
                     )
 
-        job(0, 1, 1, lambda _: low_left())
-        job(1, 1, 1, lambda _: hidden_left())
-        job(-2, 2, pairs, feed_forward)
-        job(-1, 2, heads, project)
-        job(1, 2, heads, kv_forward)
-        job(attend_at + 3, 2, heads, pair_finish)
-        job(attend_at + 1, 2, heads, pair_halve)
+        @pl.when((now >= 0) & (now < count))
+        def _():
+            across(now).wait_recv()
+            beside(now, 1).start()
+
+        sent = now - 1
+
+        @pl.when((sent >= 0) & (sent < count))
+        def _():
+            across(sent).wait_send()
+            beside(sent, 0).wait_send()
+            beside(sent, 1).wait_send()
+
+            @pl.when(sent < count - RING)
+            def _():
+                for number, bit in ((0, 2), (1, 1)):
+                    pl.semaphore_signal(
+                        at.free.at[number],
+                        1,
+                        device_id={"ctx": flip(ctx, bit)},
+                        device_id_type=MESH,
+                    )
+
+        job(4, 1, 1, lambda _: hidden_left())
+
+        @pl.when(now == 2)
+        def _():
+            for piece in range(4, 8):
+                start_piece(piece)
+
+        grads = now + grad_lead
+
+        @pl.when((grads >= 8) & (grads < late) & (grads % 4 >= 2))
+        def _():
+            start_piece(grads)
+
+        @pl.when((now < 2) | ((now % 2 == 1) & (now < 2 * pairs - 5)))
+        def _():
+            feed_forward(jnp.where(now < 2, now + 2, (now + 5) // 2))
+
+        job(-1, 1, 1, lambda _: low_left())
+        job(project_at, 2, heads, project)
+        job(forward_at, 2, heads, kv_forward)
+        job(finish_at, 2, heads, pair_finish)
+        job(halve_at, 2, heads, pair_halve)
         job(attend_at, 2, heads, attend)
-        job(attend_at + 4, 2, heads, project_back)
+        job(finish_at + 1, 2, heads, project_back)
         job(branch_at, 1, 1, lambda _: branch_send())
         for level in range(len(tensor_bits)):
             job(branch_at + 3 * (level + 1), 1, 1, lambda _: tensor_step(0, level))
@@ -662,9 +764,9 @@
         for entry in range(len(small_steps)):
             job(back_at + 1 + entry, 1, 1, lambda _: small_step(entry))
 
-        @pl.when((now + 2 >= late) & (now + 2 < count))
-        def _():
-            start_piece(now + 2)
+        @pl.when((now + lead >= late) & (now + lead < count))
+        def _():
+            start_piece(now + lead)
 
         return carry
 
@@ -678,15 +780,59 @@
 
     @pl.loop(0, heads)
     def _(head):
-        kv_across(head).wait_send()
         kv_beside(head, 0).wait_send()
-        kv_beside(head, 1).wait_send()
-
-    @pl.loop(count - 2, count)
+
+        @pl.when(ctx < 2)
+        def _():
+            kv_across(head).wait_send()
+
+        @pl.when(ctx >= 2)
+        def _():
+            kv_beside(head, 1).wait_send()
+
+    @pl.loop(count - 3, count)
     def _(piece):
         first(piece).wait_send()
         second(piece).wait_send()
-        for_result(piece, lambda copy: copy.wait())
+
+        @pl.when(piece >= count - 2)
+        def _():
+            for_result(piece, lambda copy: copy.wait())
+
+    row_result(0).wait()
+    row_result(1).wait()
+
+
+def hand_on(cuts, *refs):
+    whole = 6
+    sources, small = refs[:whole], refs[whole]
+    targets, refs = refs[whole + 1 : 2 * whole + 1], refs[2 * whole + 1 :]
+    pieces, refs = refs[: len(cuts)], refs[len(cuts) :]
+    held, sem = refs[:whole], refs[whole]
+
+    def halves(ref):
+        size = ref.shape[0] // 2
+        return [ref.at[pl.ds(half * size, size)] for half in range(2)]
+
+    copies = []
+    for number in range(whole):
+        parts = zip(halves(sources[number]), halves(held[number]), halves(targets[number]))
+        for half, (source, middle, target) in enumerate(parts):
+            copies.append(
+                (
+                    pltpu.make_async_copy(source, middle, sem.at[0, number, half]),
+                    pltpu.make_async_copy(middle, target, sem.at[1, number, half]),
+                )
+            )
+    for fetch, _ in copies:
+        fetch.start()
+    for piece, (row, low, high) in zip(pieces, cuts):
+        piece[...] = small[row : row + 1, low:high]
+    for fetch, put in copies:
+        fetch.wait()
+        put.start()
+    for _, put in copies:
+        put.wait()
 
 
 def local(
@@ -719,25 +865,15 @@
     )
     tokens = rows * lax.axis_size("ctx")
 
-    subset_count = subset_weights.shape[0]
-    matches = subset_ids[..., None] == jnp.arange(subset_count, dtype=jnp.int32)
-    row_weight = jnp.sum(jnp.where(matches, subset_weights, 0.0), -1).reshape(rows, 1)
+    half = ROT // 2
+    lane = jnp.arange(LANES, dtype=jnp.int32)[None, :]
     positions = lax.axis_index("ctx") * rows + jnp.arange(rows, dtype=jnp.int32)
-    half = ROT // 2
-    freqs = 10000.0 ** (-(jnp.arange(half, dtype=F32) * 2.0 / ROT))
-    table = positions.astype(F32)[:, None] * freqs[None, :]
-    cosine, sine = jnp.cos(table), jnp.sin(table)
-    none, rest = jnp.zeros_like(sine), jnp.zeros((rows, LANES - ROT), F32)
-    angles = jnp.stack(
-        [
-            jnp.concatenate([cosine, cosine, rest + 1.0], 1),
-            jnp.concatenate([-sine, none, rest], 1),
-            jnp.concatenate([none, sine, rest], 1),
-        ]
-    )
-    vectors = jnp.stack(
-        [attn_norm_gain, attn_norm_bias, mlp_norm_gain, mlp_norm_bias, dense_bias, down_bias]
-    )
+    freqs = 10000.0 ** (-((lane % half).astype(F32) * 2.0 / ROT))
+    table = positions.astype(F32)[:, None] * freqs
+    sine = jnp.sin(table)
+    cosine = jnp.where(lane < ROT, jnp.cos(table), 1.0)
+    sine_ahead = jnp.where(lane < half, -sine, 0.0)
+    sine_behind = jnp.where((lane >= half) & (lane < ROT), sine, 0.0)
 
     bits = lax.axis_size("tensor").bit_length() - 1
     steps = 4 + bits
@@ -748,9 +884,17 @@
     inputs = {
         "hidden": (hidden_in.reshape(rows, model), vmem),
         "cotangent": (out_cotangent.reshape(rows, model), vmem),
-        "row_weight": (row_weight, vmem),
-        "angles": (angles, vmem),
-        "vectors": (vectors, vmem),
+        "subset_ids": (subset_ids, vmem),
+        "subset_weights": (subset_weights, pl.BlockSpec(memory_space=pltpu.SMEM)),
+        "cosine": (cosine, vmem),
+        "sine_ahead": (sine_ahead, vmem),
+        "sine_behind": (sine_behind, vmem),
+        "attn_gain": (attn_norm_gain[None], vmem),
+        "attn_bias": (attn_norm_bias[None], vmem),
+        "mlp_gain": (mlp_norm_gain[None], vmem),
+        "mlp_bias": (mlp_norm_bias[None], vmem),
+        "dense_bias": (dense_bias[None], vmem),
+        "down_bias": (down_bias[None], vmem),
         "qkv_bias": (qkv_bias[None], vmem),
         "up_bias": (up_bias[None], vmem),
         "qkv_weight": (qkv_weight, hbm),
@@ -759,8 +903,8 @@
         "down_weight": (down_weight, hbm),
     }
     outputs = {
-        "layer_out": ((rows, model), LOW, vmem),
-        "input_grad": ((rows, model), LOW, vmem),
+        "layer_out": ((rows, model), LOW, hbm),
+        "input_grad": ((rows, model), LOW, hbm),
         "small_out": ((8, small_width), F32, vmem),
         "down_out": ((units, width), F32, hbm),
         "up_out": ((width, units), F32, hbm),
@@ -769,17 +913,19 @@
     }
     scratch = {
         "rows_all": pltpu.VMEM((RING, tokens, span), LOW),
-        "first_send": pltpu.VMEM((2, 2 * width, span), LOW),
+        "first_send": pltpu.VMEM((3, 2 * width, span), LOW),
         "first_recv": pltpu.VMEM((RING, 2 * width, span), LOW),
-        "second_send": pltpu.VMEM((2, width, span), LOW),
+        "second_send": pltpu.VMEM((3, width, span), LOW),
         "second_recv": pltpu.VMEM((RING, width, span), LOW),
-        "held": pltpu.VMEM((3, 2 * width, span), F32),
+        "held": pltpu.VMEM((5, 2 * width, span), F32),
         "plain": pltpu.VMEM((2, width, span), F32),
         "turned": pltpu.VMEM((2, span, width), F32),
         "left": pltpu.VMEM((3, 4 * width, tokens), LOW),
         "low_part": pltpu.VMEM((tokens, 4 * width), LOW),
         "hidden_part": pltpu.VMEM((tokens, 4 * width), LOW),
         "stats": pltpu.VMEM((tokens, LANES), F32),
+        "stats_line": pltpu.VMEM((4, 16, rows), F32),
+        "row_weight": pltpu.VMEM((rows, LANES), F32),
         "attn_in": pltpu.VMEM((rows, model), LOW),
         "mlp_in": pltpu.VMEM((rows, model), LOW),
         "low": pltpu.VMEM((rows, model), LOW),
@@ -791,10 +937,11 @@
         "query": pltpu.VMEM((heads, rows, HS), LOW),
         "gate": pltpu.VMEM((heads, rows, HS), LOW),
         "kv": pltpu.VMEM((heads, tokens, 2 * HS), LOW),
-        "pair": pltpu.VMEM((2, 2 * rows, 2 * HS), F32),
+        "pair": pltpu.VMEM((2 * rows, 2 * HS), F32),
+        "pair_own": pltpu.VMEM((rows, 2 * HS), F32),
         "pair_send": pltpu.VMEM((2 * rows, 2 * HS), LOW),
         "pair_recv": pltpu.VMEM((heads, 2 * rows, 2 * HS), LOW),
-        "pair_send_low": pltpu.VMEM((2, rows, 2 * HS), LOW),
+        "pair_send_low": pltpu.VMEM((rows, 2 * HS), LOW),
         "pair_recv_low": pltpu.VMEM((heads, rows, 2 * HS), LOW),
         "late": pltpu.VMEM((late_count, rows, span), LOW),
         "branch": pltpu.VMEM((rows, model), F32),
@@ -814,6 +961,7 @@
         "dp_send": dma((RING, 2)),
         "dp_recv": dma((RING, 2)),
         "out_sem": dma((2,)),
+        "row_sem": dma((2,)),
         "kv_send": dma((heads, 5)),
         "kv_recv": dma((heads, 5)),
         "sum_sems": dma((2, 2, bits)),
@@ -832,24 +980,49 @@
         ),
         name="layer",
     )(*[array for array, _ in inputs.values()])
+    cuts = [
+        (0, 0, model),
+        (0, model, 2 * model),
+        (1, 0, model),
+        (1, model, 2 * model),
+        (2, 0, model),
+        (2, 0, model),
+        (3, 0, heads * 3 * HS),
+        (4, 0, units),
+    ]
     layer_out, input_grad, small, down_grad, up_grad, dense_grad, qkv_grad = results
+    large = [layer_out, input_grad, down_grad, up_grad, dense_grad, qkv_grad]
+    shapes = [jax.ShapeDtypeStruct(array.shape, array.dtype) for array in large]
+    shapes += [jax.ShapeDtypeStruct((1, high - low), F32) for _, low, high in cuts]
+    done = pl.pallas_call(
+        functools.partial(hand_on, cuts),
+        out_shape=shapes,
+        in_specs=[hbm] * len(large) + [vmem],
+        out_specs=[hbm] * len(large) + [vmem] * len(cuts),
+        scratch_shapes=[pltpu.VMEM(array.shape, array.dtype) for array in large]
+        + [dma((2, len(large), 2))],
+        compiler_params=pltpu.CompilerParams(vmem_limit_bytes=60 << 20),
+        name="hand_on",
+    )(*large, small)
+    layer_out, input_grad, down_grad, up_grad, dense_grad, qkv_grad = done[:6]
+    vectors = [vector.reshape(-1) for vector in done[6:]]
+    attn_gain, attn_bias, mlp_gain, mlp_bias, dense_sum, down_sum, qkv_sum, up_sum = vectors
     shape = (seq_count, rows, model)
-    out_bias_sum = small[2, :model]
     return (
         layer_out.reshape(shape),
         input_grad.reshape(shape),
-        small[0, :model],
-        small[0, model : 2 * model],
+        attn_gain,
+        attn_bias,
         qkv_grad,
-        small[3, : heads * 3 * HS],
+        qkv_sum,
         dense_grad,
-        out_bias_sum,
-        small[1, :model],
-        small[1, model : 2 * model],
+        dense_sum,
+        mlp_gain,
+        mlp_bias,
         up_grad,
-        small[4, :units],
+        up_sum,
         down_grad,
-        out_bias_sum,
+        down_sum,
     )
 
 

time: 293 us -> 264 us (0.901)
  local copies, waits for them, and re-layouts: 17.2 us -> 0 us
  Pallas kernels: 271 us -> 260 us
    pallas_call x1, Pallas kernels: 271 us -> 252 us  [local(): pl.pallas_call(functools.partial(layer_kernel, plan, names), out_shape=[j...]
    unnamed x19 -> x0, local copies, waits for them, and re-layouts: 10 us -> none
    pallas_call x0 -> x1, Pallas kernels: none -> 7.99 us  [local(): pl.pallas_call(functools.partial(hand_on, cuts), out_shape=shapes, in_spe...]
    slice x3 -> x0, local copies, waits for them, and re-layouts: 4.74 us -> none  [the longest x1 1.62 us: local(): small[1, model:2 * model]]
where the time goes in v4:
time: 264 us; the launch traced here: 262 us
  Pallas kernels  260 us (98%)
    pallas_call x1, Pallas kernels, local(): pl.pallas_call(functools.partial(layer_kernel, plan, names), out_shape=[j...  252 us
    pallas_call x1, Pallas kernels, local(): pl.pallas_call(functools.partial(hand_on, cuts), out_shape=shapes, in_spe...  7.99 us

profile of v4, /device:TPU:0, one launch (start us, length us, event | category | flops | bytes accessed | tf_op | source)
XLA Modules:
  0.0 261.9 jit_solution(5575095300633671868)
XLA Ops:
  0.7 1.3 fusion
  2.0 251.9 %layer.1 = (bf16[256,2048]{1,0:T(8,128)(2,1)}, bf16[256,2048]{1,0:T(8,128)(2,1)}, f32[8,4096]{1,0:T(8,128)}, f32[4096,128]{1,0:T(8,128)}, f32[128,4096]{1,0:T(8,...) custom-call(bf16[256,2048]{1,0:T(8,128)(2,1)} %bitcast.20, bf16[256,2048]{1,0:T(8,128)(2,1)} %bitcast.21, ...), custom_call_target="tpu_custom_call" | custom-call | tf_op jit(solution)/shard_map/layer/pallas_call | solution.py:972
  253.9 8.0 %hand_on.1 = (bf16[256,2048]{1,0:T(8,128)(2,1)}, bf16[256,2048]{1,0:T(8,128)(2,1)}, f32[4096,128]{1,0:T(8,128)}, f32[128,4096]{1,0:T(8,128)}, f32[1024,128]{1,0:...) custom-call(bf16[256,2048]{1,0:T(8,128)(2,1)} %get-tuple-element.35., ...), custom_call_target="tpu_custom_call" | custom-call | tf_op jit(solution)/shard_map/hand_on/pallas_call | solution.py:997
  (4 shorter events, 0.0 us)

commit v5 on v4

--- a/solution.py
+++ b/solution.py
@@ -67,12 +67,19 @@
     own_rows = pl.ds(0, rows)
     tensor_bits = axis_bits("tensor")
     halving = (("ctx", 1), ("ctx", 2), ("dp", 1), ("dp", 2))
-    small_steps = halving + tuple(("tensor", bit) for bit in tensor_bits)
+    line_steps = halving[2:] + tuple(("tensor", bit) for bit in tensor_bits)
     scale = 1.0 / math.sqrt(HS)
 
     def up_load(piece):
         return pltpu.make_async_copy(
             at.up_weight.at[:, blocks_of(piece, span)], at.up_held, at.load_sem.at[0]
+        )
+
+    def up_load_aside(piece):
+        return pltpu.make_async_copy(
+            at.up_weight.at[:, blocks_of(piece, span)],
+            at.qkv_held.at[:, pl.ds(0, span)],
+            at.load_sem.at[2],
         )
 
     def down_load(piece):
@@ -238,15 +245,47 @@
             tensor_bits[level],
         )
 
-    def small_copy(entry):
-        axis, bit = small_steps[entry]
-        return send_to(
-            at.small.at[entry],
-            at.small_recv.at[entry],
-            at.small_sems.at[0, entry],
-            at.small_sems.at[1, entry],
+    quarter = at.small.shape[1] // 4
+
+    def small_half(number):
+        return send_to(
+            at.small.at[:, blocks_of(flip(ctx, (1, 3)[number]), quarter)],
+            at.small_recv.at[number],
+            at.small_sems.at[0, number],
+            at.small_sems.at[1, number],
+            "ctx",
+            1,
+        )
+
+    def small_rest():
+        return send_to(
+            at.small_held.at[1],
+            at.small_recv.at[2],
+            at.small_sems.at[0, 2],
+            at.small_sems.at[1, 2],
+            "ctx",
+            2,
+        )
+
+    def line_copy(entry):
+        axis, bit = line_steps[entry]
+        return send_to(
+            at.line.at[entry],
+            at.line_recv.at[entry],
+            at.small_sems.at[0, 3 + entry],
+            at.small_sems.at[1, 3 + entry],
             axis,
             bit,
+        )
+
+    def small_spread(place):
+        return send_to(
+            at.line.at[len(line_steps)],
+            at.small_full.at[:, blocks_of(ctx, quarter)],
+            at.spread_sems.at[0, place - 1],
+            at.spread_sems.at[1, place - 1],
+            "ctx",
+            place,
         )
 
     def turn(heads_rows, back):
@@ -262,12 +301,12 @@
         return at.late.at[piece, :, blocks_of(block % per_piece, HS)]
 
     up_load(0).start()
+    up_load_aside(1).start()
     down_load(0).start()
-    qkv_load(0).start()
     gate_load(0).start()
     dense_load(0).start()
     barrier = pltpu.get_barrier_semaphore()
-    partners = small_steps + (("ctx", 3),)
+    partners = halving[:2] + line_steps + (("ctx", 3),)
     for axis, bits in partners:
         pl.semaphore_signal(
             barrier,
@@ -277,7 +316,7 @@
         )
     pl.semaphore_wait(barrier, len(partners))
     step_rows = 32
-    at.small[0] = jnp.zeros_like(at.small[0])
+    at.small[...] = jnp.zeros_like(at.small)
     ids = at.subset_ids[...]
     weight_line = jnp.zeros(ids.shape, F32)
     for number in range(at.subset_weights.shape[0]):
@@ -364,25 +403,49 @@
         across(piece).start()
         beside(piece, 0).start()
 
+    def pre_act(pair, weights):
+        pre = dot(at.mlp_in[...], weights) + at.up_bias[:, blocks_of(pair, span)]
+        return pre, 0.5 * (1.0 + lax.erf(pre * math.sqrt(0.5)))
+
+    def activate(pair):
+        if pair % 2 == 0:
+            up_load(pair).wait()
+            pre, cumulative = pre_act(pair, at.up_held[...])
+        else:
+            up_load_aside(pair).wait()
+            pre, cumulative = pre_act(pair, at.qkv_held[:, :span])
+        at.rows_all[pair, own_rows] = (pre * cumulative).astype(LOW)
+        start_piece(pair)
+        if pair % 2 == 0:
+            up_load((pair + 2) % 4).start()
+        elif pair == 1:
+            up_load_aside(3).start()
+        else:
+            qkv_load(0).start()
+            send_hidden()
+
     def feed_forward(pair):
         up_load(pair).wait()
         down_load(pair).wait()
-        pre = dot(at.mlp_in[...], at.up_held[...]) + at.up_bias[:, blocks_of(pair, span)]
-        cumulative = 0.5 * (1.0 + lax.erf(pre * math.sqrt(0.5)))
+        pre, cumulative = pre_act(pair, at.up_held[...])
         feed_piece = jnp.where(pair < 4, pair, pair // 2 * 4 + pair % 2)
         grad_piece = feed_piece + jnp.where(pair < 4, 4, 2)
-        at.rows_all[feed_piece % RING, own_rows] = (pre * cumulative).astype(LOW)
-        start_piece(feed_piece)
+
+        @pl.when(pair >= 4)
+        def _():
+            at.rows_all[feed_piece % RING, own_rows] = (pre * cumulative).astype(LOW)
+            start_piece(feed_piece)
+
         grad_act = dot_rows(at.low[...], at.down_held[...])
         density = jnp.exp(-0.5 * pre * pre) * (1.0 / math.sqrt(2.0 * math.pi))
         grad_pre = (grad_act * (cumulative + pre * density)).astype(LOW)
         at.rows_all[grad_piece % RING, own_rows] = grad_pre
-        at.small[0, pl.ds(4, 1), blocks_of(pair, span)] = jnp.sum(
+        at.small[pl.ds(4, 1), blocks_of(pair, span)] = jnp.sum(
             grad_pre.astype(F32), 0, keepdims=True
         )
-        @pl.when(pair == 3)
-        def _():
-            send_hidden()
+        @pl.when(pair < 4)
+        def _():
+            start_piece(grad_piece)
 
         @pl.when(pair == 0)
         def _():
@@ -497,7 +560,7 @@
         late_block(3 * head + 1)[...] = turn(total[:, :HS], True).astype(LOW)
         late_block(3 * head + 2)[...] = total[:, HS:].astype(LOW)
         for number in range(3):
-            at.small[0, pl.ds(3, 1), blocks_of(3 * head + number, HS)] = jnp.sum(
+            at.small[pl.ds(3, 1), blocks_of(3 * head + number, HS)] = jnp.sum(
                 late_block(3 * head + number)[...].astype(F32), 0, keepdims=True
             )
 
@@ -555,12 +618,12 @@
             inv_std = stats[:, LANES // 2 : LANES // 2 + 1]
             normed = (at.hidden[some].astype(F32) - stats[:, :1]) * inv_std
             grad_attn, grad_mlp = at.grad_attn[some], at.grad_mlp[some]
-            at.small[0, pl.ds(2, 1), pl.ds(0, model)] += jnp.sum(grad_of(some), 0, keepdims=True)
+            at.small[pl.ds(2, 1), pl.ds(0, model)] += jnp.sum(grad_of(some), 0, keepdims=True)
             for row, grad in enumerate((grad_attn, grad_mlp)):
-                at.small[0, pl.ds(row, 1), pl.ds(0, model)] += jnp.sum(
+                at.small[pl.ds(row, 1), pl.ds(0, model)] += jnp.sum(
                     grad * normed, 0, keepdims=True
                 )
-                at.small[0, pl.ds(row, 1), pl.ds(model, model)] += jnp.sum(grad, 0, keepdims=True)
+                at.small[pl.ds(row, 1), pl.ds(model, model)] += jnp.sum(grad, 0, keepdims=True)
             grad = grad_attn * at.attn_gain[...] + grad_mlp * at.mlp_gain[...]
             part = inv_std * (
                 grad
@@ -570,27 +633,45 @@
             at.sum_send[0, some] = part.astype(LOW)
 
         tensor_copy(1, 0).start()
-        small_copy(0).start()
+        for number in range(2):
+            small_half(number).start()
 
     def small_step(entry):
-        small_copy(entry).wait()
-        if small_steps[entry][0] == "tensor":
-            both, rest = pl.ds(0, 2), pl.ds(2, at.small.shape[1] - 2)
-            at.small[entry + 1, both] = at.small[entry, both] + at.small_recv[entry, both]
-            at.small[entry + 1, rest] = at.small[entry, rest]
+        if entry == 0:
+            for number in range(2):
+                small_half(number).wait()
+                mine = blocks_of(flip(ctx, 2 * number), quarter)
+                at.small_held[number] = at.small[:, mine] + at.small_recv[number]
+            small_rest().start()
+            return
+        if entry == 1:
+            small_rest().wait()
+            at.line[0] = at.small_held[0] + at.small_recv[2]
         else:
-            at.small[entry + 1] = at.small[entry] + at.small_recv[entry]
-        if entry + 1 < len(small_steps):
-            small_copy(entry + 1).start()
-        else:
-            at.small_out[...] = at.small[entry + 1]
-
-    lead, grad_lead = 3, 4
+            line_copy(entry - 2).wait()
+            added = at.line[entry - 2] + at.line_recv[entry - 2]
+            if line_steps[entry - 2][0] == "tensor":
+                row = lax.broadcasted_iota(jnp.int32, added.shape, 0)
+                added = jnp.where(row < 2, added, at.line[entry - 2])
+            at.line[entry - 1] = added
+        if entry - 1 < len(line_steps):
+            line_copy(entry - 1).start()
+            return
+        for place in (2, 3, 1):
+            small_spread(place).start()
+        at.small_full[:, blocks_of(ctx, quarter)] = at.line[len(line_steps)]
+
+    def small_finish():
+        for place in (1, 2, 3):
+            small_spread(place).wait()
+        at.small_out[...] = at.small_full[...]
+
+    lead, grad_lead = 3, 3
     assert pairs % 2 == 0 and pairs >= 4
 
-    def places(*lags):
+    def places(base, *lags):
         return [
-            [2 + 2 * head + sum(lags[:stage]) for stage in range(5)] for head in range(heads)
+            [base + 2 * head + sum(lags[:stage]) for stage in range(5)] for head in range(heads)
         ]
 
     def in_time(jobs):
@@ -602,13 +683,13 @@
                 return False
         return True
 
-    jobs = next(pace for pace in (places(4, 2, 2, 2), places(1, 1, 1, 1)) if in_time(pace))
+    jobs = next(pace for pace in (places(3, 3, 2, 2, 2), places(2, 1, 1, 1, 1)) if in_time(pace))
     project_at, forward_at, attend_at, halve_at, finish_at = jobs[0]
-    feed_end = max(2 * (pairs - 1) - 5, 1)
+    feed_end = max(2 * (pairs - 1) - 4, 3)
     branch_at = max(attend_at + 2 * (heads - 1), feed_end) + 1
-    back_at = max(finish_at + 2 * (heads - 1) + 2, branch_at + 3 * len(tensor_bits) + 1)
+    back_at = max(finish_at + 2 * (heads - 1) + 2, branch_at + 4 * len(tensor_bits) + 1)
     total_steps = max(
-        count + 5, back_at + 1 + len(small_steps), back_at + 3 * len(tensor_bits) + 1
+        count + 5, back_at + 5 + len(line_steps), back_at + 4 * len(tensor_bits) + 1
     )
 
     def step(turn_number, carry):
@@ -732,11 +813,8 @@
                     )
 
         job(4, 1, 1, lambda _: hidden_left())
-
-        @pl.when(now == 2)
-        def _():
-            for piece in range(4, 8):
-                start_piece(piece)
+        job(-2, 1, 1, lambda _: activate(0))
+        job(-2, 1, 1, lambda _: activate(1))
 
         grads = now + grad_lead
 
@@ -744,11 +822,13 @@
         def _():
             start_piece(grads)
 
-        @pl.when((now < 2) | ((now % 2 == 1) & (now < 2 * pairs - 5)))
-        def _():
-            feed_forward(jnp.where(now < 2, now + 2, (now + 5) // 2))
+        @pl.when(((now >= 0) & (now < 4)) | ((now % 2 == 0) & (now >= 4) & (now < 2 * pairs - 4)))
+        def _():
+            feed_forward(jnp.where(now < 4, now, now // 2 + 2))
 
         job(-1, 1, 1, lambda _: low_left())
+        job(-1, 1, 1, lambda _: activate(2))
+        job(-1, 1, 1, lambda _: activate(3))
         job(project_at, 2, heads, project)
         job(forward_at, 2, heads, kv_forward)
         job(finish_at, 2, heads, pair_finish)
@@ -757,12 +837,13 @@
         job(finish_at + 1, 2, heads, project_back)
         job(branch_at, 1, 1, lambda _: branch_send())
         for level in range(len(tensor_bits)):
-            job(branch_at + 3 * (level + 1), 1, 1, lambda _: tensor_step(0, level))
+            job(branch_at + 4 * (level + 1), 1, 1, lambda _: tensor_step(0, level))
         job(back_at, 1, 1, lambda _: norm_back())
         for level in range(len(tensor_bits)):
-            job(back_at + 3 * (level + 1), 1, 1, lambda _: tensor_step(1, level))
-        for entry in range(len(small_steps)):
+            job(back_at + 4 * (level + 1), 1, 1, lambda _: tensor_step(1, level))
+        for entry in range(len(line_steps) + 2):
             job(back_at + 1 + entry, 1, 1, lambda _: small_step(entry))
+        job(back_at + 3 + len(line_steps), 1, 1, lambda _: small_finish())
 
         @pl.when((now + lead >= late) & (now + lead < count))
         def _():
@@ -876,7 +957,7 @@
     sine_behind = jnp.where((lane >= half) & (lane < ROT), sine, 0.0)
 
     bits = lax.axis_size("tensor").bit_length() - 1
-    steps = 4 + bits
+    steps = 2 + bits
     small_width = max(2 * model, units, heads * 3 * HS)
     dma = pltpu.SemaphoreType.DMA
     vmem = pl.BlockSpec(memory_space=pltpu.VMEM)
@@ -949,8 +1030,12 @@
         "grad_attn": pltpu.VMEM((rows, model), F32),
         "sum_send": pltpu.VMEM((bits, rows, model), LOW),
         "sum_recv": pltpu.VMEM((2, bits, rows, model), LOW),
-        "small": pltpu.VMEM((steps + 1, 8, small_width), F32),
-        "small_recv": pltpu.VMEM((steps, 8, small_width), F32),
+        "small": pltpu.VMEM((8, small_width), F32),
+        "small_full": pltpu.VMEM((8, small_width), F32),
+        "small_held": pltpu.VMEM((2, 8, small_width // 4), F32),
+        "small_recv": pltpu.VMEM((3, 8, small_width // 4), F32),
+        "line": pltpu.VMEM((steps + 1, 8, small_width // 4), F32),
+        "line_recv": pltpu.VMEM((steps, 8, small_width // 4), F32),
         "load_sem": dma((5,)),
         "part_send": dma((2, 3, 4)),
         "part_recv": dma((2, 3, 4)),
@@ -965,7 +1050,8 @@
         "kv_send": dma((heads, 5)),
         "kv_recv": dma((heads, 5)),
         "sum_sems": dma((2, 2, bits)),
-        "small_sems": dma((2, steps)),
+        "small_sems": dma((2, 3 + steps)),
+        "spread_sems": dma((2, 3)),
         "free": pltpu.SemaphoreType.REGULAR((4,)),
     }
     names = [*inputs, *outputs, *scratch]

time: 264 us -> 259 us (0.981)
  Pallas kernels: 260 us -> 257 us
    pallas_call x1, Pallas kernels: 252 us -> 249 us  [local(): pl.pallas_call(functools.partial(layer_kernel, plan, names), out_shape=[j...]
where the time goes in v5:
time: 259 us
  Pallas kernels  257 us (99%)
    pallas_call x1, Pallas kernels, local(): pl.pallas_call(functools.partial(layer_kernel, plan, names), out_shape=[j...  249 us
    pallas_call x1, Pallas kernels, local(): pl.pallas_call(functools.partial(hand_on, cuts), out_shape=shapes, in_spe...  7.99 us

profile of v5, /device:TPU:0, one launch (start us, length us, event | category | flops | bytes accessed | tf_op | source)
XLA Modules:
  0.0 258.6 jit_solution(12055290768235664022)
XLA Ops:
  0.7 1.3 fusion
  2.0 248.6 %layer.1 = (bf16[256,2048]{1,0:T(8,128)(2,1)}, bf16[256,2048]{1,0:T(8,128)(2,1)}, f32[8,4096]{1,0:T(8,128)}, f32[4096,128]{1,0:T(8,128)}, f32[128,4096]{1,0:T(8,...) custom-call(bf16[256,2048]{1,0:T(8,128)(2,1)} %bitcast.20, bf16[256,2048]{1,0:T(8,128)(2,1)} %bitcast.21, ...), custom_call_target="tpu_custom_call" | custom-call | tf_op jit(solution)/shard_map/layer/pallas_call | solution.py:1058
  250.6 8.0 %hand_on.1 = (bf16[256,2048]{1,0:T(8,128)(2,1)}, bf16[256,2048]{1,0:T(8,128)(2,1)}, f32[4096,128]{1,0:T(8,128)}, f32[128,4096]{1,0:T(8,128)}, f32[1024,128]{1,0:...) custom-call(bf16[256,2048]{1,0:T(8,128)(2,1)} %get-tuple-element.35., ...), custom_call_target="tpu_custom_call" | custom-call | tf_op jit(solution)/shard_map/hand_on/pallas_call | solution.py:1083
  (4 shorter events, 0.0 us)

commit v6 on v5

--- a/solution.py
+++ b/solution.py
@@ -102,18 +102,56 @@
             at.dense_weight.at[blocks_of(head, HS)], at.dense_held, at.load_sem.at[4]
         )
 
-    def part_copy(kind, place, block):
+    shared = lax.axis_size("tensor") == 2
+    side = lax.axis_index("tensor")
+
+    def part_numbers(place):
+        return range(2 if shared and place > 1 else 4)
+
+    def part_copy(kind, place, number):
         source = (at.low, at.hidden)[kind]
         target = (at.low_part, at.hidden_part)[kind]
+        block = 2 * side + number if shared and place > 1 else number
         column = block * 4 + flip(ctx, place)
         return send_to(
             source.at[:, blocks_of(column, width)],
-            target.at[pl.ds(ORDER.index(place) * rows, rows), pl.ds(block * width, width)],
-            at.part_send.at[kind, place - 1, block],
-            at.part_recv.at[kind, place - 1, block],
+            target.at[pl.ds(ORDER.index(place) * rows, rows), blocks_of(block, width)],
+            at.part_send.at[kind, place - 1, number],
+            at.part_recv.at[kind, place - 1, number],
             "ctx",
             place,
         )
+
+    def part_pass(kind, place):
+        target = (at.low_part, at.hidden_part)[kind]
+        half = target.at[pl.ds(ORDER.index(place) * rows, rows), blocks_of(side, 2 * width)]
+        return send_to(
+            half,
+            half,
+            at.pass_sems.at[0, kind, place - 2],
+            at.pass_sems.at[1, kind, place - 2],
+            "tensor",
+            1,
+        )
+
+    def part_starts(kind):
+        for place in (2, 3, 1):
+            for number in part_numbers(place):
+                part_copy(kind, place, number).start()
+
+    def pass_on(kind):
+        for place in (2, 3):
+            for number in part_numbers(place):
+                part_copy(kind, place, number).wait_recv()
+            if shared:
+                part_pass(kind, place).start()
+
+    def part_waits(kind):
+        for number in part_numbers(1):
+            part_copy(kind, 1, number).wait_recv()
+        if shared:
+            for place in (2, 3):
+                part_pass(kind, place).wait_recv()
 
     def stats_copy(place):
         return send_to(
@@ -167,19 +205,19 @@
             2,
         )
 
-    def is_given(piece):
-        return (piece < 4) | ((piece >= 8) & (piece % 4 < 2))
-
     def results(piece):
         slot = piece % 2
         turned, plain = at.turned.at[slot], at.plain.at[slot]
         feed = piece < late
-        pair = jnp.where(piece < 8, piece % 4, piece // 4 * 2 + piece % 2)
-        gives = is_given(piece)
+        gives = piece < pairs
         dense = (piece >= late) & (piece < late + attn_pieces)
         return (
-            (feed & gives, turned, at.down_out.at[blocks_of(pair, span)]),
-            (feed & jnp.logical_not(gives), plain, at.up_out.at[:, blocks_of(pair, span)]),
+            (gives, turned, at.down_out.at[blocks_of(piece, span)]),
+            (
+                feed & jnp.logical_not(gives),
+                plain,
+                at.up_out.at[:, blocks_of(piece - pairs, span)],
+            ),
             (dense, turned, at.dense_out.at[blocks_of(piece - late, span)]),
             (
                 piece >= late + attn_pieces,
@@ -331,9 +369,7 @@
         some = blocks_of(block, step_rows)
         at.low[some] = grad_of(some).astype(LOW)
 
-    for place in (2, 3, 1):
-        for block in range(4):
-            part_copy(0, place, block).start()
+    part_starts(0)
 
     @pl.loop(0, rows // step_rows)
     def _(block):
@@ -354,8 +390,7 @@
         at.stats_line[0, pl.ds(8, 8)] = line[LANES // 2 : LANES // 2 + 8]
         for place in (2, 3, 1):
             stats_copy(place).start()
-            for block in range(4):
-                part_copy(1, place, block).start()
+        part_starts(1)
         for block in range(4):
             column = blocks_of(block * 4 + ctx, width)
             at.hidden_part[own_rows, pl.ds(block * width, width)] = at.hidden[:, column]
@@ -364,9 +399,7 @@
         for block in range(4):
             column = blocks_of(block * 4 + ctx, width)
             at.low_part[own_rows, pl.ds(block * width, width)] = at.low[:, column]
-        for place in (1, 2, 3):
-            for block in range(4):
-                part_copy(0, place, block).wait_recv()
+        part_waits(0)
         for entry, bits in enumerate(ORDER):
             block = at.low_part[:, blocks_of(flip(dp, bits), width)]
             at.left[0, pl.ds(entry * width, width)] = block.T
@@ -374,8 +407,7 @@
     def hidden_left():
         for place in (1, 2, 3):
             stats_copy(place).wait_recv()
-            for block in range(4):
-                part_copy(1, place, block).wait_recv()
+        part_waits(1)
         for slot in range(1, 4):
             half = lax.broadcasted_iota(jnp.int32, (LANES, rows), 0) < LANES // 2
             line = jnp.where(half, at.stats_line[slot, :1], at.stats_line[slot, 8:9])
@@ -408,52 +440,45 @@
         return pre, 0.5 * (1.0 + lax.erf(pre * math.sqrt(0.5)))
 
     def activate(pair):
-        if pair % 2 == 0:
+        if pair in (1, 3):
+            up_load_aside(pair).wait()
+            pre, cumulative = pre_act(pair, at.qkv_held[:, :span])
+        else:
             up_load(pair).wait()
             pre, cumulative = pre_act(pair, at.up_held[...])
+        at.rows_all[pair % RING, own_rows] = (pre * cumulative).astype(LOW)
+        start_piece(pair)
+        if pair == 1:
+            up_load_aside(3).start()
+        elif pair == 3:
+            qkv_load(0).start()
         else:
-            up_load_aside(pair).wait()
-            pre, cumulative = pre_act(pair, at.qkv_held[:, :span])
-        at.rows_all[pair, own_rows] = (pre * cumulative).astype(LOW)
-        start_piece(pair)
-        if pair % 2 == 0:
-            up_load((pair + 2) % 4).start()
-        elif pair == 1:
-            up_load_aside(3).start()
-        else:
-            qkv_load(0).start()
+            following = {0: 2, 2: 4}.get(pair, pair + 1)
+            up_load(following if following < pairs else 0).start()
+        if pair == max(pairs - 2, 3):
             send_hidden()
 
     def feed_forward(pair):
         up_load(pair).wait()
         down_load(pair).wait()
         pre, cumulative = pre_act(pair, at.up_held[...])
-        feed_piece = jnp.where(pair < 4, pair, pair // 2 * 4 + pair % 2)
-        grad_piece = feed_piece + jnp.where(pair < 4, 4, 2)
-
-        @pl.when(pair >= 4)
-        def _():
-            at.rows_all[feed_piece % RING, own_rows] = (pre * cumulative).astype(LOW)
-            start_piece(feed_piece)
-
+        given = (pre * cumulative).astype(LOW)
         grad_act = dot_rows(at.low[...], at.down_held[...])
         density = jnp.exp(-0.5 * pre * pre) * (1.0 / math.sqrt(2.0 * math.pi))
         grad_pre = (grad_act * (cumulative + pre * density)).astype(LOW)
-        at.rows_all[grad_piece % RING, own_rows] = grad_pre
+        at.rows_all[(pairs + pair) % RING, own_rows] = grad_pre
         at.small[pl.ds(4, 1), blocks_of(pair, span)] = jnp.sum(
             grad_pre.astype(F32), 0, keepdims=True
         )
-        @pl.when(pair < 4)
-        def _():
-            start_piece(grad_piece)
+        start_piece(pairs + pair)
 
         @pl.when(pair == 0)
         def _():
             for held in (at.branch, at.grad_mlp, at.grad_attn):
                 held[...] = jnp.zeros_like(held)
 
-        at.branch[...] += dot(at.rows_all[feed_piece % RING, own_rows], at.down_held[...])
-        at.grad_mlp[...] += dot_rows(at.rows_all[grad_piece % RING, own_rows], at.up_held[...])
+        at.branch[...] += dot(given, at.down_held[...])
+        at.grad_mlp[...] += dot_rows(grad_pre, at.up_held[...])
 
         @pl.when(pair + 1 < pairs)
         def _():
@@ -666,8 +691,8 @@
             small_spread(place).wait()
         at.small_out[...] = at.small_full[...]
 
-    lead, grad_lead = 3, 3
-    assert pairs % 2 == 0 and pairs >= 4
+    lead = 3
+    assert pairs in (4, 8)
 
     def places(base, *lags):
         return [
@@ -685,7 +710,8 @@
 
     jobs = next(pace for pace in (places(3, 3, 2, 2, 2), places(2, 1, 1, 1, 1)) if in_time(pace))
     project_at, forward_at, attend_at, halve_at, finish_at = jobs[0]
-    feed_end = max(2 * (pairs - 1) - 4, 3)
+    feed_at = max(pairs - 4, 1)
+    feed_end = feed_at + pairs - 1
     branch_at = max(attend_at + 2 * (heads - 1), feed_end) + 1
     back_at = max(finish_at + 2 * (heads - 1) + 2, branch_at + 4 * len(tensor_bits) + 1)
     total_steps = max(
@@ -720,7 +746,7 @@
             feed = multiply < late
             group = jnp.where(
                 feed,
-                jnp.where(is_given(multiply), 0, 1),
+                jnp.where(multiply < pairs, 0, 1),
                 jnp.where(multiply < late + attn_pieces, 0, 2),
             )
             at.first_send[multiply % 3] = dot(
@@ -767,7 +793,7 @@
                 + at.first_recv[last % RING, upper].astype(F32)
                 + at.second_recv[last % RING].astype(F32)
             )
-            flat = ((last < late) & jnp.logical_not(is_given(last))) | (last >= late + attn_pieces)
+            flat = ((last < late) & (last >= pairs)) | (last >= late + attn_pieces)
 
             @pl.when(flat)
             def _():
@@ -812,23 +838,15 @@
                         device_id_type=MESH,
                     )
 
-        job(4, 1, 1, lambda _: hidden_left())
-        job(-2, 1, 1, lambda _: activate(0))
-        job(-2, 1, 1, lambda _: activate(1))
-
-        grads = now + grad_lead
-
-        @pl.when((grads >= 8) & (grads < late) & (grads % 4 >= 2))
-        def _():
-            start_piece(grads)
-
-        @pl.when(((now >= 0) & (now < 4)) | ((now % 2 == 0) & (now >= 4) & (now < 2 * pairs - 4)))
-        def _():
-            feed_forward(jnp.where(now < 4, now, now // 2 + 2))
-
-        job(-1, 1, 1, lambda _: low_left())
-        job(-1, 1, 1, lambda _: activate(2))
-        job(-1, 1, 1, lambda _: activate(3))
+        for pair, place in enumerate((-2, -2, -1, 0, 1, 2, 3, 3)[:pairs]):
+            job(place, 1, 1, lambda _: activate(pair))
+            if pair == 0:
+                job(-2, 1, 1, lambda _: pass_on(0))
+            if pair == 2:
+                job(-1, 1, 1, lambda _: low_left())
+        job(pairs - 2, 1, 1, lambda _: pass_on(1))
+        job(pairs - 1, 1, 1, lambda _: hidden_left())
+        job(feed_at, 1, pairs, feed_forward)
         job(project_at, 2, heads, project)
         job(forward_at, 2, heads, kv_forward)
         job(finish_at, 2, heads, pair_finish)
@@ -856,8 +874,10 @@
     for place in (1, 2, 3):
         stats_copy(place).wait_send()
         for kind in range(2):
-            for block in range(4):
-                part_copy(kind, place, block).wait_send()
+            for number in part_numbers(place):
+                part_copy(kind, place, number).wait_send()
+            if shared and place > 1:
+                part_pass(kind, place).wait_send()
 
     @pl.loop(0, heads)
     def _(head):
@@ -1039,6 +1059,7 @@
         "load_sem": dma((5,)),
         "part_send": dma((2, 3, 4)),
         "part_recv": dma((2, 3, 4)),
+        "pass_sems": dma((2, 2, 2)),
         "stats_send": dma((3,)),
         "stats_recv": dma((3,)),
         "ctx_send": dma((RING, 3)),

time: 259 us -> 250 us (0.965); the launches traced: 259 us -> 246 us
  Pallas kernels: 257 us -> 244 us
    pallas_call x1, Pallas kernels: 249 us -> 236 us  [local(): pl.pallas_call(functools.partial(layer_kernel, plan, names), out_shape=[j...]
where the time goes in v6:
time: 250 us; the launch traced here: 246 us
  Pallas kernels  244 us (98%)
    pallas_call x1, Pallas kernels, local(): pl.pallas_call(functools.partial(layer_kernel, plan, names), out_shape=[j...  236 us
    pallas_call x1, Pallas kernels, local(): pl.pallas_call(functools.partial(hand_on, cuts), out_shape=shapes, in_spe...  7.99 us

profile of v6, /device:TPU:0, one launch (start us, length us, event | category | flops | bytes accessed | tf_op | source)
XLA Modules:
  0.0 245.7 jit_solution(17041575841914155647)
XLA Ops:
  0.7 1.3 fusion
  2.0 235.7 %layer.1 = (bf16[256,2048]{1,0:T(8,128)(2,1)}, bf16[256,2048]{1,0:T(8,128)(2,1)}, f32[8,4096]{1,0:T(8,128)}, f32[4096,128]{1,0:T(8,128)}, f32[128,4096]{1,0:T(8,...) custom-call(bf16[256,2048]{1,0:T(8,128)(2,1)} %bitcast.20, bf16[256,2048]{1,0:T(8,128)(2,1)} %bitcast.21, ...), custom_call_target="tpu_custom_call" | custom-call | tf_op jit(solution)/shard_map/layer/pallas_call | solution.py:1079
  237.7 8.0 %hand_on.1 = (bf16[256,2048]{1,0:T(8,128)(2,1)}, bf16[256,2048]{1,0:T(8,128)(2,1)}, f32[4096,128]{1,0:T(8,128)}, f32[128,4096]{1,0:T(8,128)}, f32[1024,128]{1,0:...) custom-call(bf16[256,2048]{1,0:T(8,128)(2,1)} %get-tuple-element.35., ...), custom_call_target="tpu_custom_call" | custom-call | tf_op jit(solution)/shard_map/hand_on/pallas_call | solution.py:1104
  (4 shorter events, 0.0 us)

commit v7 on v6

--- a/solution.py
+++ b/solution.py
@@ -708,7 +708,7 @@
                 return False
         return True
 
-    jobs = next(pace for pace in (places(3, 3, 2, 2, 2), places(2, 1, 1, 1, 1)) if in_time(pace))
+    jobs = next(pace for pace in (places(1, 5, 2, 2, 2), places(2, 1, 1, 1, 1)) if in_time(pace))
     project_at, forward_at, attend_at, halve_at, finish_at = jobs[0]
     feed_at = max(pairs - 4, 1)
     feed_end = feed_at + pairs - 1
@@ -842,8 +842,8 @@
             job(place, 1, 1, lambda _: activate(pair))
             if pair == 0:
                 job(-2, 1, 1, lambda _: pass_on(0))
-            if pair == 2:
-                job(-1, 1, 1, lambda _: low_left())
+            if pair == 3:
+                job(0, 1, 1, lambda _: low_left())
         job(pairs - 2, 1, 1, lambda _: pass_on(1))
         job(pairs - 1, 1, 1, lambda _: hidden_left())
         job(feed_at, 1, pairs, feed_forward)

time: 250 us -> 247 us (0.988); the launches traced: 246 us -> 246 us
  no operation moved by 1% of the time
where the time goes in v7:
time: 247 us; the launch traced here: 246 us
  Pallas kernels  244 us (99%)
    pallas_call x1, Pallas kernels, local(): pl.pallas_call(functools.partial(layer_kernel, plan, names), out_shape=[j...  236 us
    pallas_call x1, Pallas kernels, local(): pl.pallas_call(functools.partial(hand_on, cuts), out_shape=shapes, in_spe...  7.99 us

profile of v7, /device:TPU:0, one launch (start us, length us, event | category | flops | bytes accessed | tf_op | source)
XLA Modules:
  0.0 245.7 jit_solution(7170121468513024324)
XLA Ops:
  0.7 1.3 fusion
  2.0 235.7 %layer.1 = (bf16[256,2048]{1,0:T(8,128)(2,1)}, bf16[256,2048]{1,0:T(8,128)(2,1)}, f32[8,4096]{1,0:T(8,128)}, f32[4096,128]{1,0:T(8,128)}, f32[128,4096]{1,0:T(8,...) custom-call(bf16[256,2048]{1,0:T(8,128)(2,1)} %bitcast.20, bf16[256,2048]{1,0:T(8,128)(2,1)} %bitcast.21, ...), custom_call_target="tpu_custom_call" | custom-call | tf_op jit(solution)/shard_map/layer/pallas_call | solution.py:1079
  237.7 8.0 %hand_on.1 = (bf16[256,2048]{1,0:T(8,128)(2,1)}, bf16[256,2048]{1,0:T(8,128)(2,1)}, f32[4096,128]{1,0:T(8,128)}, f32[128,4096]{1,0:T(8,128)}, f32[1024,128]{1,0:...) custom-call(bf16[256,2048]{1,0:T(8,128)(2,1)} %get-tuple-element.35., ...), custom_call_target="tpu_custom_call" | custom-call | tf_op jit(solution)/shard_map/hand_on/pallas_call | solution.py:1104
  (4 shorter events, 0.0 us)

commit v8 on v7

--- a/solution.py
+++ b/solution.py
@@ -4,6 +4,7 @@
 
 import jax
 import jax.numpy as jnp
+import numpy as np
 from jax import lax
 from jax.experimental import pallas as pl
 from jax.experimental.pallas import tpu as pltpu
@@ -379,7 +380,6 @@
         centered = inputs - mean
         inv_std = lax.rsqrt(jnp.mean(centered * centered, -1, keepdims=True) + NORM_EPS)
         normed = centered * inv_std
-        at.attn_in[some] = (normed * at.attn_gain[...] + at.attn_bias[...]).astype(LOW)
         at.mlp_in[some] = (normed * at.mlp_gain[...] + at.mlp_bias[...]).astype(LOW)
         lane = lax.broadcasted_iota(jnp.int32, (step_rows, LANES), 1)
         at.stats[some] = jnp.where(lane < LANES // 2, mean, inv_std)
@@ -394,6 +394,23 @@
         for block in range(4):
             column = blocks_of(block * 4 + ctx, width)
             at.hidden_part[own_rows, pl.ds(block * width, width)] = at.hidden[:, column]
+
+    def attention_inputs():
+        lane = lax.broadcasted_iota(jnp.int32, (rows, LANES), 1)
+        place = lax.broadcasted_iota(jnp.int32, (rows, LANES), 0) + ctx * rows
+        table = place.astype(F32) * at.freqs[...]
+        sine = jnp.sin(table)
+        at.cosine[...] = jnp.where(lane < ROT, jnp.cos(table), 1.0)
+        at.sine_ahead[...] = jnp.where(lane < ROT // 2, -sine, 0.0)
+        at.sine_behind[...] = jnp.where((lane >= ROT // 2) & (lane < ROT), sine, 0.0)
+
+        @pl.loop(0, rows // step_rows)
+        def _(block):
+            some = blocks_of(block, step_rows)
+            stats = at.stats[some]
+            centered = at.hidden[some].astype(F32) - stats[:, :1]
+            normed = centered * stats[:, LANES // 2 : LANES // 2 + 1]
+            at.attn_in[some] = (normed * at.attn_gain[...] + at.attn_bias[...]).astype(LOW)
 
     def low_left():
         for block in range(4):
@@ -844,6 +861,7 @@
                 job(-2, 1, 1, lambda _: pass_on(0))
             if pair == 3:
                 job(0, 1, 1, lambda _: low_left())
+                job(min(0, project_at - 1), 1, 1, lambda _: attention_inputs())
         job(pairs - 2, 1, 1, lambda _: pass_on(1))
         job(pairs - 1, 1, 1, lambda _: hidden_left())
         job(feed_at, 1, pairs, feed_forward)
@@ -966,15 +984,8 @@
     )
     tokens = rows * lax.axis_size("ctx")
 
-    half = ROT // 2
-    lane = jnp.arange(LANES, dtype=jnp.int32)[None, :]
-    positions = lax.axis_index("ctx") * rows + jnp.arange(rows, dtype=jnp.int32)
-    freqs = 10000.0 ** (-((lane % half).astype(F32) * 2.0 / ROT))
-    table = positions.astype(F32)[:, None] * freqs
-    sine = jnp.sin(table)
-    cosine = jnp.where(lane < ROT, jnp.cos(table), 1.0)
-    sine_ahead = jnp.where(lane < half, -sine, 0.0)
-    sine_behind = jnp.where((lane >= half) & (lane < ROT), sine, 0.0)
+    turns = np.arange(LANES) % (ROT // 2)
+    freqs = np.float32(10000.0) ** -(turns.astype(np.float32) * np.float32(2.0 / ROT))
 
     bits = lax.axis_size("tensor").bit_length() - 1
     steps = 2 + bits
@@ -987,9 +998,7 @@
         "cotangent": (out_cotangent.reshape(rows, model), vmem),
         "subset_ids": (subset_ids, vmem),
         "subset_weights": (subset_weights, pl.BlockSpec(memory_space=pltpu.SMEM)),
-        "cosine": (cosine, vmem),
-        "sine_ahead": (sine_ahead, vmem),
-        "sine_behind": (sine_behind, vmem),
+        "freqs": (jnp.asarray(freqs[None], F32), vmem),
         "attn_gain": (attn_norm_gain[None], vmem),
         "attn_bias": (attn_norm_bias[None], vmem),
         "mlp_gain": (mlp_norm_gain[None], vmem),
@@ -1027,6 +1036,9 @@
         "stats": pltpu.VMEM((tokens, LANES), F32),
         "stats_line": pltpu.VMEM((4, 16, rows), F32),
         "row_weight": pltpu.VMEM((rows, LANES), F32),
+        "cosine": pltpu.VMEM((rows, LANES), F32),
+        "sine_ahead": pltpu.VMEM((rows, LANES), F32),
+        "sine_behind": pltpu.VMEM((rows, LANES), F32),
         "attn_in": pltpu.VMEM((rows, model), LOW),
         "mlp_in": pltpu.VMEM((rows, model), LOW),
         "low": pltpu.VMEM((rows, model), LOW),

time: 247 us -> 245 us (level)
  no operation moved by 1% of the time
where the time goes in v8:
time: 245 us; the launch traced here: 244 us
  Pallas kernels  244 us (100%)
    pallas_call x1, Pallas kernels, local(): pl.pallas_call(functools.partial(layer_kernel, plan, names), out_shape=[j...  236 us
    pallas_call x1, Pallas kernels, local(): pl.pallas_call(functools.partial(hand_on, cuts), out_shape=shapes, in_spe...  7.99 us

profile of v8, /device:TPU:0, one launch (start us, length us, event | category | flops | bytes accessed | tf_op | source)
XLA Modules:
  0.0 244.3 jit_solution(6694512606202183438)
XLA Ops:
  0.7 235.6 %layer.1 = (bf16[256,2048]{1,0:T(8,128)(2,1)}, bf16[256,2048]{1,0:T(8,128)(2,1)}, f32[8,4096]{1,0:T(8,128)}, f32[4096,128]{1,0:T(8,128)}, f32[128,4096]{1,0:T(8,...) custom-call(bf16[256,2048]{1,0:T(8,128)(2,1)} %bitcast.20, bf16[256,2048]{1,0:T(8,128)(2,1)} %bitcast.21, ...), custom_call_target="tpu_custom_call" | custom-call | tf_op jit(solution)/shard_map/layer/pallas_call | solution.py:1091
  236.3 8.0 %hand_on.1 = (bf16[256,2048]{1,0:T(8,128)(2,1)}, bf16[256,2048]{1,0:T(8,128)(2,1)}, f32[4096,128]{1,0:T(8,128)}, f32[128,4096]{1,0:T(8,128)}, f32[1024,128]{1,0:...) custom-call(bf16[256,2048]{1,0:T(8,128)(2,1)} %get-tuple-element.35., ...), custom_call_target="tpu_custom_call" | custom-call | tf_op jit(solution)/shard_map/hand_on/pallas_call | solution.py:1116

commit v9 on v8

--- a/solution.py
+++ b/solution.py
@@ -855,7 +855,7 @@
                         device_id_type=MESH,
                     )
 
-        for pair, place in enumerate((-2, -2, -1, 0, 1, 2, 3, 3)[:pairs]):
+        for pair, place in enumerate((-2, -2, -1, 0, 1, 2, 3, 4)[:pairs]):
             job(place, 1, 1, lambda _: activate(pair))
             if pair == 0:
                 job(-2, 1, 1, lambda _: pass_on(0))

time: 245 us -> 249 us (1.016); the launches traced: 244 us -> 245 us
  no operation moved by 1% of the time
where the time goes in v9:
time: 249 us; the launch traced here: 245 us
  Pallas kernels  244 us (98%)
    pallas_call x1, Pallas kernels, local(): pl.pallas_call(functools.partial(layer_kernel, plan, names), out_shape=[j...  236 us
    pallas_call x1, Pallas kernels, local(): pl.pallas_call(functools.partial(hand_on, cuts), out_shape=shapes, in_spe...  7.99 us

profile of v9, /device:TPU:0, one launch (start us, length us, event | category | flops | bytes accessed | tf_op | source)
XLA Modules:
  0.0 245.0 jit_solution(6628875150254933692)
XLA Ops:
  0.7 236.3 %layer.1 = (bf16[256,2048]{1,0:T(8,128)(2,1)}, bf16[256,2048]{1,0:T(8,128)(2,1)}, f32[8,4096]{1,0:T(8,128)}, f32[4096,128]{1,0:T(8,128)}, f32[128,4096]{1,0:T(8,...) custom-call(bf16[256,2048]{1,0:T(8,128)(2,1)} %bitcast.20, bf16[256,2048]{1,0:T(8,128)(2,1)} %bitcast.21, ...), custom_call_target="tpu_custom_call" | custom-call | tf_op jit(solution)/shard_map/layer/pallas_call | solution.py:1091
  237.0 8.0 %hand_on.1 = (bf16[256,2048]{1,0:T(8,128)(2,1)}, bf16[256,2048]{1,0:T(8,128)(2,1)}, f32[4096,128]{1,0:T(8,128)}, f32[128,4096]{1,0:T(8,128)}, f32[1024,128]{1,0:...) custom-call(bf16[256,2048]{1,0:T(8,128)(2,1)} %get-tuple-element.35., ...), custom_call_target="tpu_custom_call" | custom-call | tf_op jit(solution)/shard_map/hand_on/pallas_call | solution.py:1116
